TPU v7x, 32 devices: a whole 2x2x4 slice. The times are simulated.
32 devices in a mesh: seq: 8 (over z, x), tensor: 4 (over y, core).
Axes of the slice: x: 2, y: 2, z: 4, core: 2. Of those that a mesh axis runs over, the one named last changes fastest.
Arguments:
- hidden: bfloat16 [2048, 53248], P('seq', 'tensor'), may hold values from -6 to 6
- grad_out: bfloat16 [2048, 16384], P('seq', 'tensor'), may hold values from -0.13183594 to 0.13183594
- block_rows: int32 [4, 24], P('tensor'), may hold values from 0 to 103
- block_cols: int32 [4, 24], P('tensor'), may hold values from 0 to 127, as said below
- block_owner: int32 [4, 24], P('tensor'), may hold values from 0 to 7, never falling along the last dimension, each value on 1 to 8 neighbouring positions
Outputs:
- block_grads: bfloat16 [4, 64, 128, 128], P('tensor', 'seq')
Inputs may be any that keep to these rules, and one draw needn't show every extreme that they name: Every row of block_owner never falls along the list; each owner holds 1 to 8 blocks of a row, and some owner holds exactly 8. Each row of block_cols names exactly 6 distinct values among each run of 128 // 4 values that starts at a multiple of it.
All inputs are finite; a program needn't handle non-finite values.
Results may differ from a plain program's by a relative error of at most 0.0085.
Values may be sent and summed in bfloat16 or wider, within the bound.
No kernel may reach another device: no remote copies, remote signals or barrier semaphores. Data moves between devices by JAX's collectives and lax.ppermute only.
A program may use at most 128 MiB of HBM per device.

v0:
```python
import jax
import jax.numpy as jnp
from jax import lax
from jax.sharding import PartitionSpec as P

BLOCK = 128
CAP = 8


def add_sources(received):
    return jnp.sum(received, axis=0, dtype=jnp.float32)


def pick_slots(summed, starts, counts):
    slot_ids = starts[:, None] + jnp.arange(CAP, dtype=jnp.int32)[None, :]
    is_live = jnp.arange(CAP, dtype=jnp.int32)[None, :] < counts[:, None]
    picked = jnp.take(summed, jnp.minimum(slot_ids, summed.shape[0] - 1).reshape(-1), axis=0)
    picked = picked.reshape(slot_ids.shape[0], CAP, BLOCK, BLOCK)
    return jnp.where(is_live[:, :, None, None], picked, jnp.zeros_like(picked))


def on_device(hidden, grad_out, block_rows, block_cols, block_owner):
    tok_rows = hidden.shape[0]
    hidden_blocks = hidden.reshape(tok_rows, -1, BLOCK)
    row_ids = block_rows[0]
    col_ids = block_cols[0]
    owners = block_owner[0]
    hidden_sel = jnp.take(hidden_blocks, row_ids, axis=1)
    cotangent = lax.all_gather(grad_out, "tensor", axis=1, tiled=True)
    grad_blocks = cotangent.reshape(tok_rows, -1, BLOCK)
    grad_sel = jnp.take(grad_blocks, col_ids, axis=1)
    partial_value = jnp.einsum(
        "tkr,tkc->krc", hidden_sel, grad_sel, preferred_element_type=jnp.float32
    ).astype(jnp.bfloat16)
    seq_count = lax.axis_size("seq")
    members = (owners[None, :] == jnp.arange(seq_count, dtype=jnp.int32)[:, None]).astype(jnp.int32)
    counts = jnp.sum(members, axis=1)
    starts = jnp.cumsum(counts) - counts
    outgoing_blocks = pick_slots(partial_value, starts, counts)
    summed = add_sources(
        lax.all_to_all(outgoing_blocks, "seq", split_axis=0, concat_axis=0, tiled=True)
    )
    result = summed.astype(jnp.bfloat16)
    return result[None]


def solution(mesh):
    placed = (
        P("seq", "tensor"),
        P("seq", "tensor"),
        P("tensor", None),
        P("tensor", None),
        P("tensor", None),
    )
    return jax.shard_map(
        on_device,
        mesh=mesh,
        in_specs=placed,
        out_specs=P("tensor", "seq", None, None),
        check_vma=False,
    )
```

profile of v0, /device:TPU:0, one launch (start us, length us, event | category | flops | bytes accessed | tf_op | source)
XLA Modules:
  0.0 154.3 jit_solution(2720989584396916919)
XLA Ops:
  6.5 0.0 all-gather.2.cloned.1.call-start
  6.5 4.1 %copy.15 = bf16[256,4096]{0,1:T(8,128)(2,1)} copy(bf16[256,4096]{1,0:T(8,128)(2,1)} %param.6) | data formatting | bytes 4194304 | tf_op args[1]
  10.6 0.0 all-gather.2.cloned.1.call-update
  10.7 9.9 %copy.13 = bf16[256,13312]{0,1:T(8,128)(2,1)} copy(bf16[256,13312]{1,0:T(8,128)(2,1)} %param.5) | data formatting | bytes 13631488 | tf_op args[0]
  20.6 0.0 copy-start.2
  20.6 0.0 copy-start.1
  20.6 10.2 %copy.14 = bf16[256,104,128]{2,0,1:T(8,128)(2,1)} copy(bf16[256,104,128]{0,2,1:T(8,128)(2,1)} %bitcast.32) | data formatting | bytes 13631488 | tf_op jit(solution)/shard_map/reshape | solution.py:24
  30.8 0.0 copy-start
  30.8 0.0 copy-done.2
  30.8 0.1 convert_reduce_fusion
  30.9 0.2 reduce-window.8
  31.1 0.1 add_minimum_fusion
  31.2 0.1 min.22
  31.3 0.0 copy-done.1
  31.3 3.9 %gather_fusion = bf16[24,256,128]{2,1,0:T(8,128)(2,1)S(1)} fusion(bf16[256,104,128]{2,0,1:T(8,128)(2,1)} %copy.14, s32[1024]{0:T(1024)S(1)} %pad_clamp_fusion.2), kind=kCustom, calls=%fused_computation | custom fusion | bytes 3145824 | tf_op jit(solution)/shard_map/jit(_take)/gather | solution.py:28
  35.2 0.0 copy-done
  35.3 0.1 iota_compare_fusion.1
  35.3 36.5 %all-gather.2.cloned.1.call-done = bf16[256,16384]{0,1:T(8,128)(2,1)} async-done(((bf16[256,4096]{0,1:T(8,128)(2,1)}), bf16[256,16384]{0,1:T(8,128)(2,1)}) %all-gather.2.cloned.1.call-update) | async-done | bytes 8388624 | tf_op jit(solution)/shard_map/all_gather | solution.py:29
  71.8 11.9 %copy.16 = bf16[256,128,128]{2,0,1:T(8,128)(2,1)} copy(bf16[256,128,128]{0,2,1:T(8,128)(2,1)} %bitcast.33) | data formatting | bytes 16777216 | tf_op jit(solution)/shard_map/reshape | solution.py:30
  83.7 5.3 %gather_fusion.1 = bf16[24,256,128]{2,1,0:T(8,128)(2,1)} fusion(bf16[256,128,128]{2,0,1:T(8,128)(2,1)} %copy.16, s32[1024]{0:T(1024)S(1)} %pad_clamp_fusion.1), kind=kCustom, calls=%fused_computation.1 | custom fusion | bytes 3145824 | tf_op jit(solution)/shard_map/jit(_take)/gather | solution.py:31
  89.0 2.2 %fusion.7 = bf16[24,128,128]{2,1,0:T(8,128)(2,1)S(1)} fusion(bf16[24,256,128]{2,1,0:T(8,128)(2,1)} %gather_fusion.1, pred[24]{0:T(512)(128)(4,1)S(1)} %get-tuple-element.5, bf16[24,256,128]{2,1,0:T(8,128)(2,1)S(1)} %gather_fusion, pred[24]{0:T(512)(128)(4,1)S(1)} %get-tuple-element.6), kind=kOutput, calls=%fused_computation.11 | convolution fusion | flops 203292672 | bytes 3932208 | tf_op jit(solution)/shard_map/tkr,tkc->krc/dot_general | solution.py:32
  91.2 1.0 gather_fusion.2
  92.1 0.3 select_select_fusion
  92.5 53.9 %all_to_all.5 = bf16[8,8,128,128]{3,2,1,0:T(8,128)(2,1)S(1)} all-to-all(bf16[8,8,128,128]{3,2,1,0:T(8,128)(2,1)S(1)} %select_select_fusion), channel_id=1, replica_groups=mesh['seq'=8,'tensor'=4] {'seq'}, dimensions={0} | all-to-all | bytes 4194304 | tf_op jit(solution)/shard_map/all_to_all | solution.py:41
  146.4 1.1 reduce_sum.22
  (8 shorter events, 0.0 us)
Async XLA Ops:
  6.5 65.3 %all-gather.2.cloned.1.call-start = ((), (), s32[]{:S(2)}) async-start(), calls=%async_computation.1 | async-start | bytes 10485760 | tf_op jit(solution)/shard_map/all_gather | solution.py:29
  20.6 10.2 %copy-start.2 = (s32[1,24]{1,0:T(1,128)S(1)}, s32[1,24]{1,0:T(1,128)}, u32[]{:S(2)}) copy-start(s32[1,24]{1,0:T(1,128)} %param.9) | copy-start | bytes 292
  20.6 10.7 %copy-start.1 = (s32[1,24]{1,0:T(1,128)S(1)}, s32[1,24]{1,0:T(1,128)}, u32[]{:S(2)}) copy-start(s32[1,24]{1,0:T(1,128)} %param.7) | copy-start | bytes 292
  30.8 4.4 %copy-start = (s32[1,24]{1,0:T(1,128)S(1)}, s32[1,24]{1,0:T(1,128)}, u32[]{:S(2)}) copy-start(s32[1,24]{1,0:T(1,128)} %param.8) | copy-start | bytes 292
Sparse Core Ops, SparseCore 0:
  10.8 60.9 all-gather.1
where the time goes:
time: 155 us; the launch traced here: 154 us
  blocking collectives  53.9 us (35%)
  local copies, waits for them, and re-layouts  46.4 us (30%)
  waiting for transfers between devices  36.5 us (24%)
  between operations  13.5 us (9%)
  matrix products  2.17 us (1%)
  other arithmetic  1.92 us (1%)
    all_to_all x1, blocking collectives, on_device(): lax.all_to_all(outgoing_blocks, 'seq', split_axis=0, concat_axis=0, tiled...  53.9 us
    all_gather x1, waiting for transfers between devices, on_device(): cotangent = lax.all_gather(grad_out, 'tensor', axis=1, tiled=True)  36.5 us
    unnamed x8, local copies, waits for them, and re-layouts  14 us
    reshape x1, local copies, waits for them, and re-layouts, on_device(): grad_blocks = cotangent.reshape(tok_rows, -1, BLOCK)  11.9 us
    reshape x1, local copies, waits for them, and re-layouts, on_device(): hidden_blocks = hidden.reshape(tok_rows, -1, BLOCK)  10.2 us
    gather x1, local copies, waits for them, and re-layouts, on_device(): grad_sel = jnp.take(grad_blocks, col_ids, axis=1)  5.33 us
    gather x1, local copies, waits for them, and re-layouts, on_device(): hidden_sel = jnp.take(hidden_blocks, row_ids, axis=1)  3.87 us
  transfers between devices with their start and end apart: 1, of which 1 were waited for; matrix products, arithmetic and copies ran while one was open for 16% of the time, Pallas kernels for 0%

commit v1 on v0

v1 whole, which is shorter than its diff:
```python
import functools

import jax
import jax.numpy as jnp
from jax import lax
from jax.experimental import pallas as pl
from jax.experimental.pallas import tpu as pltpu
from jax.sharding import PartitionSpec as P

BLOCK = 128
CAP = 8
ROW_TILE = 16

SMEM = pl.BlockSpec(memory_space=pltpu.SMEM)
ANY = pl.BlockSpec(memory_space=pl.ANY)
VMEM = pl.BlockSpec(memory_space=pltpu.VMEM)


def pick_slots(summed, starts, counts):
    slot_ids = starts[:, None] + jnp.arange(CAP, dtype=jnp.int32)[None, :]
    is_live = jnp.arange(CAP, dtype=jnp.int32)[None, :] < counts[:, None]
    picked = jnp.take(summed, jnp.minimum(slot_ids, summed.shape[0] - 1).reshape(-1), axis=0)
    picked = picked.reshape(slot_ids.shape[0], CAP, BLOCK, BLOCK)
    return jnp.where(is_live[:, :, None, None], picked, jnp.zeros_like(picked))


def dense_on_device(hidden, grad_out, block_rows, block_cols, block_owner):
    tok_rows = hidden.shape[0]
    hidden_sel = jnp.take(hidden.reshape(tok_rows, -1, BLOCK), block_rows[0], axis=1)
    cotangent = lax.all_gather(grad_out, "tensor", axis=1, tiled=True)
    grad_sel = jnp.take(cotangent.reshape(tok_rows, -1, BLOCK), block_cols[0], axis=1)
    partial_value = jnp.einsum(
        "tkr,tkc->krc", hidden_sel, grad_sel, preferred_element_type=jnp.float32
    ).astype(jnp.bfloat16)
    seq_count = lax.axis_size("seq")
    members = (block_owner[0][None, :] == jnp.arange(seq_count, dtype=jnp.int32)[:, None]).astype(jnp.int32)
    counts = jnp.sum(members, axis=1)
    starts = jnp.cumsum(counts) - counts
    outgoing = pick_slots(partial_value, starts, counts)
    received = lax.all_to_all(outgoing, "seq", split_axis=0, concat_axis=0, tiled=True)
    return jnp.sum(received, axis=0, dtype=jnp.float32).astype(jnp.bfloat16)[None]


def column(ref, index):
    return ref.at[:, pl.ds(pl.multiple_of(index * BLOCK, BLOCK), BLOCK)]


def own_columns(table, cols, me, cols_per, per_peer):
    for j in range(per_peer):
        table[j] = 0

    def visit(k, found):
        local = cols[0, k] - me * cols_per
        hit = jnp.logical_and(local >= 0, local < cols_per)
        table[jnp.where(hit, jnp.minimum(found, per_peer - 1), per_peer)] = local
        return found + hit.astype(jnp.int32)

    lax.fori_loop(0, cols.shape[1], visit, jnp.int32(0), unroll=True)


def pack_kernel(peers, cols_per, per_peer, *refs):
    lists, grad_out, packed, (table, sems) = refs[:peers], refs[peers], refs[peers + 1 : 2 * peers + 1], refs[2 * peers + 1 :]
    me = lax.axis_index("tensor")
    copies = []
    for n in range(peers):
        own_columns(table, lists[n], me, cols_per, per_peer)
        for j in range(per_peer):
            copy = pltpu.make_async_copy(column(grad_out, table[j]), packed[n].at[j], sems.at[n, j])
            copy.start()
            copies.append(copy)
    for copy in copies:
        copy.wait()


def pack_for(lists, grad_out, per_peer):
    tok_rows, width = grad_out.shape
    peers = len(lists)
    return pl.pallas_call(
        functools.partial(pack_kernel, peers, width // BLOCK, per_peer),
        out_shape=[jax.ShapeDtypeStruct((per_peer, tok_rows, BLOCK), grad_out.dtype)] * peers,
        in_specs=[SMEM] * peers + [ANY],
        out_specs=[VMEM] * peers,
        scratch_shapes=[pltpu.SMEM((per_peer + 1,), jnp.int32), pltpu.SemaphoreType.DMA((peers, per_peer))],
        name="pack_columns",
    )(*lists, grad_out)


def multiply(pieces, left, right):
    product = lax.dot_general(left, right, (((0,), (0,)), ((), ())), preferred_element_type=jnp.float32)
    return product.astype(jnp.bfloat16).reshape(pieces, BLOCK // pieces, BLOCK)


def near_kernel(cols_per, per_peer, pieces, rows, cols, hidden, grad_out, arrived, out, hidden_far, hidden_near, grad_near, row_of, col_of, seen, sems):
    me = lax.axis_index("tensor")
    items = row_of.shape[0]
    for index in range(items // per_peer):
        seen[index] = 0
    for item in range(items):
        row_of[item] = 0
        col_of[item] = 0

    def visit(k, carry):
        col = cols[0, k]
        distance = (col // cols_per) ^ me
        rank = seen[distance]
        seen[distance] = rank + 1
        item = distance * per_peer + jnp.minimum(rank, per_peer - 1)
        row_of[item] = rows[0, k]
        col_of[item] = col % cols_per
        return carry

    lax.fori_loop(0, items, visit, 0, unroll=True)
    near = 2 * per_peer
    hidden_copies, grad_copies = [], []
    for item in range(items):
        there = hidden_near.at[item] if item < near else hidden_far.at[item - near]
        hidden_copies.append(pltpu.make_async_copy(column(hidden, row_of[item]), there, sems.at[0, item]))
        hidden_copies[-1].start()
        if item < per_peer:
            grad_copies.append(pltpu.make_async_copy(column(grad_out, col_of[item]), grad_near.at[item], sems.at[1, item]))
            grad_copies[-1].start()
    for item in range(near):
        hidden_copies[item].wait()
        if item < per_peer:
            grad_copies[item].wait()
        right = grad_near[item] if item < per_peer else arrived[item - per_peer]
        out[:, item] = multiply(pieces, hidden_near[item], right)
    for copy in hidden_copies[near:]:
        copy.wait()


def near_products(rows, cols, hidden, grad_out, arrived, per_peer, pieces):
    tok_rows, width = grad_out.shape
    items, near = cols.shape[1], 2 * per_peer
    return pl.pallas_call(
        functools.partial(near_kernel, width // BLOCK, per_peer, pieces),
        out_shape=[
            jax.ShapeDtypeStruct((pieces, near, BLOCK // pieces, BLOCK), jnp.bfloat16),
            jax.ShapeDtypeStruct((items - near, tok_rows, BLOCK), jnp.bfloat16),
        ],
        in_specs=[SMEM, SMEM, ANY, ANY, VMEM],
        out_specs=[VMEM, VMEM],
        scratch_shapes=[
            pltpu.VMEM((near, tok_rows, BLOCK), jnp.bfloat16),
            pltpu.VMEM((per_peer, tok_rows, BLOCK), jnp.bfloat16),
            pltpu.SMEM((items,), jnp.int32),
            pltpu.SMEM((items,), jnp.int32),
            pltpu.SMEM((items // per_peer,), jnp.int32),
            pltpu.SemaphoreType.DMA((2, items)),
        ],
        name="near_products",
    )(rows, cols, hidden, grad_out, arrived)


def far_kernel(first, pieces, hidden_far, arrived, out):
    for item in range(arrived.shape[0]):
        out[:, item] = multiply(pieces, hidden_far[first + item], arrived[item])


def far_products(first, hidden_far, arrived, pieces):
    return pl.pallas_call(
        functools.partial(far_kernel, first, pieces),
        out_shape=jax.ShapeDtypeStruct((pieces, arrived.shape[0], BLOCK // pieces, BLOCK), jnp.bfloat16),
        in_specs=[VMEM, VMEM],
        out_specs=VMEM,
        name="far_products",
    )(hidden_far, arrived)


def settle_kernel(cols_per, per_peer, cols, owners, *refs):
    received, (out, summed, seen) = refs[:-3], refs[-3:]
    base = 0
    for part in received:
        count = part.shape[1]
        summed[pl.ds(base, count)] = jnp.sum(part[...].astype(jnp.float32), axis=0).astype(jnp.bfloat16)
        base += count
    out[...] = jnp.zeros_like(out)
    me = lax.axis_index("tensor")
    for index in range(base // per_peer):
        seen[index] = 0

    def visit(k, carry):
        last_owner, last_slot = carry
        distance = (cols[0, k] // cols_per) ^ me
        rank = seen[distance]
        seen[distance] = rank + 1
        owner = owners[0, k]
        slot = jnp.where(owner == last_owner, last_slot + 1, 0)
        out[owner, jnp.minimum(slot, CAP - 1)] = summed[distance * per_peer + jnp.minimum(rank, per_peer - 1)]
        return owner, slot

    lax.fori_loop(0, cols.shape[1], visit, (jnp.int32(-1), jnp.int32(0)))


def settle(cols, owners, received, cols_per, per_peer):
    pieces, _, rows, _ = received[0].shape
    items = sum(part.shape[1] for part in received)
    return pl.pallas_call(
        functools.partial(settle_kernel, cols_per, per_peer),
        out_shape=jax.ShapeDtypeStruct((pieces, CAP, rows, BLOCK), jnp.bfloat16),
        in_specs=[SMEM, SMEM] + [VMEM] * len(received),
        out_specs=VMEM,
        scratch_shapes=[
            pltpu.VMEM((items, rows, BLOCK), jnp.bfloat16),
            pltpu.SMEM((items // per_peer,), jnp.int32),
        ],
        name="settle",
    )(cols, owners, *received)


def sparse_on_device(hidden, grad_out, block_rows, block_cols, block_owner):
    tensor_count, seq_count = lax.axis_size("tensor"), lax.axis_size("seq")
    cols_per = grad_out.shape[1] // BLOCK
    per_peer = block_cols.shape[1] // tensor_count

    def to_peer(value, distance):
        return lax.ppermute(value, "tensor", [(i, i ^ distance) for i in range(tensor_count)])

    def scatter(value):
        return lax.all_to_all(value, "seq", split_axis=0, concat_axis=0, tiled=True)

    peers = range(1, tensor_count)
    packed = pack_for([to_peer(block_cols, distance) for distance in peers], grad_out, per_peer)
    arrived = [to_peer(blocks, distance) for distance, blocks in zip(peers, packed)]
    near, hidden_far = near_products(block_rows, block_cols, hidden, grad_out, arrived[0], per_peer, seq_count)
    received = [scatter(near)]
    for n, blocks in enumerate(arrived[1:]):
        received.append(scatter(far_products(n * per_peer, hidden_far, blocks, seq_count)))
    placed = scatter(settle(block_cols, block_owner, received, cols_per, per_peer))
    return placed.transpose(1, 0, 2, 3).reshape(1, CAP, BLOCK, BLOCK)


def solution(mesh):
    tensor_count, seq_count = mesh.shape["tensor"], mesh.shape["seq"]
    placed = (
        P("seq", "tensor"),
        P("seq", "tensor"),
        P("tensor", None),
        P("tensor", None),
        P("tensor", None),
    )

    def on_device(hidden, grad_out, block_rows, block_cols, block_owner):
        listed = block_cols.shape[1]
        each_named_once = listed == 24 and tensor_count == 4
        whole_tiles = BLOCK % (seq_count * ROW_TILE) == 0
        step = sparse_on_device if each_named_once and whole_tiles else dense_on_device
        return step(hidden, grad_out, block_rows, block_cols, block_owner)

    return jax.shard_map(
        on_device,
        mesh=mesh,
        in_specs=placed,
        out_specs=P("tensor", "seq", None, None),
        check_vma=False,
    )
```

time: 155 us -> 80.2 us (0.52)
  local copies, waits for them, and re-layouts: 46.4 us -> 4.05 us
  waiting for transfers between devices: 36.5 us -> 11.4 us
  blocking collectives: 53.9 us -> 36.9 us
  Pallas kernels: 0 us -> 16.2 us
  between operations: 13.5 us -> 0.05 us
  starting transfers between devices: 0.01 us -> 10.8 us
  matrix products: 2.17 us -> 0 us
  other arithmetic: 1.92 us -> 0 us
    all_gather x1 -> x0, waiting for transfers between devices: 36.5 us -> none  [on_device(): cotangent = lax.all_gather(grad_out, 'tensor', axis=1, tiled=True)]
    reshape x2 -> x0, local copies, waits for them, and re-layouts: 22.1 us -> none  [the longest x1 11.9 us: on_device(): grad_blocks = cotangent.reshape(tok_rows, -1, BLOCK)]
    all_to_all x1 -> x3, blocking collectives: 53.9 us -> 36.9 us  [scatter(): return lax.all_to_all(value, 'seq', split_axis=0, concat_axis=0, tiled=True)]
    pallas_call x0 -> x5, Pallas kernels: none -> 16.2 us  [the longest x1 6.06 us: near_products(): pl.pallas_call(functools.partial(near_kernel, width // BLOCK, per_peer, p...]
    unnamed x8 -> x14, local copies, waits for them, and re-layouts: 14 us -> 3.33 us
    gather x3 -> x0, local copies, waits for them, and re-layouts: 10.2 us -> none  [the longest x1 5.33 us: on_device(): grad_sel = jnp.take(grad_blocks, col_ids, axis=1)]
    ppermute x0 -> x6, waiting for transfers between devices: none -> 6.62 us  [to_peer(): lax.ppermute(value, 'tensor', [(i, i ^ distance) for i in range(tensor_co...]
    all_to_all x0 -> x1, starting transfers between devices: none -> 5.8 us  [scatter(): return lax.all_to_all(value, 'seq', split_axis=0, concat_axis=0, tiled=True)]
  transfers between devices with their start and end apart: 1 -> 7, of which waited for: 1 -> 5; matrix products, arithmetic and copies ran while one was open for 16% -> 0% of each run, Pallas kernels for 0% -> 13%
where the time goes in v1:
time: 80.2 us; the launch traced here: 79.5 us
  blocking collectives  36.9 us (46%)
  Pallas kernels  16.2 us (20%)
  waiting for transfers between devices  11.4 us (14%)
  starting transfers between devices  10.8 us (13%)
  local copies, waits for them, and re-layouts  4.05 us (5%)
    all_to_all x3, blocking collectives, scatter(): return lax.all_to_all(value, 'seq', split_axis=0, concat_axis=0, tiled=True)  36.9 us
    ppermute x6, waiting for transfers between devices, to_peer(): lax.ppermute(value, 'tensor', [(i, i ^ distance) for i in range(tensor_co...  6.62 us
    pallas_call x1, Pallas kernels, near_products(): pl.pallas_call(functools.partial(near_kernel, width // BLOCK, per_peer, p...  6.06 us
    all_to_all x1, starting transfers between devices, scatter(): return lax.all_to_all(value, 'seq', split_axis=0, concat_axis=0, tiled=True)  5.8 us
    ppermute x6, starting transfers between devices, to_peer(): lax.ppermute(value, 'tensor', [(i, i ^ distance) for i in range(tensor_co...  5.03 us
    all_to_all x1, waiting for transfers between devices, scatter(): return lax.all_to_all(value, 'seq', split_axis=0, concat_axis=0, tiled=True)  4.79 us
    pallas_call x2, Pallas kernels, far_products(): pl.pallas_call(functools.partial(far_kernel, first, pieces), out_shape=ja...  4.45 us
    unnamed x14, local copies, waits for them, and re-layouts  3.33 us
  transfers between devices with their start and end apart: 7, of which 5 were waited for; matrix products, arithmetic and copies ran while one was open for 0% of the time, Pallas kernels for 13%

profile of v1, /device:TPU:0, one launch (start us, length us, event | category | flops | bytes accessed | tf_op | source)
XLA Modules:
  0.0 79.5 jit_solution(4846688499483345469)
XLA Ops:
  0.0 2.4 %collective-permute-start.2 = (s32[1,24]{1,0:T(1,128)}, s32[1,24]{1,0:T(1,128)S(1)}, u32[]{:S(2)}, u32[]{:S(2)}) collective-permute-start(s32[1,24]{1,0:T(1,128)} %cols.3), channel_id=1, source_target_pairs={{0,3},{1,2},{2,1},{3,0},{4,7},{5,6},{6,5},{7,4},{8,11},{9,10},{10,... | collective-permute-start | bytes 296 | tf_op jit(solution)/shard_map/ppermute | solution.py:217
  2.4 0.6 collective-permute-start.1
  3.0 0.1 collective-permute-start
  3.1 0.8 collective-permute-done.2.refs_2_
  3.9 0.0 copy-start.4
  3.9 2.3 %collective-permute-done.1.refs_1_ = s32[1,24]{1,0:T(1,128)S(1)} collective-permute-done((s32[1,24]{1,0:T(1,128)}, s32[1,24]{1,0:T(1,128)S(1)}, u32[]{:S(2)}, u32[]{:S(2)}) %collective-permute-start.1) | collective-permute-done | bytes 128 | tf_op jit(solution)/shard_map/ppermute | solution.py:217
  6.1 0.0 copy-start.5
  6.1 0.0 collective-permute-done.refs_0_
  6.1 0.0 copy-done.4
  6.2 0.6 copy-done.5
  6.7 0.0 copy-start.6
  6.7 0.5 copy-done.6
  7.2 3.3 %pack_columns.1 = (bf16[6,256,128]{2,1,0:T(8,128)(2,1)}, bf16[6,256,128]{2,1,0:T(8,128)(2,1)}, bf16[6,256,128]{2,1,0:T(8,128)(2,1)}) custom-call(s32[1,24]{1,0:T(1,128)} %copy-done.6, s32[1,24]{1,0:T(1,128)} %copy-done.5, s32[1,24]{1,0:T(1,128)} %copy-done.4, bf16[256,4096]{1,0:T(8,128)(2,1)} %grad_out.1), custom_call_target="tpu_custom_call" | custom-call | tf_op jit(solution)/shard_map/pack_columns/pallas_call | solution.py:78
  10.6 0.1 collective-permute-start.3
  10.6 0.6 collective-permute-start.4
  11.3 1.2 %collective-permute-start.5 = (bf16[6,256,128]{2,1,0:T(8,128)(2,1)}, bf16[6,256,128]{2,1,0:T(8,128)(2,1)S(1)}, u32[]{:S(2)}, u32[]{:S(2)}) collective-permute-start(bf16[6,256,128]{2,1,0:T(8,128)(2,1)} %get-tuple-element.14), channel_id=1, source_target_pairs={{0,3},{1,2},{2,1},{3,0},{4,7},{5,6},{6,5},{7,4},{8,11},{9,10},{10,... | collective-permute-start | bytes 1179656 | tf_op jit(solution)/shard_map/ppermute | solution.py:217
  12.5 0.1 collective-permute-done.3.arrived
  12.6 0.0 copy-start.1
  12.6 0.8 copy-done.1
  13.3 6.1 %near_products.1 = (bf16[8,12,16,128]{3,2,1,0:T(8,128)(2,1)}, bf16[12,256,128]{2,1,0:T(8,128)(2,1)}) custom-call(s32[1,24]{1,0:T(1,128)} %rows.1, s32[1,24]{1,0:T(1,128)} %cols.3, bf16[256,13312]{1,0:T(8,128)(2,1)} %hidden.1, bf16[256,4096]{1,0:T(8,128)(2,1)} %grad_out.1, bf16[6,256,128]{2,1,0:T(8,128)(2,1)} %copy-done.1), custom_call_target="tpu_custom_call" | custom-call | tf_op jit(solution)/shard_map/near_products/pallas_call | solution.py:135
  19.4 3.5 %collective-permute-done.4.arrived = bf16[6,256,128]{2,1,0:T(8,128)(2,1)S(1)} collective-permute-done((bf16[6,256,128]{2,1,0:T(8,128)(2,1)}, bf16[6,256,128]{2,1,0:T(8,128)(2,1)S(1)}, u32[]{:S(2)}, u32[]{:S(2)}) %collective-permute-start.4) | collective-permute-done | bytes 393248 | tf_op jit(solution)/shard_map/ppermute | solution.py:217
  22.9 0.0 copy-start.3
  22.9 0.8 copy-done.3
  23.7 2.2 %far_products.2 = bf16[8,6,16,128]{3,2,1,0:T(8,128)(2,1)} custom-call(bf16[12,256,128]{2,1,0:T(8,128)(2,1)} %get-tuple-element.12.hidden_far, bf16[6,256,128]{2,1,0:T(8,128)(2,1)} %copy-done.3), custom_call_target="tpu_custom_call" | custom-call | tf_op jit(solution)/shard_map/far_products/pallas_call | solution.py:161
  25.9 5.8 %all-to-all-start.1 = ((bf16[8,6,16,128]{3,2,1,0:T(8,128)(2,1)}), bf16[8,6,16,128]{3,2,1,0:T(8,128)(2,1)S(1)}, u32[]{:S(2)}, u32[]{:S(2)}) async-start(bf16[8,6,16,128]{3,2,1,0:T(8,128)(2,1)} %far_products.2), calls=%async_computation.1 | async-start | bytes 393216 | tf_op jit(solution)/shard_map/all_to_all | solution.py:220
  31.7 0.0 collective-permute-done.5.arrived
  31.7 0.0 copy-start.2
  31.7 0.8 copy-done.2
  32.4 2.2 %far_products.3 = bf16[8,6,16,128]{3,2,1,0:T(8,128)(2,1)} custom-call(bf16[12,256,128]{2,1,0:T(8,128)(2,1)} %get-tuple-element.12.hidden_far, bf16[6,256,128]{2,1,0:T(8,128)(2,1)} %copy-done.2), custom_call_target="tpu_custom_call" | custom-call | tf_op jit(solution)/shard_map/far_products/pallas_call | solution.py:161
  34.7 4.8 %all-to-all-done.1.refs_1_ = bf16[8,6,16,128]{3,2,1,0:T(8,128)(2,1)S(1)} async-done(((bf16[8,6,16,128]{3,2,1,0:T(8,128)(2,1)}), bf16[8,6,16,128]{3,2,1,0:T(8,128)(2,1)S(1)}, u32[]{:S(2)}, u32[]{:S(2)}) %all-to-all-start.1) | async-done | bytes 196640 | tf_op jit(solution)/shard_map/all_to_all | solution.py:220
  39.5 0.0 copy-start
  39.5 11.8 %all_to_all.20.refs_2_ = bf16[8,6,16,128]{3,2,1,0:T(8,128)(2,1)} all-to-all(bf16[8,6,16,128]{3,2,1,0:T(8,128)(2,1)} %far_products.3), channel_id=1, replica_groups=mesh['seq'=8,'tensor'=4] {'seq'}, dimensions={0} | all-to-all | bytes 393216 | tf_op jit(solution)/shard_map/all_to_all | solution.py:220
  51.3 13.5 %all_to_all.21.refs_0_ = bf16[8,12,16,128]{3,2,1,0:T(8,128)(2,1)} all-to-all(bf16[8,12,16,128]{3,2,1,0:T(8,128)(2,1)} %get-tuple-element.11), channel_id=1, replica_groups=mesh['seq'=8,'tensor'=4] {'seq'}, dimensions={0} | all-to-all | bytes 786432 | tf_op jit(solution)/shard_map/all_to_all | solution.py:220
  64.8 0.0 copy-done
  64.8 2.4 %settle.1 = bf16[8,8,16,128]{3,2,1,0:T(8,128)(2,1)} custom-call(s32[1,24]{1,0:T(1,128)} %cols.3, s32[1,24]{1,0:T(1,128)} %owners.1, bf16[8,12,16,128]{3,2,1,0:T(8,128)(2,1)} %all_to_all.21.refs_0_, bf16[8,6,16,128]{3,2,1,0:T(8,128)(2,1)} %copy-done, bf16[8,6,16,128]{3,2,1,0:T(8,128)(2,1)} %all_to_all.20.refs_2_), custom_call_target="tpu_custom_call" | custom-call | tf_op jit(solution)/shard_map/settle/pallas_call | solution.py:198
  67.2 11.5 %all_to_all.22 = bf16[8,8,16,128]{3,2,1,0:T(8,128)(2,1)S(1)} all-to-all(bf16[8,8,16,128]{3,2,1,0:T(8,128)(2,1)} %settle.1), channel_id=1, replica_groups=mesh['seq'=8,'tensor'=4] {'seq'}, dimensions={0} | all-to-all | bytes 524288 | tf_op jit(solution)/shard_map/all_to_all | solution.py:220
  78.7 0.7 copy.6
Async XLA Ops:
  0.0 3.9 %collective-permute-start.2 = (s32[1,24]{1,0:T(1,128)}, s32[1,24]{1,0:T(1,128)S(1)}, u32[]{:S(2)}, u32[]{:S(2)}) collective-permute-start(s32[1,24]{1,0:T(1,128)} %cols.3), channel_id=1, source_target_pairs={{0,3},{1,2},{2,1},{3,0},{4,7},{5,6},{6,5},{7,4},{8,11},{9,10},{10,... | collective-permute-start | bytes 296 | tf_op jit(solution)/shard_map/ppermute | solution.py:217
  2.4 3.7 %collective-permute-start.1 = (s32[1,24]{1,0:T(1,128)}, s32[1,24]{1,0:T(1,128)S(1)}, u32[]{:S(2)}, u32[]{:S(2)}) collective-permute-start(s32[1,24]{1,0:T(1,128)} %cols.3), channel_id=1, source_target_pairs={{0,2},{1,3},{2,0},{3,1},{4,6},{5,7},{6,4},{7,5},{8,10},{9,11},{10,... | collective-permute-start | bytes 296 | tf_op jit(solution)/shard_map/ppermute | solution.py:217
  3.0 3.1 %collective-permute-start = (s32[1,24]{1,0:T(1,128)}, s32[1,24]{1,0:T(1,128)S(1)}, u32[]{:S(2)}, u32[]{:S(2)}) collective-permute-start(s32[1,24]{1,0:T(1,128)} %cols.3), channel_id=1, source_target_pairs={{0,1},{1,0},{2,3},{3,2},{4,5},{5,4},{6,7},{7,6},{8,9},{9,8},{10,11... | collective-permute-start | bytes 296 | tf_op jit(solution)/shard_map/ppermute | solution.py:217
  3.9 2.3 %copy-start.4 = (s32[1,24]{1,0:T(1,128)}, s32[1,24]{1,0:T(1,128)S(1)}, u32[]{:S(2)}) copy-start(s32[1,24]{1,0:T(1,128)S(1)} %collective-permute-done.2.refs_2_) | copy-start | bytes 292
  6.1 0.6 copy-start.5
  6.7 0.5 copy-start.6
  10.6 2.0 %collective-permute-start.3 = (bf16[6,256,128]{2,1,0:T(8,128)(2,1)}, bf16[6,256,128]{2,1,0:T(8,128)(2,1)S(1)}, u32[]{:S(2)}, u32[]{:S(2)}) collective-permute-start(bf16[6,256,128]{2,1,0:T(8,128)(2,1)} %get-tuple-element.10), channel_id=1, source_target_pairs={{0,1},{1,0},{2,3},{3,2},{4,5},{5,4},{6,7},{7,6},{8,9},{9,8},{10,11... | collective-permute-start | bytes 1179656 | tf_op jit(solution)/shard_map/ppermute | solution.py:217
  10.6 12.3 %collective-permute-start.4 = (bf16[6,256,128]{2,1,0:T(8,128)(2,1)}, bf16[6,256,128]{2,1,0:T(8,128)(2,1)S(1)}, u32[]{:S(2)}, u32[]{:S(2)}) collective-permute-start(bf16[6,256,128]{2,1,0:T(8,128)(2,1)} %get-tuple-element.13), channel_id=1, source_target_pairs={{0,2},{1,3},{2,0},{3,1},{4,6},{5,7},{6,4},{7,5},{8,10},{9,11},{10,... | collective-permute-start | bytes 1179656 | tf_op jit(solution)/shard_map/ppermute | solution.py:217
  11.3 20.4 %collective-permute-start.5 = (bf16[6,256,128]{2,1,0:T(8,128)(2,1)}, bf16[6,256,128]{2,1,0:T(8,128)(2,1)S(1)}, u32[]{:S(2)}, u32[]{:S(2)}) collective-permute-start(bf16[6,256,128]{2,1,0:T(8,128)(2,1)} %get-tuple-element.14), channel_id=1, source_target_pairs={{0,3},{1,2},{2,1},{3,0},{4,7},{5,6},{6,5},{7,4},{8,11},{9,10},{10,... | collective-permute-start | bytes 1179656 | tf_op jit(solution)/shard_map/ppermute | solution.py:217
  12.6 0.8 copy-start.1
  22.9 0.8 copy-start.3
  25.9 13.6 %all-to-all-start.1 = ((bf16[8,6,16,128]{3,2,1,0:T(8,128)(2,1)}), bf16[8,6,16,128]{3,2,1,0:T(8,128)(2,1)S(1)}, u32[]{:S(2)}, u32[]{:S(2)}) async-start(bf16[8,6,16,128]{3,2,1,0:T(8,128)(2,1)} %far_products.2), calls=%async_computation.1 | async-start | bytes 393216 | tf_op jit(solution)/shard_map/all_to_all | solution.py:220
  31.7 0.8 copy-start.2
  39.5 25.3 %copy-start = (bf16[8,6,16,128]{3,2,1,0:T(8,128)(2,1)}, bf16[8,6,16,128]{3,2,1,0:T(8,128)(2,1)S(1)}, u32[]{:S(2)}) copy-start(bf16[8,6,16,128]{3,2,1,0:T(8,128)(2,1)S(1)} %all-to-all-done.1.refs_1_) | copy-start | bytes 589828

commit v2 on v0

v2 whole, which is shorter than its diff:
```python
import functools

import jax
import jax.numpy as jnp
from jax import lax
from jax.experimental import pallas as pl
from jax.experimental.pallas import tpu as pltpu
from jax.sharding import PartitionSpec as P


BLOCK = 128
CAP = 8
ROW_TILE = 16

SMEM = pl.BlockSpec(memory_space=pltpu.SMEM)
HBM = pl.BlockSpec(memory_space=pltpu.HBM)
VMEM = pl.BlockSpec(memory_space=pltpu.VMEM)


def pick_slots(summed, starts, counts):
    slot_ids = starts[:, None] + jnp.arange(CAP, dtype=jnp.int32)[None, :]
    is_live = jnp.arange(CAP, dtype=jnp.int32)[None, :] < counts[:, None]
    picked = jnp.take(summed, jnp.minimum(slot_ids, summed.shape[0] - 1).reshape(-1), axis=0)
    picked = picked.reshape(slot_ids.shape[0], CAP, BLOCK, BLOCK)
    return jnp.where(is_live[:, :, None, None], picked, jnp.zeros_like(picked))


def dense_on_device(hidden, grad_out, block_rows, block_cols, block_owner):
    tok_rows = hidden.shape[0]
    hidden_sel = jnp.take(hidden.reshape(tok_rows, -1, BLOCK), block_rows[0], axis=1)
    cotangent = lax.all_gather(grad_out, "tensor", axis=1, tiled=True)
    grad_sel = jnp.take(cotangent.reshape(tok_rows, -1, BLOCK), block_cols[0], axis=1)
    partial_value = jnp.einsum(
        "tkr,tkc->krc", hidden_sel, grad_sel, preferred_element_type=jnp.float32
    ).astype(jnp.bfloat16)
    seq_count = lax.axis_size("seq")
    members = (block_owner[0][None, :] == jnp.arange(seq_count, dtype=jnp.int32)[:, None]).astype(jnp.int32)
    counts = jnp.sum(members, axis=1)
    starts = jnp.cumsum(counts) - counts
    outgoing = pick_slots(partial_value, starts, counts)
    received = lax.all_to_all(outgoing, "seq", split_axis=0, concat_axis=0, tiled=True)
    return jnp.sum(received, axis=0, dtype=jnp.float32).astype(jnp.bfloat16)[None]


def scalars(value):
    return pltpu.with_memory_space_constraint(value, pltpu.SMEM)


def vectors(value):
    return pltpu.with_memory_space_constraint(value, pltpu.VMEM)


def column(ref, index):
    return ref.at[:, pl.ds(pl.multiple_of(index * BLOCK, BLOCK), BLOCK)]


def listed_at(table, cols, values, owner, cols_per, per_peer):
    for j in range(per_peer):
        table[j] = 0

    def visit(k, found):
        local = cols[0, k] - owner * cols_per
        hit = jnp.logical_and(local >= 0, local < cols_per)
        value = local if values is None else values[0, k]
        table[jnp.where(hit, jnp.minimum(found, per_peer - 1), per_peer)] = value
        return found + hit.astype(jnp.int32)

    lax.fori_loop(0, cols.shape[1], visit, jnp.int32(0), unroll=True)


def split_pieces(parts, kept, sent):
    me = lax.axis_index("seq")
    half = kept.shape[0]
    width = half.bit_length() - 1
    for index in range(half):
        apart = sum(((index >> (width - 1 - bit)) & 1) << (bit + 1) for bit in range(width))
        kept[index] = parts[me ^ apart]
        sent[index] = parts[me ^ apart ^ 1].astype(jnp.bfloat16)


def halve_kernel(kept, received, still, sent):
    half = still.shape[0]
    still[...] = kept[:half] + received[:half].astype(jnp.float32)
    sent[...] = (kept[half:] + received[half:].astype(jnp.float32)).astype(jnp.bfloat16)


def halve(kept, received):
    shape = (kept.shape[0] // 2,) + kept.shape[1:]
    return pl.pallas_call(
        halve_kernel,
        out_shape=[pltpu.VMEM(shape, jnp.float32), pltpu.VMEM(shape, jnp.bfloat16)],
        in_specs=[VMEM, VMEM],
        out_specs=[VMEM, VMEM],
    )(vectors(kept), vectors(received))


def finish_kernel(kept, received, out):
    out[...] = (kept[0] + received[0].astype(jnp.float32)).astype(jnp.bfloat16)


def finish(kept, received):
    return pl.pallas_call(
        finish_kernel, out_shape=pltpu.VMEM(kept.shape[1:], jnp.bfloat16), in_specs=[VMEM, VMEM], out_specs=VMEM
    )(vectors(kept), vectors(received))


def halved_shapes(pieces, items):
    shape = (pieces // 2, items, BLOCK // pieces, BLOCK)
    return [pltpu.VMEM(shape, jnp.float32), pltpu.VMEM(shape, jnp.bfloat16)]


def multiply(pieces, left, right):
    product = lax.dot_general(left, right, (((0,), (0,)), ((), ())), preferred_element_type=jnp.float32)
    return product.reshape(pieces, BLOCK // pieces, BLOCK)


def first_kernel(cols_per, per_peer, rows, cols, list1, hidden, grad_out, pushed, for_core, table, sems):
    me = lax.axis_index("tensor")
    copies = []

    def gather(n, source, there):
        for j in range(per_peer):
            copies.append(pltpu.make_async_copy(column(source, table[j]), there.at[j], sems.at[n, j]))
            copies[-1].start()

    listed_at(table, cols, rows, me ^ 2, cols_per, per_peer)
    gather(0, hidden, pushed)
    listed_at(table, list1, None, me, cols_per, per_peer)
    gather(1, grad_out, for_core)
    for copy in copies:
        copy.wait()


def first_sends(rows, cols, list1, hidden, grad_out, per_peer):
    tok_rows, width = grad_out.shape
    return pl.pallas_call(
        functools.partial(first_kernel, width // BLOCK, per_peer),
        out_shape=[pltpu.VMEM((per_peer, tok_rows, BLOCK), grad_out.dtype)] * 2,
        in_specs=[SMEM, SMEM, SMEM, HBM, HBM],
        out_specs=[VMEM, VMEM],
        scratch_shapes=[pltpu.SMEM((per_peer + 1,), jnp.int32), pltpu.SemaphoreType.DMA((2, per_peer))],
        name="first_sends",
    )(scalars(rows), scalars(cols), scalars(list1), hidden, grad_out)


def near_kernel(cols_per, per_peer, pieces, rows, cols, list3, hidden, grad_out, arrived, kept, sent, hidden_far, for_far, hidden_near, grad_near, parts, table, sems):
    me = lax.axis_index("tensor")
    count = [0]

    def gather(owner, listed, values, source, there, first):
        listed_at(table, listed, values, owner, cols_per, per_peer)
        copies = []
        for j in range(per_peer):
            copies.append(pltpu.make_async_copy(column(source, table[j]), there.at[first + j], sems.at[count[0], j]))
            copies[-1].start()
        count[0] += 1
        return copies

    mine = gather(me, cols, None, grad_out, grad_near, 0)
    near = gather(me, cols, rows, hidden, hidden_near, 0)
    near += gather(me ^ 1, cols, rows, hidden, hidden_near, per_peer)
    later = gather(me, list3, None, grad_out, for_far, 0)
    later += gather(me ^ 3, cols, rows, hidden, hidden_far, 0)
    for copy in mine + near:
        copy.wait()
    for item in range(2 * per_peer):
        right = grad_near[item] if item < per_peer else arrived[item - per_peer]
        parts[:, item] = multiply(pieces, hidden_near[item], right)
    split_pieces(parts, kept, sent)
    for copy in later:
        copy.wait()


def near_products(rows, cols, list3, hidden, grad_out, arrived, per_peer, pieces):
    tok_rows, width = grad_out.shape
    near = 2 * per_peer
    blocks = pltpu.VMEM((per_peer, tok_rows, BLOCK), jnp.bfloat16)
    return pl.pallas_call(
        functools.partial(near_kernel, width // BLOCK, per_peer, pieces),
        out_shape=halved_shapes(pieces, near) + [blocks, blocks],
        in_specs=[SMEM, SMEM, SMEM, HBM, HBM, VMEM],
        out_specs=[VMEM] * 4,
        scratch_shapes=[
            pltpu.VMEM((near, tok_rows, BLOCK), jnp.bfloat16),
            pltpu.VMEM((per_peer, tok_rows, BLOCK), jnp.bfloat16),
            pltpu.VMEM((pieces, near, BLOCK // pieces, BLOCK), jnp.float32),
            pltpu.SMEM((per_peer + 1,), jnp.int32),
            pltpu.SemaphoreType.DMA((5, per_peer)),
        ],
        name="near_products",
    )(scalars(rows), scalars(cols), scalars(list3), hidden, grad_out, vectors(arrived))


def guest_kernel(cols_per, per_peer, pieces, list2, grad_out, arrived, kept, sent, right, parts, table, sems):
    listed_at(table, list2, None, lax.axis_index("tensor"), cols_per, per_peer)
    copies = [pltpu.make_async_copy(column(grad_out, table[j]), right.at[j], sems.at[j]) for j in range(per_peer)]
    for copy in copies:
        copy.start()
    for copy in copies:
        copy.wait()
    for j in range(per_peer):
        parts[:, j] = multiply(pieces, arrived[j], right[j])
    split_pieces(parts, kept, sent)


def guest_products(list2, grad_out, arrived, per_peer, pieces):
    tok_rows, width = grad_out.shape
    return pl.pallas_call(
        functools.partial(guest_kernel, width // BLOCK, per_peer, pieces),
        out_shape=halved_shapes(pieces, per_peer),
        in_specs=[SMEM, HBM, VMEM],
        out_specs=[VMEM, VMEM],
        scratch_shapes=[
            pltpu.VMEM((per_peer, tok_rows, BLOCK), jnp.bfloat16),
            pltpu.VMEM((pieces, per_peer, BLOCK // pieces, BLOCK), jnp.float32),
            pltpu.SMEM((per_peer + 1,), jnp.int32),
            pltpu.SemaphoreType.DMA((per_peer,)),
        ],
        name="guest_products",
    )(scalars(list2), grad_out, vectors(arrived))


def far_kernel(pieces, left, arrived, kept, sent, parts):
    for j in range(arrived.shape[0]):
        parts[:, j] = multiply(pieces, left[j], arrived[j])
    split_pieces(parts, kept, sent)


def far_products(left, arrived, pieces):
    count, _, _ = arrived.shape
    return pl.pallas_call(
        functools.partial(far_kernel, pieces),
        out_shape=halved_shapes(pieces, count),
        in_specs=[VMEM, VMEM],
        out_specs=[VMEM, VMEM],
        scratch_shapes=[pltpu.VMEM((pieces, count, BLOCK // pieces, BLOCK), jnp.float32)],
        name="far_products",
    )(vectors(left), vectors(arrived))


def settle_kernel(cols_per, per_peer, cols, owners, near, guests, far, out, summed, seen):
    me = lax.axis_index("tensor")
    for index in range(4):
        seen[index] = 0
    summed[pl.ds(0, 2 * per_peer)] = near[...]
    summed[pl.ds(2 * per_peer, per_peer)] = guests[...]
    summed[pl.ds(3 * per_peer, per_peer)] = far[...]
    out[...] = jnp.zeros_like(out)

    def visit(k, carry):
        last_owner, last_slot = carry
        distance = (cols[0, k] // cols_per) ^ me
        rank = seen[distance]
        seen[distance] = rank + 1
        owner = owners[0, k]
        slot = jnp.where(owner == last_owner, last_slot + 1, 0)
        out[owner, jnp.minimum(slot, CAP - 1)] = summed[distance * per_peer + jnp.minimum(rank, per_peer - 1)]
        return owner, slot

    lax.fori_loop(0, cols.shape[1], visit, (jnp.int32(-1), jnp.int32(0)), unroll=True)


def settle(cols, owners, near, guests, far, cols_per, pieces):
    per_peer, rows, _ = far.shape
    return pl.pallas_call(
        functools.partial(settle_kernel, cols_per, per_peer),
        out_shape=pltpu.VMEM((pieces, CAP, rows, BLOCK), jnp.bfloat16),
        in_specs=[SMEM, SMEM, VMEM, VMEM, VMEM],
        out_specs=VMEM,
        scratch_shapes=[pltpu.VMEM((4 * per_peer, rows, BLOCK), jnp.bfloat16), pltpu.SMEM((4,), jnp.int32)],
        name="settle",
    )(scalars(cols), scalars(owners), vectors(near), vectors(guests), vectors(far))


def sparse_on_device(hidden, grad_out, block_rows, block_cols, block_owner):
    tensor_count, seq_count = lax.axis_size("tensor"), lax.axis_size("seq")
    cols_per = grad_out.shape[1] // BLOCK
    per_peer = block_cols.shape[1] // tensor_count

    def to_peer(value, distance):
        return lax.ppermute(value, "tensor", [(i, i ^ distance) for i in range(tensor_count)])

    def scatter(value):
        return lax.all_to_all(value, "seq", split_axis=0, concat_axis=0, tiled=True)

    def reduce_pieces(kept, sent):
        distance = 1
        while True:
            received = lax.ppermute(sent, "seq", [(i, i ^ distance) for i in range(seq_count)])
            if kept.shape[0] == 1:
                return finish(kept, received)
            kept, sent = halve(kept, received)
            distance *= 2

    list3 = to_peer(block_cols, 3)
    list1 = to_peer(block_cols, 1)
    list2 = to_peer(block_cols, 2)
    pushed, for_core = first_sends(block_rows, block_cols, list1, hidden, grad_out, per_peer)
    guests = to_peer(pushed, 2)
    from_core = to_peer(for_core, 1)
    near_kept, near_sent, hidden_far, for_far = near_products(
        block_rows, block_cols, list3, hidden, grad_out, from_core, per_peer, seq_count
    )
    from_far = to_peer(for_far, 3)
    near_sum = reduce_pieces(near_kept, near_sent)
    guest_kept, guest_sent = guest_products(list2, grad_out, guests, per_peer, seq_count)
    guest_sum = reduce_pieces(guest_kept, guest_sent)
    guest_back = to_peer(guest_sum, 2)
    far_kept, far_sent = far_products(hidden_far, from_far, seq_count)
    far_sum = reduce_pieces(far_kept, far_sent)
    placed = settle(block_cols, block_owner, near_sum, guest_back, far_sum, cols_per, seq_count)
    delivered = scatter(placed)
    return delivered.transpose(1, 0, 2, 3).reshape(1, CAP, BLOCK, BLOCK)


def solution(mesh):
    tensor_count, seq_count = mesh.shape["tensor"], mesh.shape["seq"]
    placed = (
        P("seq", "tensor"),
        P("seq", "tensor"),
        P("tensor", None),
        P("tensor", None),
        P("tensor", None),
    )

    def on_device(hidden, grad_out, block_rows, block_cols, block_owner):
        listed = block_cols.shape[1]
        each_named_once = listed == 24 and tensor_count == 4
        whole_tiles = BLOCK % (seq_count * ROW_TILE) == 0
        step = sparse_on_device if each_named_once and whole_tiles else dense_on_device
        return step(hidden, grad_out, block_rows, block_cols, block_owner)

    return jax.shard_map(
        on_device,
        mesh=mesh,
        in_specs=placed,
        out_specs=P("tensor", "seq", None, None),
        check_vma=False,
    )
```

time: 155 us -> 70.3 us (0.45)
  local copies, waits for them, and re-layouts: 46.4 us -> 2.25 us
  blocking collectives: 53.9 us -> 12.5 us
  starting transfers between devices: 0.01 us -> 21.5 us
  between operations: 13.5 us -> 0.1 us
  waiting for transfers between devices: 36.5 us -> 23.6 us
  Pallas kernels: 0 us -> 10.1 us
  matrix products: 2.17 us -> 0 us
  other arithmetic: 1.92 us -> 0 us
    all_to_all x1, blocking collectives: 53.9 us -> 12.5 us  [scatter(): return lax.all_to_all(value, 'seq', split_axis=0, concat_axis=0, tiled=True)]
    all_gather x1 -> x0, waiting for transfers between devices: 36.5 us -> none  [on_device(): cotangent = lax.all_gather(grad_out, 'tensor', axis=1, tiled=True)]
    ppermute x0 -> x16, waiting for transfers between devices: none -> 23.6 us  [the longest x7 20.6 us: to_peer(): lax.ppermute(value, 'tensor', [(i, i ^ distance) for i in range(tensor_co...]
    reshape x2 -> x0, local copies, waits for them, and re-layouts: 22.1 us -> none  [the longest x1 11.9 us: on_device(): grad_blocks = cotangent.reshape(tok_rows, -1, BLOCK)]
    ppermute x0 -> x16, starting transfers between devices: none -> 21.5 us  [the longest x9 14.2 us: reduce_pieces(): lax.ppermute(sent, 'seq', [(i, i ^ distance) for i in range(seq_count)])]
    unnamed x8 -> x10, local copies, waits for them, and re-layouts: 14 us -> 1.53 us
    gather x3 -> x0, local copies, waits for them, and re-layouts: 10.2 us -> none  [the longest x1 5.33 us: on_device(): grad_sel = jnp.take(grad_blocks, col_ids, axis=1)]
    pallas_call x0 -> x14, Pallas kernels: none -> 10.1 us  [the longest x1 3.63 us: near_products(): pl.pallas_call(functools.partial(near_kernel, width // BLOCK, per_peer, p...]
  transfers between devices with their start and end apart: 1 -> 16, of which waited for: 1 -> 7; matrix products, arithmetic and copies ran while one was open for 16% -> 0% of each run, Pallas kernels for 0% -> 9%
where the time goes in v2:
time: 70.3 us; the launch traced here: 70 us
  waiting for transfers between devices  23.6 us (34%)
  starting transfers between devices  21.5 us (31%)
  blocking collectives  12.5 us (18%)
  Pallas kernels  10.1 us (14%)
  local copies, waits for them, and re-layouts  2.25 us (3%)
    ppermute x7, waiting for transfers between devices, to_peer(): lax.ppermute(value, 'tensor', [(i, i ^ distance) for i in range(tensor_co...  20.6 us
    ppermute x9, starting transfers between devices, reduce_pieces(): lax.ppermute(sent, 'seq', [(i, i ^ distance) for i in range(seq_count)])  14.2 us
    all_to_all x1, blocking collectives, scatter(): return lax.all_to_all(value, 'seq', split_axis=0, concat_axis=0, tiled=True)  12.5 us
    ppermute x7, starting transfers between devices, to_peer(): lax.ppermute(value, 'tensor', [(i, i ^ distance) for i in range(tensor_co...  7.28 us
    pallas_call x1, Pallas kernels, near_products(): pl.pallas_call(functools.partial(near_kernel, width // BLOCK, per_peer, p...  3.63 us
    ppermute x9, waiting for transfers between devices, reduce_pieces(): lax.ppermute(sent, 'seq', [(i, i ^ distance) for i in range(seq_count)])  2.96 us
    pallas_call x1, Pallas kernels, first_sends(): pl.pallas_call(functools.partial(first_kernel, width // BLOCK, per_peer),...  2.84 us
    pallas_call x1, Pallas kernels, guest_products(): pl.pallas_call(functools.partial(guest_kernel, width // BLOCK, per_peer,...  2.15 us
  transfers between devices with their start and end apart: 16, of which 7 were waited for; matrix products, arithmetic and copies ran while one was open for 0% of the time, Pallas kernels for 9%

profile of v2, /device:TPU:0, one launch (start us, length us, event | category | flops | bytes accessed | tf_op | source)
XLA Modules:
  0.0 70.0 jit_solution(874761732627618175)
XLA Ops:
  0.0 0.0 copy-start
  0.0 0.5 collective-permute-start.1
  0.5 1.0 %collective-permute-done.1.list1 = s32[1,24]{1,0:T(1,128)S(1)} collective-permute-done((s32[1,24]{1,0:T(1,128)}, s32[1,24]{1,0:T(1,128)S(1)}, u32[]{:S(2)}, u32[]{:S(2)}) %collective-permute-start.1) | collective-permute-done | bytes 128 | tf_op jit(solution)/shard_map/ppermute | solution.py:281
  1.4 0.0 copy-start.3
  1.5 0.5 copy-done.3
  2.0 2.8 %first_sends.1 = (bf16[6,256,128]{2,1,0:T(8,128)(2,1)}, bf16[6,256,128]{2,1,0:T(8,128)(2,1)S(1)}) custom-call(s32[1,24]{1,0:T(1,128)} %rows.3, s32[1,24]{1,0:T(1,128)} %cols.5, s32[1,24]{1,0:T(1,128)} %copy-done.3, bf16[256,13312]{1,0:T(8,128)(2,1)} %hidden.3, bf16[256,4096]{1,0:T(8,128)(2,1)} %grad_out.5), custom_call_target="tpu_custom_call" | custom-call | tf_op jit(solution)/shard_map/first_sends/pallas_call | solution.py:136
  4.8 0.0 copy-start.1
  4.8 0.4 collective-permute-start.2
  5.2 2.7 %collective-permute-start.7 = (bf16[6,256,128]{2,1,0:T(8,128)(2,1)}, bf16[6,256,128]{2,1,0:T(8,128)(2,1)S(1)}, u32[]{:S(2)}, u32[]{:S(2)}) collective-permute-start(bf16[6,256,128]{2,1,0:T(8,128)(2,1)} %get-tuple-element.34), channel_id=1, source_target_pairs={{0,2},{1,3},{2,0},{3,1},{4,6},{5,7},{6,4},{7,5},{8,10},{9,11},{10,... | collective-permute-start | bytes 1179656 | tf_op jit(solution)/shard_map/ppermute | solution.py:281
  7.9 0.0 copy-done
  7.9 0.0 collective-permute-start
  7.9 9.5 %collective-permute-done.list3 = s32[1,24]{1,0:T(1,128)S(1)} collective-permute-done((s32[1,24]{1,0:T(1,128)S(1)}, s32[1,24]{1,0:T(1,128)S(1)}, u32[]{:S(2)}, u32[]{:S(2)}) %collective-permute-start) | collective-permute-done | bytes 128 | tf_op jit(solution)/shard_map/ppermute | solution.py:281
  17.4 0.0 copy-start.2
  17.4 0.0 collective-permute-done.2.arrived
  17.4 0.5 copy-done.2
  17.9 3.6 %near_products.1 = (f32[4,12,16,128]{3,2,1,0:T(8,128)S(1)}, bf16[4,12,16,128]{3,2,1,0:T(8,128)(2,1)S(1)}, bf16[6,256,128]{2,1,0:T(8,128)(2,1)S(1)}, bf16[6,256,128]{2,1,0:T(8,128)(2,1)}) custom-call(s32[1,24]{1,0:T(1,128)} %rows.3, s32[1,24]{1,0:T(1,128)} %cols.5, s32[1,24]{1,0:T(1,128)} %copy-done.2, bf16[256,13312]{1,0:T(8,128)(2,1)} %hidden.3, ...), custom_call_target="tpu_custom_call" | custom-call | tf_op jit(solution)/shard_map/near_products/pallas_call | solution.py:178
  21.5 1.9 %collective-permute-start.12 = (bf16[6,256,128]{2,1,0:T(8,128)(2,1)}, bf16[6,256,128]{2,1,0:T(8,128)(2,1)S(1)}, u32[]{:S(2)}, u32[]{:S(2)}) collective-permute-start(bf16[6,256,128]{2,1,0:T(8,128)(2,1)} %get-tuple-element.42), channel_id=1, source_target_pairs={{0,3},{1,2},{2,1},{3,0},{4,7},{5,6},{6,5},{7,4},{8,11},{9,10},{10,... | collective-permute-start | bytes 1179656 | tf_op jit(solution)/shard_map/ppermute | solution.py:281
  23.4 1.5 %collective-permute-start.3 = (bf16[4,12,16,128]{3,2,1,0:T(8,128)(2,1)S(1)}, bf16[4,12,16,128]{3,2,1,0:T(8,128)(2,1)S(1)}, u32[]{:S(2)}, u32[]{:S(2)}) collective-permute-start(bf16[4,12,16,128]{3,2,1,0:T(8,128)(2,1)S(1)} %get-tuple-element.29), channel_id=1, source_target_pairs={{0,4},{4,0},{8,12},{12,8},{16,20},{20,16},{24,28},{28,24},{1,5},{5... | collective-permute-start | bytes 589832 | tf_op jit(solution)/shard_map/ppermute | solution.py:289
  24.9 0.0 copy-done.1
  24.9 0.5 collective-permute-start.6
  25.4 7.9 %collective-permute-done.6.list2 = s32[1,24]{1,0:T(1,128)S(1)} collective-permute-done((s32[1,24]{1,0:T(1,128)S(1)}, s32[1,24]{1,0:T(1,128)S(1)}, u32[]{:S(2)}, u32[]{:S(2)}) %collective-permute-start.6) | collective-permute-done | bytes 128 | tf_op jit(solution)/shard_map/ppermute | solution.py:281
  33.3 0.0 collective-permute-done.7.arrived
  33.3 0.5 copy-done.4
  33.8 2.2 %guest_products.1 = (f32[4,6,16,128]{3,2,1,0:T(8,128)S(1)}, bf16[4,6,16,128]{3,2,1,0:T(8,128)(2,1)S(1)}) custom-call(s32[1,24]{1,0:T(1,128)} %copy-done.4, bf16[256,4096]{1,0:T(8,128)(2,1)} %grad_out.5, bf16[6,256,128]{2,1,0:T(8,128)(2,1)S(1)} %collective-permute-done.7.arrived), custom_call_target="tpu_custom_call" | custom-call | tf_op jit(solution)/shard_map/guest_products/pallas_call | solution.py:208
  36.0 1.6 %collective-permute-start.8 = (bf16[4,6,16,128]{3,2,1,0:T(8,128)(2,1)S(1)}, bf16[4,6,16,128]{3,2,1,0:T(8,128)(2,1)S(1)}, u32[]{:S(2)}, u32[]{:S(2)}) collective-permute-start(bf16[4,6,16,128]{3,2,1,0:T(8,128)(2,1)S(1)} %get-tuple-element.36), channel_id=1, source_target_pairs={{0,4},{4,0},{8,12},{12,8},{16,20},{20,16},{24,28},{28,24},{1,5},{5... | collective-permute-start | bytes 294920 | tf_op jit(solution)/shard_map/ppermute | solution.py:289
  37.5 0.0 collective-permute-done.12.arrived
  37.5 0.3 far_products.1
  37.9 0.6 collective-permute-start.13
  38.5 0.0 collective-permute-done.3.received
  38.5 1.6 %collective-permute-start.4 = (bf16[2,12,16,128]{3,2,1,0:T(8,128)(2,1)S(1)}, bf16[2,12,16,128]{3,2,1,0:T(8,128)(2,1)S(1)}, u32[]{:S(2)}, u32[]{:S(2)}) collective-permute-start(bf16[2,12,16,128]{3,2,1,0:T(8,128)(2,1)S(1)} %get-tuple-element.31), channel_id=1, source_target_pairs={{0,8},{4,12},{8,0},{12,4},{16,24},{20,28},{24,16},{28,20},{1,9},{5... | collective-permute-start | bytes 294920 | tf_op jit(solution)/shard_map/ppermute | solution.py:289
  40.2 1.5 %collective-permute-done.8.received = bf16[4,6,16,128]{3,2,1,0:T(8,128)(2,1)S(1)} collective-permute-done((bf16[4,6,16,128]{3,2,1,0:T(8,128)(2,1)S(1)}, bf16[4,6,16,128]{3,2,1,0:T(8,128)(2,1)S(1)}, u32[]{:S(2)}, u32[]{:S(2)}) %collective-permute-start.8) | collective-permute-done | bytes 98336 | tf_op jit(solution)/shard_map/ppermute | solution.py:289
  41.7 1.6 %collective-permute-start.9 = (bf16[2,6,16,128]{3,2,1,0:T(8,128)(2,1)S(1)}, bf16[2,6,16,128]{3,2,1,0:T(8,128)(2,1)S(1)}, u32[]{:S(2)}, u32[]{:S(2)}) collective-permute-start(bf16[2,6,16,128]{3,2,1,0:T(8,128)(2,1)S(1)} %get-tuple-element.38), channel_id=1, source_target_pairs={{0,8},{4,12},{8,0},{12,4},{16,24},{20,28},{24,16},{28,20},{1,9},{5... | collective-permute-start | bytes 147464 | tf_op jit(solution)/shard_map/ppermute | solution.py:289
  43.3 0.0 collective-permute-done.13.received
  43.4 1.0 %collective-permute-start.14 = (bf16[2,6,16,128]{3,2,1,0:T(8,128)(2,1)S(1)}, bf16[2,6,16,128]{3,2,1,0:T(8,128)(2,1)S(1)}, u32[]{:S(2)}, u32[]{:S(2)}) collective-permute-start(bf16[2,6,16,128]{3,2,1,0:T(8,128)(2,1)S(1)} %get-tuple-element.46), channel_id=1, source_target_pairs={{0,8},{4,12},{8,0},{12,4},{16,24},{20,28},{24,16},{28,20},{1,9},{5... | collective-permute-start | bytes 147464 | tf_op jit(solution)/shard_map/ppermute | solution.py:289
  44.4 0.0 collective-permute-done.4.received
  44.4 2.7 %collective-permute-start.5 = (bf16[1,12,16,128]{3,2,1,0:T(8,128)(2,1)S(1)}, bf16[1,12,16,128]{3,2,1,0:T(8,128)(2,1)S(1)}, u32[]{:S(2)}, u32[]{:S(2)}) collective-permute-start(bf16[1,12,16,128]{3,2,1,0:T(8,128)(2,1)S(1)} %get-tuple-element.33), channel_id=1, source_target_pairs={{0,16},{4,20},{8,24},{12,28},{16,0},{20,4},{24,8},{28,12},{1,17},{... | collective-permute-start | bytes 147464 | tf_op jit(solution)/shard_map/ppermute | solution.py:289
  47.1 0.0 collective-permute-done.9.received
  47.1 1.6 %collective-permute-start.10 = (bf16[1,6,16,128]{3,2,1,0:T(8,128)(2,1)S(1)}, bf16[1,6,16,128]{3,2,1,0:T(8,128)(2,1)S(1)}, u32[]{:S(2)}, u32[]{:S(2)}) collective-permute-start(bf16[1,6,16,128]{3,2,1,0:T(8,128)(2,1)S(1)} %get-tuple-element.40), channel_id=1, source_target_pairs={{0,16},{4,20},{8,24},{12,28},{16,0},{20,4},{24,8},{28,12},{1,17},{... | collective-permute-start | bytes 73736 | tf_op jit(solution)/shard_map/ppermute | solution.py:289
  48.7 0.0 collective-permute-done.14.received
  48.7 2.0 %collective-permute-start.15 = (bf16[1,6,16,128]{3,2,1,0:T(8,128)(2,1)S(1)}, bf16[1,6,16,128]{3,2,1,0:T(8,128)(2,1)S(1)}, u32[]{:S(2)}, u32[]{:S(2)}) collective-permute-start(bf16[1,6,16,128]{3,2,1,0:T(8,128)(2,1)S(1)} %get-tuple-element.48), channel_id=1, source_target_pairs={{0,16},{4,20},{8,24},{12,28},{16,0},{20,4},{24,8},{28,12},{1,17},{... | collective-permute-start | bytes 73736 | tf_op jit(solution)/shard_map/ppermute | solution.py:289
  50.7 1.2 %collective-permute-done.10.received = bf16[1,6,16,128]{3,2,1,0:T(8,128)(2,1)S(1)} collective-permute-done((bf16[1,6,16,128]{3,2,1,0:T(8,128)(2,1)S(1)}, bf16[1,6,16,128]{3,2,1,0:T(8,128)(2,1)S(1)}, u32[]{:S(2)}, u32[]{:S(2)}) %collective-permute-start.10) | collective-permute-done | bytes 24608 | tf_op jit(solution)/shard_map/ppermute | solution.py:289
  51.9 1.3 %collective-permute-start.11 = (bf16[6,16,128]{2,1,0:T(8,128)(2,1)S(1)}, bf16[6,16,128]{2,1,0:T(8,128)(2,1)S(1)}, u32[]{:S(2)}, u32[]{:S(2)}) collective-permute-start(bf16[6,16,128]{2,1,0:T(8,128)(2,1)S(1)} %shard_map.60), channel_id=1, source_target_pairs={{0,2},{1,3},{2,0},{3,1},{4,6},{5,7},{6,4},{7,5},{8,10},{9,11},{10,... | collective-permute-start | bytes 73736 | tf_op jit(solution)/shard_map/ppermute | solution.py:281
  53.2 0.0 collective-permute-done.5.received
  53.2 0.2 collective-permute-done.15.received
  53.5 2.3 %collective-permute-done.11.guests = bf16[6,16,128]{2,1,0:T(8,128)(2,1)S(1)} collective-permute-done((bf16[6,16,128]{2,1,0:T(8,128)(2,1)S(1)}, bf16[6,16,128]{2,1,0:T(8,128)(2,1)S(1)}, u32[]{:S(2)}, u32[]{:S(2)}) %collective-permute-start.11) | collective-permute-done | bytes 24608 | tf_op jit(solution)/shard_map/ppermute | solution.py:281
  55.8 0.9 %settle.1 = bf16[8,8,16,128]{3,2,1,0:T(8,128)(2,1)S(1)} custom-call(s32[1,24]{1,0:T(1,128)} %cols.5, s32[1,24]{1,0:T(1,128)} %owners.1, bf16[12,16,128]{2,1,0:T(8,128)(2,1)S(1)} %shard_map.57.near, bf16[6,16,128]{2,1,0:T(8,128)(2,1)S(1)} %collective-permute-done.11.guests, bf16[6,16,128]{2,1,0:T(8,128)(2,1)S(1)} %shard_map.63.far), custom_call_target="tpu_custom_call" | custom-call | tf_op jit(solution)/shard_map/settle/pallas_call | solution.py:265
  56.7 12.5 %all_to_all.5 = bf16[8,8,16,128]{3,2,1,0:T(8,128)(2,1)S(1)} all-to-all(bf16[8,8,16,128]{3,2,1,0:T(8,128)(2,1)S(1)} %settle.1), channel_id=1, replica_groups=mesh['seq'=8,'tensor'=4] {'seq'}, dimensions={0} | all-to-all | bytes 524288 | tf_op jit(solution)/shard_map/all_to_all | solution.py:284
  69.2 0.7 %copy.6 = bf16[8,8,16,128]{3,2,1,0:T(8,128)(2,1)} copy(bf16[8,8,16,128]{3,2,0,1:T(8,128)(2,1)S(1)} %bitcast.2) | data formatting | bytes 524288 | tf_op jit(solution)/shard_map/transpose | solution.py:313
  (10 shorter events, 0.2 us)
Async XLA Ops:
  0.0 7.9 %copy-start = (s32[1,24]{1,0:T(1,128)S(1)}, s32[1,24]{1,0:T(1,128)}, u32[]{:S(2)}) copy-start(s32[1,24]{1,0:T(1,128)} %cols.5) | copy-start | bytes 292
  0.0 1.4 %collective-permute-start.1 = (s32[1,24]{1,0:T(1,128)}, s32[1,24]{1,0:T(1,128)S(1)}, u32[]{:S(2)}, u32[]{:S(2)}) collective-permute-start(s32[1,24]{1,0:T(1,128)} %cols.5), channel_id=1, source_target_pairs={{0,1},{1,0},{2,3},{3,2},{4,5},{5,4},{6,7},{7,6},{8,9},{9,8},{10,11... | collective-permute-start | bytes 296 | tf_op jit(solution)/shard_map/ppermute | solution.py:281
  1.4 0.5 copy-start.3
  4.8 20.1 %copy-start.1 = (s32[1,24]{1,0:T(1,128)S(1)}, s32[1,24]{1,0:T(1,128)}, u32[]{:S(2)}) copy-start(s32[1,24]{1,0:T(1,128)} %cols.5) | copy-start | bytes 292
  4.8 12.6 %collective-permute-start.2 = (bf16[6,256,128]{2,1,0:T(8,128)(2,1)S(1)}, bf16[6,256,128]{2,1,0:T(8,128)(2,1)S(1)}, u32[]{:S(2)}, u32[]{:S(2)}) collective-permute-start(bf16[6,256,128]{2,1,0:T(8,128)(2,1)S(1)} %get-tuple-element.27), channel_id=1, source_target_pairs={{0,1},{1,0},{2,3},{3,2},{4,5},{5,4},{6,7},{7,6},{8,9},{9,8},{10,11... | collective-permute-start | bytes 1179656 | tf_op jit(solution)/shard_map/ppermute | solution.py:281
  5.2 28.1 %collective-permute-start.7 = (bf16[6,256,128]{2,1,0:T(8,128)(2,1)}, bf16[6,256,128]{2,1,0:T(8,128)(2,1)S(1)}, u32[]{:S(2)}, u32[]{:S(2)}) collective-permute-start(bf16[6,256,128]{2,1,0:T(8,128)(2,1)} %get-tuple-element.34), channel_id=1, source_target_pairs={{0,2},{1,3},{2,0},{3,1},{4,6},{5,7},{6,4},{7,5},{8,10},{9,11},{10,... | collective-permute-start | bytes 1179656 | tf_op jit(solution)/shard_map/ppermute | solution.py:281
  7.9 9.5 %collective-permute-start = (s32[1,24]{1,0:T(1,128)S(1)}, s32[1,24]{1,0:T(1,128)S(1)}, u32[]{:S(2)}, u32[]{:S(2)}) collective-permute-start(s32[1,24]{1,0:T(1,128)S(1)} %copy-done), channel_id=1, source_target_pairs={{0,3},{1,2},{2,1},{3,0},{4,7},{5,6},{6,5},{7,4},{8,11},{9,10},{10,... | collective-permute-start | bytes 296 | tf_op jit(solution)/shard_map/ppermute | solution.py:281
  17.4 0.5 copy-start.2
  21.5 16.0 %collective-permute-start.12 = (bf16[6,256,128]{2,1,0:T(8,128)(2,1)}, bf16[6,256,128]{2,1,0:T(8,128)(2,1)S(1)}, u32[]{:S(2)}, u32[]{:S(2)}) collective-permute-start(bf16[6,256,128]{2,1,0:T(8,128)(2,1)} %get-tuple-element.42), channel_id=1, source_target_pairs={{0,3},{1,2},{2,1},{3,0},{4,7},{5,6},{6,5},{7,4},{8,11},{9,10},{10,... | collective-permute-start | bytes 1179656 | tf_op jit(solution)/shard_map/ppermute | solution.py:281
  23.4 15.1 %collective-permute-start.3 = (bf16[4,12,16,128]{3,2,1,0:T(8,128)(2,1)S(1)}, bf16[4,12,16,128]{3,2,1,0:T(8,128)(2,1)S(1)}, u32[]{:S(2)}, u32[]{:S(2)}) collective-permute-start(bf16[4,12,16,128]{3,2,1,0:T(8,128)(2,1)S(1)} %get-tuple-element.29), channel_id=1, source_target_pairs={{0,4},{4,0},{8,12},{12,8},{16,20},{20,16},{24,28},{28,24},{1,5},{5... | collective-permute-start | bytes 589832 | tf_op jit(solution)/shard_map/ppermute | solution.py:289
  24.9 8.4 %collective-permute-start.6 = (s32[1,24]{1,0:T(1,128)S(1)}, s32[1,24]{1,0:T(1,128)S(1)}, u32[]{:S(2)}, u32[]{:S(2)}) collective-permute-start(s32[1,24]{1,0:T(1,128)S(1)} %copy-done.1), channel_id=1, source_target_pairs={{0,2},{1,3},{2,0},{3,1},{4,6},{5,7},{6,4},{7,5},{8,10},{9,11},{10,... | collective-permute-start | bytes 296 | tf_op jit(solution)/shard_map/ppermute | solution.py:281
  33.3 0.5 copy-start.4
  36.0 5.7 %collective-permute-start.8 = (bf16[4,6,16,128]{3,2,1,0:T(8,128)(2,1)S(1)}, bf16[4,6,16,128]{3,2,1,0:T(8,128)(2,1)S(1)}, u32[]{:S(2)}, u32[]{:S(2)}) collective-permute-start(bf16[4,6,16,128]{3,2,1,0:T(8,128)(2,1)S(1)} %get-tuple-element.36), channel_id=1, source_target_pairs={{0,4},{4,0},{8,12},{12,8},{16,20},{20,16},{24,28},{28,24},{1,5},{5... | collective-permute-start | bytes 294920 | tf_op jit(solution)/shard_map/ppermute | solution.py:289
  37.9 5.5 %collective-permute-start.13 = (bf16[4,6,16,128]{3,2,1,0:T(8,128)(2,1)S(1)}, bf16[4,6,16,128]{3,2,1,0:T(8,128)(2,1)S(1)}, u32[]{:S(2)}, u32[]{:S(2)}) collective-permute-start(bf16[4,6,16,128]{3,2,1,0:T(8,128)(2,1)S(1)} %get-tuple-element.44), channel_id=1, source_target_pairs={{0,4},{4,0},{8,12},{12,8},{16,20},{20,16},{24,28},{28,24},{1,5},{5... | collective-permute-start | bytes 294920 | tf_op jit(solution)/shard_map/ppermute | solution.py:289
  38.5 5.9 %collective-permute-start.4 = (bf16[2,12,16,128]{3,2,1,0:T(8,128)(2,1)S(1)}, bf16[2,12,16,128]{3,2,1,0:T(8,128)(2,1)S(1)}, u32[]{:S(2)}, u32[]{:S(2)}) collective-permute-start(bf16[2,12,16,128]{3,2,1,0:T(8,128)(2,1)S(1)} %get-tuple-element.31), channel_id=1, source_target_pairs={{0,8},{4,12},{8,0},{12,4},{16,24},{20,28},{24,16},{28,20},{1,9},{5... | collective-permute-start | bytes 294920 | tf_op jit(solution)/shard_map/ppermute | solution.py:289
  41.7 5.4 %collective-permute-start.9 = (bf16[2,6,16,128]{3,2,1,0:T(8,128)(2,1)S(1)}, bf16[2,6,16,128]{3,2,1,0:T(8,128)(2,1)S(1)}, u32[]{:S(2)}, u32[]{:S(2)}) collective-permute-start(bf16[2,6,16,128]{3,2,1,0:T(8,128)(2,1)S(1)} %get-tuple-element.38), channel_id=1, source_target_pairs={{0,8},{4,12},{8,0},{12,4},{16,24},{20,28},{24,16},{28,20},{1,9},{5... | collective-permute-start | bytes 147464 | tf_op jit(solution)/shard_map/ppermute | solution.py:289
  43.4 5.3 %collective-permute-start.14 = (bf16[2,6,16,128]{3,2,1,0:T(8,128)(2,1)S(1)}, bf16[2,6,16,128]{3,2,1,0:T(8,128)(2,1)S(1)}, u32[]{:S(2)}, u32[]{:S(2)}) collective-permute-start(bf16[2,6,16,128]{3,2,1,0:T(8,128)(2,1)S(1)} %get-tuple-element.46), channel_id=1, source_target_pairs={{0,8},{4,12},{8,0},{12,4},{16,24},{20,28},{24,16},{28,20},{1,9},{5... | collective-permute-start | bytes 147464 | tf_op jit(solution)/shard_map/ppermute | solution.py:289
  44.4 8.8 %collective-permute-start.5 = (bf16[1,12,16,128]{3,2,1,0:T(8,128)(2,1)S(1)}, bf16[1,12,16,128]{3,2,1,0:T(8,128)(2,1)S(1)}, u32[]{:S(2)}, u32[]{:S(2)}) collective-permute-start(bf16[1,12,16,128]{3,2,1,0:T(8,128)(2,1)S(1)} %get-tuple-element.33), channel_id=1, source_target_pairs={{0,16},{4,20},{8,24},{12,28},{16,0},{20,4},{24,8},{28,12},{1,17},{... | collective-permute-start | bytes 147464 | tf_op jit(solution)/shard_map/ppermute | solution.py:289
  47.1 4.8 %collective-permute-start.10 = (bf16[1,6,16,128]{3,2,1,0:T(8,128)(2,1)S(1)}, bf16[1,6,16,128]{3,2,1,0:T(8,128)(2,1)S(1)}, u32[]{:S(2)}, u32[]{:S(2)}) collective-permute-start(bf16[1,6,16,128]{3,2,1,0:T(8,128)(2,1)S(1)} %get-tuple-element.40), channel_id=1, source_target_pairs={{0,16},{4,20},{8,24},{12,28},{16,0},{20,4},{24,8},{28,12},{1,17},{... | collective-permute-start | bytes 73736 | tf_op jit(solution)/shard_map/ppermute | solution.py:289
  48.7 4.8 %collective-permute-start.15 = (bf16[1,6,16,128]{3,2,1,0:T(8,128)(2,1)S(1)}, bf16[1,6,16,128]{3,2,1,0:T(8,128)(2,1)S(1)}, u32[]{:S(2)}, u32[]{:S(2)}) collective-permute-start(bf16[1,6,16,128]{3,2,1,0:T(8,128)(2,1)S(1)} %get-tuple-element.48), channel_id=1, source_target_pairs={{0,16},{4,20},{8,24},{12,28},{16,0},{20,4},{24,8},{28,12},{1,17},{... | collective-permute-start | bytes 73736 | tf_op jit(solution)/shard_map/ppermute | solution.py:289
  51.9 3.9 %collective-permute-start.11 = (bf16[6,16,128]{2,1,0:T(8,128)(2,1)S(1)}, bf16[6,16,128]{2,1,0:T(8,128)(2,1)S(1)}, u32[]{:S(2)}, u32[]{:S(2)}) collective-permute-start(bf16[6,16,128]{2,1,0:T(8,128)(2,1)S(1)} %shard_map.60), channel_id=1, source_target_pairs={{0,2},{1,3},{2,0},{3,1},{4,6},{5,7},{6,4},{7,5},{8,10},{9,11},{10,... | collective-permute-start | bytes 73736 | tf_op jit(solution)/shard_map/ppermute | solution.py:281

commit v3 on v2

--- a/solution.py
+++ b/solution.py
@@ -55,17 +55,13 @@
 
 
 def listed_at(table, cols, values, owner, cols_per, per_peer):
-    for j in range(per_peer):
-        table[j] = 0
-
-    def visit(k, found):
-        local = cols[0, k] - owner * cols_per
+    listed = [cols[0, k] - owner * cols_per for k in range(cols.shape[1])]
+    taken = listed if values is None else [values[0, k] for k in range(cols.shape[1])]
+    found = jnp.int32(0)
+    for local, value in zip(listed, taken):
         hit = jnp.logical_and(local >= 0, local < cols_per)
-        value = local if values is None else values[0, k]
         table[jnp.where(hit, jnp.minimum(found, per_peer - 1), per_peer)] = value
-        return found + hit.astype(jnp.int32)
-
-    lax.fori_loop(0, cols.shape[1], visit, jnp.int32(0), unroll=True)
+        found += hit.astype(jnp.int32)
 
 
 def split_pieces(parts, kept, sent):
@@ -78,29 +74,42 @@
         sent[index] = parts[me ^ apart ^ 1].astype(jnp.bfloat16)
 
 
-def halve_kernel(kept, received, still, sent):
+def halve_kernel(*refs):
+    parts, (still, sent) = refs[:-2], refs[-2:]
     half = still.shape[0]
-    still[...] = kept[:half] + received[:half].astype(jnp.float32)
-    sent[...] = (kept[half:] + received[half:].astype(jnp.float32)).astype(jnp.bfloat16)
-
-
-def halve(kept, received):
-    shape = (kept.shape[0] // 2,) + kept.shape[1:]
+    first = 0
+    for kept, received in zip(parts[0::2], parts[1::2]):
+        items = pl.ds(first, kept.shape[1])
+        still[:, items] = kept[:half] + received[:half].astype(jnp.float32)
+        sent[:, items] = (kept[half:] + received[half:].astype(jnp.float32)).astype(jnp.bfloat16)
+        first += kept.shape[1]
+
+
+def halve(parts):
+    half, _, rows, _ = parts[0][0].shape
+    shape = (half // 2, sum(kept.shape[1] for kept, _ in parts), rows, BLOCK)
     return pl.pallas_call(
         halve_kernel,
         out_shape=[pltpu.VMEM(shape, jnp.float32), pltpu.VMEM(shape, jnp.bfloat16)],
+        in_specs=[VMEM] * (2 * len(parts)),
+        out_specs=[VMEM, VMEM],
+    )(*[vectors(value) for part in parts for value in part])
+
+
+def finish_kernel(kept, received, *outs):
+    first = 0
+    for out in outs:
+        items = pl.ds(first, out.shape[0])
+        out[...] = (kept[0, items] + received[0, items].astype(jnp.float32)).astype(jnp.bfloat16)
+        first += out.shape[0]
+
+
+def finish(kept, received, counts):
+    return pl.pallas_call(
+        finish_kernel,
+        out_shape=[pltpu.VMEM((count,) + kept.shape[2:], jnp.bfloat16) for count in counts],
         in_specs=[VMEM, VMEM],
-        out_specs=[VMEM, VMEM],
-    )(vectors(kept), vectors(received))
-
-
-def finish_kernel(kept, received, out):
-    out[...] = (kept[0] + received[0].astype(jnp.float32)).astype(jnp.bfloat16)
-
-
-def finish(kept, received):
-    return pl.pallas_call(
-        finish_kernel, out_shape=pltpu.VMEM(kept.shape[1:], jnp.bfloat16), in_specs=[VMEM, VMEM], out_specs=VMEM
+        out_specs=[VMEM] * len(counts),
     )(vectors(kept), vectors(received))
 
 
@@ -114,36 +123,51 @@
     return product.reshape(pieces, BLOCK // pieces, BLOCK)
 
 
-def first_kernel(cols_per, per_peer, rows, cols, list1, hidden, grad_out, pushed, for_core, table, sems):
+def push_kernel(cols_per, per_peer, rows, cols, hidden, pushed, table, sems):
+    listed_at(table, cols, rows, lax.axis_index("tensor") ^ 2, cols_per, per_peer)
+    copies = [pltpu.make_async_copy(column(hidden, table[j]), pushed.at[j], sems.at[j]) for j in range(per_peer)]
+    for copy in copies:
+        copy.start()
+    for copy in copies:
+        copy.wait()
+
+
+def push_blocks(rows, cols, hidden, cols_per, per_peer):
+    return pl.pallas_call(
+        functools.partial(push_kernel, cols_per, per_peer),
+        out_shape=pltpu.VMEM((per_peer, hidden.shape[0], BLOCK), hidden.dtype),
+        in_specs=[SMEM, SMEM, HBM],
+        out_specs=VMEM,
+        scratch_shapes=[pltpu.SMEM((per_peer + 1,), jnp.int32), pltpu.SemaphoreType.DMA((per_peer,))],
+        name="push_blocks",
+    )(scalars(rows), scalars(cols), hidden)
+
+
+def pack_kernel(cols_per, per_peer, list1, list3, grad_out, for_core, for_far, table, sems):
     me = lax.axis_index("tensor")
     copies = []
-
-    def gather(n, source, there):
+    for n, (listed, there) in enumerate(((list1, for_core), (list3, for_far))):
+        listed_at(table, listed, None, me, cols_per, per_peer)
         for j in range(per_peer):
-            copies.append(pltpu.make_async_copy(column(source, table[j]), there.at[j], sems.at[n, j]))
+            copies.append(pltpu.make_async_copy(column(grad_out, table[j]), there.at[j], sems.at[n, j]))
             copies[-1].start()
-
-    listed_at(table, cols, rows, me ^ 2, cols_per, per_peer)
-    gather(0, hidden, pushed)
-    listed_at(table, list1, None, me, cols_per, per_peer)
-    gather(1, grad_out, for_core)
-    for copy in copies:
-        copy.wait()
-
-
-def first_sends(rows, cols, list1, hidden, grad_out, per_peer):
+    for copy in copies:
+        copy.wait()
+
+
+def pack_columns(list1, list3, grad_out, per_peer):
     tok_rows, width = grad_out.shape
     return pl.pallas_call(
-        functools.partial(first_kernel, width // BLOCK, per_peer),
+        functools.partial(pack_kernel, width // BLOCK, per_peer),
         out_shape=[pltpu.VMEM((per_peer, tok_rows, BLOCK), grad_out.dtype)] * 2,
-        in_specs=[SMEM, SMEM, SMEM, HBM, HBM],
+        in_specs=[SMEM, SMEM, HBM],
         out_specs=[VMEM, VMEM],
         scratch_shapes=[pltpu.SMEM((per_peer + 1,), jnp.int32), pltpu.SemaphoreType.DMA((2, per_peer))],
-        name="first_sends",
-    )(scalars(rows), scalars(cols), scalars(list1), hidden, grad_out)
-
-
-def near_kernel(cols_per, per_peer, pieces, rows, cols, list3, hidden, grad_out, arrived, kept, sent, hidden_far, for_far, hidden_near, grad_near, parts, table, sems):
+        name="pack_columns",
+    )(scalars(list1), scalars(list3), grad_out)
+
+
+def near_kernel(cols_per, per_peer, pieces, rows, cols, hidden, grad_out, arrived, kept, sent, hidden_far, hidden_near, grad_near, parts, table, sems):
     me = lax.axis_index("tensor")
     count = [0]
 
@@ -159,8 +183,7 @@
     mine = gather(me, cols, None, grad_out, grad_near, 0)
     near = gather(me, cols, rows, hidden, hidden_near, 0)
     near += gather(me ^ 1, cols, rows, hidden, hidden_near, per_peer)
-    later = gather(me, list3, None, grad_out, for_far, 0)
-    later += gather(me ^ 3, cols, rows, hidden, hidden_far, 0)
+    later = gather(me ^ 3, cols, rows, hidden, hidden_far, 0)
     for copy in mine + near:
         copy.wait()
     for item in range(2 * per_peer):
@@ -171,24 +194,24 @@
         copy.wait()
 
 
-def near_products(rows, cols, list3, hidden, grad_out, arrived, per_peer, pieces):
+def near_products(rows, cols, hidden, grad_out, arrived, per_peer, pieces):
     tok_rows, width = grad_out.shape
     near = 2 * per_peer
     blocks = pltpu.VMEM((per_peer, tok_rows, BLOCK), jnp.bfloat16)
     return pl.pallas_call(
         functools.partial(near_kernel, width // BLOCK, per_peer, pieces),
-        out_shape=halved_shapes(pieces, near) + [blocks, blocks],
-        in_specs=[SMEM, SMEM, SMEM, HBM, HBM, VMEM],
-        out_specs=[VMEM] * 4,
+        out_shape=halved_shapes(pieces, near) + [blocks],
+        in_specs=[SMEM, SMEM, HBM, HBM, VMEM],
+        out_specs=[VMEM] * 3,
         scratch_shapes=[
             pltpu.VMEM((near, tok_rows, BLOCK), jnp.bfloat16),
             pltpu.VMEM((per_peer, tok_rows, BLOCK), jnp.bfloat16),
             pltpu.VMEM((pieces, near, BLOCK // pieces, BLOCK), jnp.float32),
             pltpu.SMEM((per_peer + 1,), jnp.int32),
-            pltpu.SemaphoreType.DMA((5, per_peer)),
+            pltpu.SemaphoreType.DMA((4, per_peer)),
         ],
         name="near_products",
-    )(scalars(rows), scalars(cols), scalars(list3), hidden, grad_out, vectors(arrived))
+    )(scalars(rows), scalars(cols), hidden, grad_out, vectors(arrived))
 
 
 def guest_kernel(cols_per, per_peer, pieces, list2, grad_out, arrived, kept, sent, right, parts, table, sems):
@@ -247,17 +270,20 @@
     summed[pl.ds(3 * per_peer, per_peer)] = far[...]
     out[...] = jnp.zeros_like(out)
 
-    def visit(k, carry):
-        last_owner, last_slot = carry
-        distance = (cols[0, k] // cols_per) ^ me
-        rank = seen[distance]
-        seen[distance] = rank + 1
-        owner = owners[0, k]
-        slot = jnp.where(owner == last_owner, last_slot + 1, 0)
-        out[owner, jnp.minimum(slot, CAP - 1)] = summed[distance * per_peer + jnp.minimum(rank, per_peer - 1)]
-        return owner, slot
-
-    lax.fori_loop(0, cols.shape[1], visit, (jnp.int32(-1), jnp.int32(0)), unroll=True)
+    listed = range(cols.shape[1])
+    distances = [lax.shift_right_logical(cols[0, k], cols_per.bit_length() - 1) ^ me for k in listed]
+    placed_at = [owners[0, k] for k in listed]
+    slot = jnp.int32(0)
+    ranks = []
+    for k in listed:
+        rank = seen[distances[k]]
+        seen[distances[k]] = rank + 1
+        ranks.append(rank)
+    for k in listed:
+        slot = jnp.where(placed_at[k] == placed_at[k - 1], slot + 1, 0) if k else slot
+        out[placed_at[k], jnp.minimum(slot, CAP - 1)] = summed[
+            distances[k] * per_peer + jnp.minimum(ranks[k], per_peer - 1)
+        ]
 
 
 def settle(cols, owners, near, guests, far, cols_per, pieces):
@@ -283,25 +309,29 @@
     def scatter(value):
         return lax.all_to_all(value, "seq", split_axis=0, concat_axis=0, tiled=True)
 
+    def exchange(sent, distance):
+        return lax.ppermute(sent, "seq", [(i, i ^ distance) for i in range(seq_count)])
+
     def reduce_pieces(kept, sent):
         distance = 1
         while True:
-            received = lax.ppermute(sent, "seq", [(i, i ^ distance) for i in range(seq_count)])
-            if kept.shape[0] == 1:
-                return finish(kept, received)
-            kept, sent = halve(kept, received)
+            received = exchange(sent, distance)
             distance *= 2
+            if distance == seq_count:
+                return finish(kept, received, (kept.shape[1],))[0]
+            kept, sent = halve([(kept, received)])
 
     list3 = to_peer(block_cols, 3)
+    pushed = push_blocks(block_rows, block_cols, hidden, cols_per, per_peer)
+    guests = to_peer(pushed, 2)
     list1 = to_peer(block_cols, 1)
     list2 = to_peer(block_cols, 2)
-    pushed, for_core = first_sends(block_rows, block_cols, list1, hidden, grad_out, per_peer)
-    guests = to_peer(pushed, 2)
+    for_core, for_far = pack_columns(list1, list3, grad_out, per_peer)
     from_core = to_peer(for_core, 1)
-    near_kept, near_sent, hidden_far, for_far = near_products(
-        block_rows, block_cols, list3, hidden, grad_out, from_core, per_peer, seq_count
+    from_far = to_peer(for_far, 3)
+    near_kept, near_sent, hidden_far = near_products(
+        block_rows, block_cols, hidden, grad_out, from_core, per_peer, seq_count
     )
-    from_far = to_peer(for_far, 3)
     near_sum = reduce_pieces(near_kept, near_sent)
     guest_kept, guest_sent = guest_products(list2, grad_out, guests, per_peer, seq_count)
     guest_sum = reduce_pieces(guest_kept, guest_sent)

time: 70.3 us -> 66.4 us (0.945)
  waiting for transfers between devices: 23.6 us -> 18.7 us
    ppermute x7, waiting for transfers between devices: 20.6 us -> 15.2 us  [to_peer(): lax.ppermute(value, 'tensor', [(i, i ^ distance) for i in range(tensor_co...]
    pallas_call x4 -> x5, Pallas kernels: 2.88 us -> 3.96 us  [the longest x1 2.07 us: pack_columns(): pl.pallas_call(functools.partial(pack_kernel, width // BLOCK, per_peer),...]
    ppermute x7, starting transfers between devices: 7.28 us -> 8.27 us  [to_peer(): lax.ppermute(value, 'tensor', [(i, i ^ distance) for i in range(tensor_co...]
    pallas_call x1, Pallas kernels: 3.63 us -> 2.8 us  [near_products(): pl.pallas_call(functools.partial(near_kernel, width // BLOCK, per_peer, p...]
    unnamed x10 -> x8, local copies, waits for them, and re-layouts: 1.53 us -> 1.05 us
  transfers between devices with their start and end apart: 16 -> 16, of which waited for: 7 -> 6; matrix products, arithmetic and copies ran while one was open for 0% -> 0% of each run, Pallas kernels for 9% -> 11%
where the time goes in v3:
time: 66.4 us; the launch traced here: 65.9 us
  starting transfers between devices  22.1 us (33%)
  waiting for transfers between devices  18.7 us (28%)
  blocking collectives  13.1 us (20%)
  Pallas kernels  10.2 us (15%)
  local copies, waits for them, and re-layouts  1.77 us (3%)
    ppermute x7, waiting for transfers between devices, to_peer(): lax.ppermute(value, 'tensor', [(i, i ^ distance) for i in range(tensor_co...  15.2 us
    ppermute x9, starting transfers between devices, exchange(): lax.ppermute(sent, 'seq', [(i, i ^ distance) for i in range(seq_count)])  13.8 us
    all_to_all x1, blocking collectives, scatter(): return lax.all_to_all(value, 'seq', split_axis=0, concat_axis=0, tiled=True)  13.1 us
    ppermute x7, starting transfers between devices, to_peer(): lax.ppermute(value, 'tensor', [(i, i ^ distance) for i in range(tensor_co...  8.27 us
    ppermute x9, waiting for transfers between devices, exchange(): lax.ppermute(sent, 'seq', [(i, i ^ distance) for i in range(seq_count)])  3.47 us
    pallas_call x1, Pallas kernels, near_products(): pl.pallas_call(functools.partial(near_kernel, width // BLOCK, per_peer, p...  2.8 us
    pallas_call x1, Pallas kernels, guest_products(): pl.pallas_call(functools.partial(guest_kernel, width // BLOCK, per_peer,...  2.15 us
    pallas_call x1, Pallas kernels, pack_columns(): pl.pallas_call(functools.partial(pack_kernel, width // BLOCK, per_peer),...  2.07 us
  transfers between devices with their start and end apart: 16, of which 6 were waited for; matrix products, arithmetic and copies ran while one was open for 0% of the time, Pallas kernels for 11%

profile of v3, /device:TPU:0, one launch (start us, length us, event | category | flops | bytes accessed | tf_op | source)
XLA Modules:
  0.0 65.9 jit_solution(5673089058886020975)
XLA Ops:
  0.0 0.5 collective-permute-start
  0.5 2.6 %collective-permute-start.1 = (s32[1,24]{1,0:T(1,128)}, s32[1,24]{1,0:T(1,128)S(1)}, u32[]{:S(2)}, u32[]{:S(2)}) collective-permute-start(s32[1,24]{1,0:T(1,128)} %cols.5), channel_id=1, source_target_pairs={{0,3},{1,2},{2,1},{3,0},{4,7},{5,6},{6,5},{7,4},{8,11},{9,10},{10,... | collective-permute-start | bytes 296 | tf_op jit(solution)/shard_map/ppermute | solution.py:307
  3.1 0.0 collective-permute-done.list1
  3.1 0.0 copy-start.1
  3.1 1.4 %collective-permute-done.1.list3 = s32[1,24]{1,0:T(1,128)S(1)} collective-permute-done((s32[1,24]{1,0:T(1,128)}, s32[1,24]{1,0:T(1,128)S(1)}, u32[]{:S(2)}, u32[]{:S(2)}) %collective-permute-start.1) | collective-permute-done | bytes 128 | tf_op jit(solution)/shard_map/ppermute | solution.py:307
  4.5 0.0 copy-done.1
  4.5 0.0 copy-start.3
  4.5 0.5 copy-done.3
  5.1 2.1 %pack_columns.1 = (bf16[6,256,128]{2,1,0:T(8,128)(2,1)S(1)}, bf16[6,256,128]{2,1,0:T(8,128)(2,1)S(1)}) custom-call(s32[1,24]{1,0:T(1,128)} %copy-done.1, s32[1,24]{1,0:T(1,128)} %copy-done.3, bf16[256,4096]{1,0:T(8,128)(2,1)} %grad_out.5), custom_call_target="tpu_custom_call" | custom-call | tf_op jit(solution)/shard_map/pack_columns/pallas_call | solution.py:160
  7.2 0.0 copy-start
  7.2 0.1 collective-permute-start.2
  7.2 1.8 %push_blocks.1 = bf16[6,256,128]{2,1,0:T(8,128)(2,1)S(1)} custom-call(s32[1,24]{1,0:T(1,128)} %rows.3, s32[1,24]{1,0:T(1,128)} %cols.5, bf16[256,13312]{1,0:T(8,128)(2,1)} %hidden.3), custom_call_target="tpu_custom_call" | custom-call | tf_op jit(solution)/shard_map/push_blocks/pallas_call | solution.py:136
  9.1 2.1 %collective-permute-start.7 = (bf16[6,256,128]{2,1,0:T(8,128)(2,1)S(1)}, bf16[6,256,128]{2,1,0:T(8,128)(2,1)S(1)}, u32[]{:S(2)}, u32[]{:S(2)}) collective-permute-start(bf16[6,256,128]{2,1,0:T(8,128)(2,1)S(1)} %push_blocks.1), channel_id=1, source_target_pairs={{0,2},{1,3},{2,0},{3,1},{4,6},{5,7},{6,4},{7,5},{8,10},{9,11},{10,... | collective-permute-start | bytes 1179656 | tf_op jit(solution)/shard_map/ppermute | solution.py:307
  11.2 0.0 collective-permute-start.12
  11.2 0.0 collective-permute-done.2.arrived
  11.3 2.8 %near_products.1 = (f32[4,12,16,128]{3,2,1,0:T(8,128)S(1)}, bf16[4,12,16,128]{3,2,1,0:T(8,128)(2,1)S(1)}, bf16[6,256,128]{2,1,0:T(8,128)(2,1)S(1)}) custom-call(s32[1,24]{1,0:T(1,128)} %rows.3, s32[1,24]{1,0:T(1,128)} %cols.5, bf16[256,13312]{1,0:T(8,128)(2,1)} %hidden.3, bf16[256,4096]{1,0:T(8,128)(2,1)} %grad_out.5, ...), custom_call_target="tpu_custom_call" | custom-call | tf_op jit(solution)/shard_map/near_products/pallas_call | solution.py:201
  14.1 1.6 %collective-permute-start.3 = (bf16[4,12,16,128]{3,2,1,0:T(8,128)(2,1)S(1)}, bf16[4,12,16,128]{3,2,1,0:T(8,128)(2,1)S(1)}, u32[]{:S(2)}, u32[]{:S(2)}) collective-permute-start(bf16[4,12,16,128]{3,2,1,0:T(8,128)(2,1)S(1)} %get-tuple-element.28), channel_id=1, source_target_pairs={{0,4},{4,0},{8,12},{12,8},{16,20},{20,16},{24,28},{28,24},{1,5},{5... | collective-permute-start | bytes 589832 | tf_op jit(solution)/shard_map/ppermute | solution.py:313
  15.6 0.0 copy-done
  15.6 1.4 %collective-permute-start.6 = (s32[1,24]{1,0:T(1,128)S(1)}, s32[1,24]{1,0:T(1,128)S(1)}, u32[]{:S(2)}, u32[]{:S(2)}) collective-permute-start(s32[1,24]{1,0:T(1,128)S(1)} %copy-done), channel_id=1, source_target_pairs={{0,2},{1,3},{2,0},{3,1},{4,6},{5,7},{6,4},{7,5},{8,10},{9,11},{10,... | collective-permute-start | bytes 296 | tf_op jit(solution)/shard_map/ppermute | solution.py:307
  17.0 12.1 %collective-permute-done.6.list2 = s32[1,24]{1,0:T(1,128)S(1)} collective-permute-done((s32[1,24]{1,0:T(1,128)S(1)}, s32[1,24]{1,0:T(1,128)S(1)}, u32[]{:S(2)}, u32[]{:S(2)}) %collective-permute-start.6) | collective-permute-done | bytes 128 | tf_op jit(solution)/shard_map/ppermute | solution.py:307
  29.1 0.0 copy-start.2
  29.1 0.0 collective-permute-done.7.arrived
  29.1 0.5 copy-done.2
  29.6 2.2 %guest_products.1 = (f32[4,6,16,128]{3,2,1,0:T(8,128)S(1)}, bf16[4,6,16,128]{3,2,1,0:T(8,128)(2,1)S(1)}) custom-call(s32[1,24]{1,0:T(1,128)} %copy-done.2, bf16[256,4096]{1,0:T(8,128)(2,1)} %grad_out.5, bf16[6,256,128]{2,1,0:T(8,128)(2,1)S(1)} %collective-permute-done.7.arrived), custom_call_target="tpu_custom_call" | custom-call | tf_op jit(solution)/shard_map/guest_products/pallas_call | solution.py:231
  31.8 1.6 %collective-permute-start.8 = (bf16[4,6,16,128]{3,2,1,0:T(8,128)(2,1)S(1)}, bf16[4,6,16,128]{3,2,1,0:T(8,128)(2,1)S(1)}, u32[]{:S(2)}, u32[]{:S(2)}) collective-permute-start(bf16[4,6,16,128]{3,2,1,0:T(8,128)(2,1)S(1)} %get-tuple-element.34), channel_id=1, source_target_pairs={{0,4},{4,0},{8,12},{12,8},{16,20},{20,16},{24,28},{28,24},{1,5},{5... | collective-permute-start | bytes 294920 | tf_op jit(solution)/shard_map/ppermute | solution.py:313
  33.4 0.0 collective-permute-done.12.arrived
  33.4 0.3 far_products.1
  33.8 0.5 collective-permute-start.13
  34.3 0.0 collective-permute-done.3.refs_1_
  34.3 1.7 %collective-permute-start.4 = (bf16[2,12,16,128]{3,2,1,0:T(8,128)(2,1)S(1)}, bf16[2,12,16,128]{3,2,1,0:T(8,128)(2,1)S(1)}, u32[]{:S(2)}, u32[]{:S(2)}) collective-permute-start(bf16[2,12,16,128]{3,2,1,0:T(8,128)(2,1)S(1)} %get-tuple-element.30), channel_id=1, source_target_pairs={{0,8},{4,12},{8,0},{12,4},{16,24},{20,28},{24,16},{28,20},{1,9},{5... | collective-permute-start | bytes 294920 | tf_op jit(solution)/shard_map/ppermute | solution.py:313
  36.1 1.4 %collective-permute-done.8.refs_1_ = bf16[4,6,16,128]{3,2,1,0:T(8,128)(2,1)S(1)} collective-permute-done((bf16[4,6,16,128]{3,2,1,0:T(8,128)(2,1)S(1)}, bf16[4,6,16,128]{3,2,1,0:T(8,128)(2,1)S(1)}, u32[]{:S(2)}, u32[]{:S(2)}) %collective-permute-start.8) | collective-permute-done | bytes 98336 | tf_op jit(solution)/shard_map/ppermute | solution.py:313
  37.4 1.6 %collective-permute-start.9 = (bf16[2,6,16,128]{3,2,1,0:T(8,128)(2,1)S(1)}, bf16[2,6,16,128]{3,2,1,0:T(8,128)(2,1)S(1)}, u32[]{:S(2)}, u32[]{:S(2)}) collective-permute-start(bf16[2,6,16,128]{3,2,1,0:T(8,128)(2,1)S(1)} %get-tuple-element.36), channel_id=1, source_target_pairs={{0,8},{4,12},{8,0},{12,4},{16,24},{20,28},{24,16},{28,20},{1,9},{5... | collective-permute-start | bytes 147464 | tf_op jit(solution)/shard_map/ppermute | solution.py:313
  39.1 0.0 collective-permute-done.13.refs_1_
  39.1 1.0 %collective-permute-start.14 = (bf16[2,6,16,128]{3,2,1,0:T(8,128)(2,1)S(1)}, bf16[2,6,16,128]{3,2,1,0:T(8,128)(2,1)S(1)}, u32[]{:S(2)}, u32[]{:S(2)}) collective-permute-start(bf16[2,6,16,128]{3,2,1,0:T(8,128)(2,1)S(1)} %get-tuple-element.44), channel_id=1, source_target_pairs={{0,8},{4,12},{8,0},{12,4},{16,24},{20,28},{24,16},{28,20},{1,9},{5... | collective-permute-start | bytes 147464 | tf_op jit(solution)/shard_map/ppermute | solution.py:313
  40.1 1.5 %collective-permute-done.9.refs_1_ = bf16[2,6,16,128]{3,2,1,0:T(8,128)(2,1)S(1)} collective-permute-done((bf16[2,6,16,128]{3,2,1,0:T(8,128)(2,1)S(1)}, bf16[2,6,16,128]{3,2,1,0:T(8,128)(2,1)S(1)}, u32[]{:S(2)}, u32[]{:S(2)}) %collective-permute-start.9) | collective-permute-done | bytes 49184 | tf_op jit(solution)/shard_map/ppermute | solution.py:313
  41.6 2.7 %collective-permute-start.10 = (bf16[1,6,16,128]{3,2,1,0:T(8,128)(2,1)S(1)}, bf16[1,6,16,128]{3,2,1,0:T(8,128)(2,1)S(1)}, u32[]{:S(2)}, u32[]{:S(2)}) collective-permute-start(bf16[1,6,16,128]{3,2,1,0:T(8,128)(2,1)S(1)} %get-tuple-element.38), channel_id=1, source_target_pairs={{0,16},{4,20},{8,24},{12,28},{16,0},{20,4},{24,8},{28,12},{1,17},{... | collective-permute-start | bytes 73736 | tf_op jit(solution)/shard_map/ppermute | solution.py:313
  44.3 0.0 collective-permute-done.4.refs_1_
  44.3 0.4 collective-permute-start.5
  44.7 0.0 collective-permute-done.14.refs_1_
  44.7 2.7 %collective-permute-start.15 = (bf16[1,6,16,128]{3,2,1,0:T(8,128)(2,1)S(1)}, bf16[1,6,16,128]{3,2,1,0:T(8,128)(2,1)S(1)}, u32[]{:S(2)}, u32[]{:S(2)}) collective-permute-start(bf16[1,6,16,128]{3,2,1,0:T(8,128)(2,1)S(1)} %get-tuple-element.46), channel_id=1, source_target_pairs={{0,16},{4,20},{8,24},{12,28},{16,0},{20,4},{24,8},{28,12},{1,17},{... | collective-permute-start | bytes 73736 | tf_op jit(solution)/shard_map/ppermute | solution.py:313
  47.4 0.0 collective-permute-done.10.received
  47.4 1.6 %collective-permute-start.11 = (bf16[6,16,128]{2,1,0:T(8,128)(2,1)S(1)}, bf16[6,16,128]{2,1,0:T(8,128)(2,1)S(1)}, u32[]{:S(2)}, u32[]{:S(2)}) collective-permute-start(bf16[6,16,128]{2,1,0:T(8,128)(2,1)S(1)} %shard_map.60), channel_id=1, source_target_pairs={{0,2},{1,3},{2,0},{3,1},{4,6},{5,7},{6,4},{7,5},{8,10},{9,11},{10,... | collective-permute-start | bytes 73736 | tf_op jit(solution)/shard_map/ppermute | solution.py:307
  49.0 0.6 collective-permute-done.15.received
  49.6 0.0 collective-permute-done.5.received
  49.6 1.6 %collective-permute-done.11.guests = bf16[6,16,128]{2,1,0:T(8,128)(2,1)S(1)} collective-permute-done((bf16[6,16,128]{2,1,0:T(8,128)(2,1)S(1)}, bf16[6,16,128]{2,1,0:T(8,128)(2,1)S(1)}, u32[]{:S(2)}, u32[]{:S(2)}) %collective-permute-start.11) | collective-permute-done | bytes 24608 | tf_op jit(solution)/shard_map/ppermute | solution.py:307
  51.3 0.9 %settle.1 = bf16[8,8,16,128]{3,2,1,0:T(8,128)(2,1)S(1)} custom-call(s32[1,24]{1,0:T(1,128)} %cols.5, s32[1,24]{1,0:T(1,128)} %owners.1, bf16[12,16,128]{2,1,0:T(8,128)(2,1)S(1)} %shard_map.57.near, bf16[6,16,128]{2,1,0:T(8,128)(2,1)S(1)} %collective-permute-done.11.guests, bf16[6,16,128]{2,1,0:T(8,128)(2,1)S(1)} %shard_map.63.far), custom_call_target="tpu_custom_call" | custom-call | tf_op jit(solution)/shard_map/settle/pallas_call | solution.py:291
  52.1 13.1 %all_to_all.5 = bf16[8,8,16,128]{3,2,1,0:T(8,128)(2,1)S(1)} all-to-all(bf16[8,8,16,128]{3,2,1,0:T(8,128)(2,1)S(1)} %settle.1), channel_id=1, replica_groups=mesh['seq'=8,'tensor'=4] {'seq'}, dimensions={0} | all-to-all | bytes 524288 | tf_op jit(solution)/shard_map/all_to_all | solution.py:310
  65.2 0.7 %copy.6 = bf16[8,8,16,128]{3,2,1,0:T(8,128)(2,1)} copy(bf16[8,8,16,128]{3,2,0,1:T(8,128)(2,1)S(1)} %bitcast.2) | data formatting | bytes 524288 | tf_op jit(solution)/shard_map/transpose | solution.py:343
  (9 shorter events, 0.2 us)
Async XLA Ops:
  0.0 3.1 %collective-permute-start = (s32[1,24]{1,0:T(1,128)}, s32[1,24]{1,0:T(1,128)S(1)}, u32[]{:S(2)}, u32[]{:S(2)}) collective-permute-start(s32[1,24]{1,0:T(1,128)} %cols.5), channel_id=1, source_target_pairs={{0,1},{1,0},{2,3},{3,2},{4,5},{5,4},{6,7},{7,6},{8,9},{9,8},{10,11... | collective-permute-start | bytes 296 | tf_op jit(solution)/shard_map/ppermute | solution.py:307
  0.5 4.0 %collective-permute-start.1 = (s32[1,24]{1,0:T(1,128)}, s32[1,24]{1,0:T(1,128)S(1)}, u32[]{:S(2)}, u32[]{:S(2)}) collective-permute-start(s32[1,24]{1,0:T(1,128)} %cols.5), channel_id=1, source_target_pairs={{0,3},{1,2},{2,1},{3,0},{4,7},{5,6},{6,5},{7,4},{8,11},{9,10},{10,... | collective-permute-start | bytes 296 | tf_op jit(solution)/shard_map/ppermute | solution.py:307
  3.1 1.4 %copy-start.1 = (s32[1,24]{1,0:T(1,128)}, s32[1,24]{1,0:T(1,128)S(1)}, u32[]{:S(2)}) copy-start(s32[1,24]{1,0:T(1,128)S(1)} %collective-permute-done.list1) | copy-start | bytes 292
  4.5 0.5 copy-start.3
  7.2 8.5 %copy-start = (s32[1,24]{1,0:T(1,128)S(1)}, s32[1,24]{1,0:T(1,128)}, u32[]{:S(2)}) copy-start(s32[1,24]{1,0:T(1,128)} %cols.5) | copy-start | bytes 292
  7.2 4.1 %collective-permute-start.2 = (bf16[6,256,128]{2,1,0:T(8,128)(2,1)S(1)}, bf16[6,256,128]{2,1,0:T(8,128)(2,1)S(1)}, u32[]{:S(2)}, u32[]{:S(2)}) collective-permute-start(bf16[6,256,128]{2,1,0:T(8,128)(2,1)S(1)} %get-tuple-element.26), channel_id=1, source_target_pairs={{0,1},{1,0},{2,3},{3,2},{4,5},{5,4},{6,7},{7,6},{8,9},{9,8},{10,11... | collective-permute-start | bytes 1179656 | tf_op jit(solution)/shard_map/ppermute | solution.py:307
  9.1 20.0 %collective-permute-start.7 = (bf16[6,256,128]{2,1,0:T(8,128)(2,1)S(1)}, bf16[6,256,128]{2,1,0:T(8,128)(2,1)S(1)}, u32[]{:S(2)}, u32[]{:S(2)}) collective-permute-start(bf16[6,256,128]{2,1,0:T(8,128)(2,1)S(1)} %push_blocks.1), channel_id=1, source_target_pairs={{0,2},{1,3},{2,0},{3,1},{4,6},{5,7},{6,4},{7,5},{8,10},{9,11},{10,... | collective-permute-start | bytes 1179656 | tf_op jit(solution)/shard_map/ppermute | solution.py:307
  11.2 22.2 %collective-permute-start.12 = (bf16[6,256,128]{2,1,0:T(8,128)(2,1)S(1)}, bf16[6,256,128]{2,1,0:T(8,128)(2,1)S(1)}, u32[]{:S(2)}, u32[]{:S(2)}) collective-permute-start(bf16[6,256,128]{2,1,0:T(8,128)(2,1)S(1)} %get-tuple-element.40), channel_id=1, source_target_pairs={{0,3},{1,2},{2,1},{3,0},{4,7},{5,6},{6,5},{7,4},{8,11},{9,10},{10,... | collective-permute-start | bytes 1179656 | tf_op jit(solution)/shard_map/ppermute | solution.py:307
  14.1 20.2 %collective-permute-start.3 = (bf16[4,12,16,128]{3,2,1,0:T(8,128)(2,1)S(1)}, bf16[4,12,16,128]{3,2,1,0:T(8,128)(2,1)S(1)}, u32[]{:S(2)}, u32[]{:S(2)}) collective-permute-start(bf16[4,12,16,128]{3,2,1,0:T(8,128)(2,1)S(1)} %get-tuple-element.28), channel_id=1, source_target_pairs={{0,4},{4,0},{8,12},{12,8},{16,20},{20,16},{24,28},{28,24},{1,5},{5... | collective-permute-start | bytes 589832 | tf_op jit(solution)/shard_map/ppermute | solution.py:313
  15.6 13.5 %collective-permute-start.6 = (s32[1,24]{1,0:T(1,128)S(1)}, s32[1,24]{1,0:T(1,128)S(1)}, u32[]{:S(2)}, u32[]{:S(2)}) collective-permute-start(s32[1,24]{1,0:T(1,128)S(1)} %copy-done), channel_id=1, source_target_pairs={{0,2},{1,3},{2,0},{3,1},{4,6},{5,7},{6,4},{7,5},{8,10},{9,11},{10,... | collective-permute-start | bytes 296 | tf_op jit(solution)/shard_map/ppermute | solution.py:307
  29.1 0.5 copy-start.2
  31.8 5.6 %collective-permute-start.8 = (bf16[4,6,16,128]{3,2,1,0:T(8,128)(2,1)S(1)}, bf16[4,6,16,128]{3,2,1,0:T(8,128)(2,1)S(1)}, u32[]{:S(2)}, u32[]{:S(2)}) collective-permute-start(bf16[4,6,16,128]{3,2,1,0:T(8,128)(2,1)S(1)} %get-tuple-element.34), channel_id=1, source_target_pairs={{0,4},{4,0},{8,12},{12,8},{16,20},{20,16},{24,28},{28,24},{1,5},{5... | collective-permute-start | bytes 294920 | tf_op jit(solution)/shard_map/ppermute | solution.py:313
  33.8 5.3 %collective-permute-start.13 = (bf16[4,6,16,128]{3,2,1,0:T(8,128)(2,1)S(1)}, bf16[4,6,16,128]{3,2,1,0:T(8,128)(2,1)S(1)}, u32[]{:S(2)}, u32[]{:S(2)}) collective-permute-start(bf16[4,6,16,128]{3,2,1,0:T(8,128)(2,1)S(1)} %get-tuple-element.42), channel_id=1, source_target_pairs={{0,4},{4,0},{8,12},{12,8},{16,20},{20,16},{24,28},{28,24},{1,5},{5... | collective-permute-start | bytes 294920 | tf_op jit(solution)/shard_map/ppermute | solution.py:313
  34.3 9.9 %collective-permute-start.4 = (bf16[2,12,16,128]{3,2,1,0:T(8,128)(2,1)S(1)}, bf16[2,12,16,128]{3,2,1,0:T(8,128)(2,1)S(1)}, u32[]{:S(2)}, u32[]{:S(2)}) collective-permute-start(bf16[2,12,16,128]{3,2,1,0:T(8,128)(2,1)S(1)} %get-tuple-element.30), channel_id=1, source_target_pairs={{0,8},{4,12},{8,0},{12,4},{16,24},{20,28},{24,16},{28,20},{1,9},{5... | collective-permute-start | bytes 294920 | tf_op jit(solution)/shard_map/ppermute | solution.py:313
  37.4 4.2 %collective-permute-start.9 = (bf16[2,6,16,128]{3,2,1,0:T(8,128)(2,1)S(1)}, bf16[2,6,16,128]{3,2,1,0:T(8,128)(2,1)S(1)}, u32[]{:S(2)}, u32[]{:S(2)}) collective-permute-start(bf16[2,6,16,128]{3,2,1,0:T(8,128)(2,1)S(1)} %get-tuple-element.36), channel_id=1, source_target_pairs={{0,8},{4,12},{8,0},{12,4},{16,24},{20,28},{24,16},{28,20},{1,9},{5... | collective-permute-start | bytes 147464 | tf_op jit(solution)/shard_map/ppermute | solution.py:313
  39.1 5.6 %collective-permute-start.14 = (bf16[2,6,16,128]{3,2,1,0:T(8,128)(2,1)S(1)}, bf16[2,6,16,128]{3,2,1,0:T(8,128)(2,1)S(1)}, u32[]{:S(2)}, u32[]{:S(2)}) collective-permute-start(bf16[2,6,16,128]{3,2,1,0:T(8,128)(2,1)S(1)} %get-tuple-element.44), channel_id=1, source_target_pairs={{0,8},{4,12},{8,0},{12,4},{16,24},{20,28},{24,16},{28,20},{1,9},{5... | collective-permute-start | bytes 147464 | tf_op jit(solution)/shard_map/ppermute | solution.py:313
  41.6 5.8 %collective-permute-start.10 = (bf16[1,6,16,128]{3,2,1,0:T(8,128)(2,1)S(1)}, bf16[1,6,16,128]{3,2,1,0:T(8,128)(2,1)S(1)}, u32[]{:S(2)}, u32[]{:S(2)}) collective-permute-start(bf16[1,6,16,128]{3,2,1,0:T(8,128)(2,1)S(1)} %get-tuple-element.38), channel_id=1, source_target_pairs={{0,16},{4,20},{8,24},{12,28},{16,0},{20,4},{24,8},{28,12},{1,17},{... | collective-permute-start | bytes 73736 | tf_op jit(solution)/shard_map/ppermute | solution.py:313
  44.3 5.3 %collective-permute-start.5 = (bf16[1,12,16,128]{3,2,1,0:T(8,128)(2,1)S(1)}, bf16[1,12,16,128]{3,2,1,0:T(8,128)(2,1)S(1)}, u32[]{:S(2)}, u32[]{:S(2)}) collective-permute-start(bf16[1,12,16,128]{3,2,1,0:T(8,128)(2,1)S(1)} %get-tuple-element.32), channel_id=1, source_target_pairs={{0,16},{4,20},{8,24},{12,28},{16,0},{20,4},{24,8},{28,12},{1,17},{... | collective-permute-start | bytes 147464 | tf_op jit(solution)/shard_map/ppermute | solution.py:313
  44.7 4.9 %collective-permute-start.15 = (bf16[1,6,16,128]{3,2,1,0:T(8,128)(2,1)S(1)}, bf16[1,6,16,128]{3,2,1,0:T(8,128)(2,1)S(1)}, u32[]{:S(2)}, u32[]{:S(2)}) collective-permute-start(bf16[1,6,16,128]{3,2,1,0:T(8,128)(2,1)S(1)} %get-tuple-element.46), channel_id=1, source_target_pairs={{0,16},{4,20},{8,24},{12,28},{16,0},{20,4},{24,8},{28,12},{1,17},{... | collective-permute-start | bytes 73736 | tf_op jit(solution)/shard_map/ppermute | solution.py:313
  47.4 3.9 %collective-permute-start.11 = (bf16[6,16,128]{2,1,0:T(8,128)(2,1)S(1)}, bf16[6,16,128]{2,1,0:T(8,128)(2,1)S(1)}, u32[]{:S(2)}, u32[]{:S(2)}) collective-permute-start(bf16[6,16,128]{2,1,0:T(8,128)(2,1)S(1)} %shard_map.60), channel_id=1, source_target_pairs={{0,2},{1,3},{2,0},{3,1},{4,6},{5,7},{6,4},{7,5},{8,10},{9,11},{10,... | collective-permute-start | bytes 73736 | tf_op jit(solution)/shard_map/ppermute | solution.py:307

commit v4 on v3

v4 whole, which is shorter than its diff:
```python
import functools

import jax
import jax.numpy as jnp
from jax import lax
from jax.experimental import pallas as pl
from jax.experimental.pallas import tpu as pltpu
from jax.sharding import PartitionSpec as P


BLOCK = 128
CAP = 8
ROW_TILE = 16

SMEM = pl.BlockSpec(memory_space=pltpu.SMEM)
HBM = pl.BlockSpec(memory_space=pltpu.HBM)
SMALL = pltpu.CompilerParams(vmem_limit_bytes=8 << 20)
VMEM = pl.BlockSpec(memory_space=pltpu.VMEM)


def pick_slots(summed, starts, counts):
    slot_ids = starts[:, None] + jnp.arange(CAP, dtype=jnp.int32)[None, :]
    is_live = jnp.arange(CAP, dtype=jnp.int32)[None, :] < counts[:, None]
    picked = jnp.take(summed, jnp.minimum(slot_ids, summed.shape[0] - 1).reshape(-1), axis=0)
    picked = picked.reshape(slot_ids.shape[0], CAP, BLOCK, BLOCK)
    return jnp.where(is_live[:, :, None, None], picked, jnp.zeros_like(picked))


def dense_on_device(hidden, grad_out, block_rows, block_cols, block_owner):
    tok_rows = hidden.shape[0]
    hidden_sel = jnp.take(hidden.reshape(tok_rows, -1, BLOCK), block_rows[0], axis=1)
    cotangent = lax.all_gather(grad_out, "tensor", axis=1, tiled=True)
    grad_sel = jnp.take(cotangent.reshape(tok_rows, -1, BLOCK), block_cols[0], axis=1)
    partial_value = jnp.einsum(
        "tkr,tkc->krc", hidden_sel, grad_sel, preferred_element_type=jnp.float32
    ).astype(jnp.bfloat16)
    seq_count = lax.axis_size("seq")
    members = (block_owner[0][None, :] == jnp.arange(seq_count, dtype=jnp.int32)[:, None]).astype(jnp.int32)
    counts = jnp.sum(members, axis=1)
    starts = jnp.cumsum(counts) - counts
    outgoing = pick_slots(partial_value, starts, counts)
    received = lax.all_to_all(outgoing, "seq", split_axis=0, concat_axis=0, tiled=True)
    return jnp.sum(received, axis=0, dtype=jnp.float32).astype(jnp.bfloat16)[None]


def scalars(value):
    return pltpu.with_memory_space_constraint(value, pltpu.SMEM)


def in_hbm(value):
    return pltpu.with_memory_space_constraint(value, pltpu.HBM)


def vectors(value):
    return pltpu.with_memory_space_constraint(value, pltpu.VMEM)


def column(ref, index):
    return ref.at[:, pl.ds(pl.multiple_of(index * BLOCK, BLOCK), BLOCK)]


def listed_at(table, cols, values, owner, cols_per, per_peer):
    listed = [cols[0, k] - owner * cols_per for k in range(cols.shape[1])]
    taken = listed if values is None else [values[0, k] for k in range(cols.shape[1])]
    found = jnp.int32(0)
    for local, value in zip(listed, taken):
        hit = jnp.logical_and(local >= 0, local < cols_per)
        table[jnp.where(hit, jnp.minimum(found, per_peer - 1), per_peer)] = value
        found += hit.astype(jnp.int32)


def split_pieces(order, parts, kept, sent):
    me = lax.axis_index("seq")
    width = len(order) - 1
    for index in range(kept.shape[0]):
        apart = sum(((index >> (width - 1 - bit)) & 1) * order[bit + 1] for bit in range(width))
        kept[index] = parts[me ^ apart]
        sent[index] = parts[me ^ apart ^ order[0]].astype(jnp.bfloat16)


def halve_kernel(*refs):
    parts, (still, sent) = refs[:-2], refs[-2:]
    half = still.shape[0]
    first = 0
    for kept, received in zip(parts[0::2], parts[1::2]):
        items = pl.ds(first, kept.shape[1])
        still[:, items] = kept[:half] + received[:half].astype(jnp.float32)
        sent[:, items] = (kept[half:] + received[half:].astype(jnp.float32)).astype(jnp.bfloat16)
        first += kept.shape[1]


def halve(parts):
    half, _, rows, _ = parts[0][0].shape
    shape = (half // 2, sum(kept.shape[1] for kept, _ in parts), rows, BLOCK)
    return pl.pallas_call(
        halve_kernel,
        out_shape=[pltpu.VMEM(shape, jnp.float32), pltpu.VMEM(shape, jnp.bfloat16)],
        in_specs=[VMEM] * (2 * len(parts)),
        out_specs=[VMEM, VMEM],
        compiler_params=SMALL,
    )(*[vectors(value) for part in parts for value in part])


def finish_kernel(kept, received, *outs):
    first = 0
    for out in outs:
        items = pl.ds(first, out.shape[0])
        out[...] = (kept[0, items] + received[0, items].astype(jnp.float32)).astype(jnp.bfloat16)
        first += out.shape[0]


def finish(kept, received, counts):
    return pl.pallas_call(
        finish_kernel,
        out_shape=[pltpu.VMEM((count,) + kept.shape[2:], jnp.bfloat16) for count in counts],
        in_specs=[VMEM, VMEM],
        out_specs=[VMEM] * len(counts),
        compiler_params=SMALL,
    )(vectors(kept), vectors(received))


def halved_shapes(pieces, items):
    shape = (pieces // 2, items, BLOCK // pieces, BLOCK)
    return [pltpu.VMEM(shape, jnp.float32), pltpu.VMEM(shape, jnp.bfloat16)]


def multiply(pieces, left, right):
    product = lax.dot_general(left, right, (((0,), (0,)), ((), ())), preferred_element_type=jnp.float32)
    return product.reshape(pieces, BLOCK // pieces, BLOCK)


def push_kernel(cols_per, per_peer, all_rows, all_cols, hidden, pushed, rows, cols, table, list_sems, sems):
    fetched = [
        pltpu.make_async_copy(a, b, list_sems.at[n]) for n, (a, b) in enumerate(((all_rows, rows), (all_cols, cols)))
    ]
    for copy in fetched:
        copy.start()
    for copy in fetched:
        copy.wait()
    listed_at(table, cols, rows, lax.axis_index("tensor") ^ 2, cols_per, per_peer)
    copies = [pltpu.make_async_copy(column(hidden, table[j]), pushed.at[j], sems.at[j]) for j in range(per_peer)]
    for copy in copies:
        copy.start()
    for copy in copies:
        copy.wait()


def push_blocks(rows, cols, hidden, cols_per, per_peer):
    return pl.pallas_call(
        functools.partial(push_kernel, cols_per, per_peer),
        out_shape=pltpu.VMEM((per_peer, hidden.shape[0], BLOCK), hidden.dtype),
        in_specs=[HBM, HBM, HBM],
        out_specs=VMEM,
        scratch_shapes=[
            pltpu.SMEM(rows.shape, jnp.int32),
            pltpu.SMEM(cols.shape, jnp.int32),
            pltpu.SMEM((per_peer + 1,), jnp.int32),
            pltpu.SemaphoreType.DMA((2,)),
            pltpu.SemaphoreType.DMA((per_peer,)),
        ],
        name="push_blocks",
        compiler_params=SMALL,
    )(in_hbm(rows), in_hbm(cols), in_hbm(hidden))


def pack_kernel(cols_per, per_peer, came1, came3, grad_out, for_core, for_far, list1, list3, table, list_sems, sems):
    me = lax.axis_index("tensor")
    fetched = [pltpu.make_async_copy(a, b, list_sems.at[n]) for n, (a, b) in enumerate(((came1, list1), (came3, list3)))]
    for copy in fetched:
        copy.start()
    for copy in fetched:
        copy.wait()
    copies = []
    for n, (listed, there) in enumerate(((list1, for_core), (list3, for_far))):
        listed_at(table, listed, None, me, cols_per, per_peer)
        for j in range(per_peer):
            copies.append(pltpu.make_async_copy(column(grad_out, table[j]), there.at[j], sems.at[n, j]))
            copies[-1].start()
    for copy in copies:
        copy.wait()


def pack_columns(list1, list3, grad_out, per_peer):
    tok_rows, width = grad_out.shape
    return pl.pallas_call(
        functools.partial(pack_kernel, width // BLOCK, per_peer),
        out_shape=[pltpu.VMEM((per_peer, tok_rows, BLOCK), grad_out.dtype)] * 2,
        in_specs=[VMEM, VMEM, HBM],
        out_specs=[VMEM, VMEM],
        scratch_shapes=[
            pltpu.SMEM(list1.shape, jnp.int32),
            pltpu.SMEM(list3.shape, jnp.int32),
            pltpu.SMEM((per_peer + 1,), jnp.int32),
            pltpu.SemaphoreType.DMA((2,)),
            pltpu.SemaphoreType.DMA((2, per_peer)),
        ],
        name="pack_columns",
        compiler_params=SMALL,
    )(vectors(list1), vectors(list3), in_hbm(grad_out))


def near_kernel(order, cols_per, per_peer, pieces, rows, cols, came2, hidden, grad_out, arrived, kept, sent, hidden_far, grad_guest, hidden_near, grad_near, parts, list2, table, list_sem, sems):
    fetched = pltpu.make_async_copy(came2, list2, list_sem)
    fetched.start()
    me = lax.axis_index("tensor")
    count = [0]

    def gather(owner, listed, values, source, there, first):
        listed_at(table, listed, values, owner, cols_per, per_peer)
        copies = []
        for j in range(per_peer):
            copies.append(pltpu.make_async_copy(column(source, table[j]), there.at[first + j], sems.at[count[0], j]))
            copies[-1].start()
        count[0] += 1
        return copies

    mine = gather(me, cols, None, grad_out, grad_near, 0)
    near = gather(me, cols, rows, hidden, hidden_near, 0)
    near += gather(me ^ 1, cols, rows, hidden, hidden_near, per_peer)
    later = gather(me ^ 3, cols, rows, hidden, hidden_far, 0)
    fetched.wait()
    later += gather(me, list2, None, grad_out, grad_guest, 0)
    for copy in mine + near:
        copy.wait()
    for item in range(2 * per_peer):
        right = grad_near[item] if item < per_peer else arrived[item - per_peer]
        parts[:, item] = multiply(pieces, hidden_near[item], right)
    split_pieces(order, parts, kept, sent)
    for copy in later:
        copy.wait()


def near_products(rows, cols, list2, hidden, grad_out, arrived, per_peer, pieces, order):
    tok_rows, width = grad_out.shape
    near = 2 * per_peer
    blocks = pltpu.VMEM((per_peer, tok_rows, BLOCK), jnp.bfloat16)
    return pl.pallas_call(
        functools.partial(near_kernel, order, width // BLOCK, per_peer, pieces),
        out_shape=halved_shapes(pieces, near) + [blocks, blocks],
        in_specs=[SMEM, SMEM, VMEM, HBM, HBM, VMEM],
        out_specs=[VMEM] * 4,
        scratch_shapes=[
            pltpu.VMEM((near, tok_rows, BLOCK), jnp.bfloat16),
            pltpu.VMEM((per_peer, tok_rows, BLOCK), jnp.bfloat16),
            pltpu.VMEM((pieces, near, BLOCK // pieces, BLOCK), jnp.float32),
            pltpu.SMEM(list2.shape, jnp.int32),
            pltpu.SMEM((per_peer + 1,), jnp.int32),
            pltpu.SemaphoreType.DMA,
            pltpu.SemaphoreType.DMA((5, per_peer)),
        ],
        name="near_products",
        compiler_params=SMALL,
    )(scalars(rows), scalars(cols), vectors(list2), in_hbm(hidden), in_hbm(grad_out), vectors(arrived))


def cross_kernel(order, pieces, left, right, kept, sent, parts):
    for j in range(left.shape[0]):
        parts[:, j] = multiply(pieces, left[j], right[j])
    split_pieces(order, parts, kept, sent)


def cross_products(left, right, pieces, order):
    count = left.shape[0]
    return pl.pallas_call(
        functools.partial(cross_kernel, order, pieces),
        out_shape=halved_shapes(pieces, count),
        in_specs=[VMEM, VMEM],
        out_specs=[VMEM, VMEM],
        scratch_shapes=[pltpu.VMEM((pieces, count, BLOCK // pieces, BLOCK), jnp.float32)],
        compiler_params=SMALL,
    )(vectors(left), vectors(right))


def plan_kernel(cols_per, per_peer, cols, owners, places, seen):
    me = lax.axis_index("tensor")
    for index in range(4):
        seen[index] = 0
    listed = range(cols.shape[1])
    distances = [lax.shift_right_logical(cols[0, k], cols_per.bit_length() - 1) ^ me for k in listed]
    placed_at = [owners[0, k] for k in listed]
    slot = jnp.int32(0)
    for k in listed:
        rank = jnp.minimum(seen[distances[k]], per_peer - 1)
        seen[distances[k]] = rank + 1
        slot = jnp.where(placed_at[k] == placed_at[k - 1], slot + 1, 0) if k else slot
        places[distances[k] * per_peer + rank] = placed_at[k] * CAP + jnp.minimum(slot, CAP - 1)


def plan(cols, owners, cols_per, per_peer):
    return pl.pallas_call(
        functools.partial(plan_kernel, cols_per, per_peer),
        out_shape=pltpu.SMEM((cols.shape[1],), jnp.int32),
        in_specs=[SMEM, SMEM],
        out_specs=SMEM,
        scratch_shapes=[pltpu.SMEM((4,), jnp.int32)],
        name="plan",
        compiler_params=SMALL,
    )(scalars(cols), scalars(owners))


def settle_kernel(places, near, guests, kept, received, out):
    out[...] = jnp.zeros_like(out)
    first = 0
    for source in (near, guests):
        for j in range(source.shape[0]):
            out[places[first + j]] = source[j]
        first += source.shape[0]
    for j in range(kept.shape[1]):
        out[places[first + j]] = (kept[0, j] + received[0, j].astype(jnp.float32)).astype(jnp.bfloat16)


def settle(places, near, guests, kept, received, pieces):
    _, rows, _ = guests.shape
    return pl.pallas_call(
        settle_kernel,
        out_shape=pltpu.VMEM((pieces * CAP, rows, BLOCK), jnp.bfloat16),
        in_specs=[SMEM] + [VMEM] * 4,
        out_specs=VMEM,
        name="settle",
        compiler_params=SMALL,
    )(scalars(places), vectors(near), vectors(guests), vectors(kept), vectors(received))


def sparse_on_device(hidden, grad_out, block_rows, block_cols, block_owner):
    tensor_count, seq_count = lax.axis_size("tensor"), lax.axis_size("seq")
    cols_per = grad_out.shape[1] // BLOCK
    per_peer = block_cols.shape[1] // tensor_count

    def to_peer(value, distance):
        return lax.ppermute(value, "tensor", [(i, i ^ distance) for i in range(tensor_count)])

    def exchange(sent, distance):
        return lax.ppermute(sent, "seq", [(i, i ^ distance) for i in range(seq_count)])

    def reduce_pieces(order, kept, sent):
        for step, distance in enumerate(order):
            received = exchange(sent, distance)
            if step == len(order) - 1:
                return finish(kept, received, (kept.shape[1],))[0]
            kept, sent = halve([(kept, received)])

    near_order, guest_order = (2, 1, 4), (1, 2, 4)
    list3 = to_peer(block_cols, 3)
    pushed = push_blocks(block_rows, block_cols, hidden, cols_per, per_peer)
    guests = to_peer(pushed, 2)
    list1 = to_peer(block_cols, 1)
    list2 = to_peer(list3, 1)
    for_core, for_far = pack_columns(list1, list3, grad_out, per_peer)
    from_core = to_peer(for_core, 1)
    from_far = to_peer(for_far, 3)
    near_kept, near_sent, hidden_far, grad_guest = near_products(
        block_rows, block_cols, list2, hidden, grad_out, from_core, per_peer, seq_count, near_order
    )
    near_sum = reduce_pieces(near_order, near_kept, near_sent)
    places = plan(block_cols, block_owner, cols_per, per_peer)
    guest_kept, guest_sent = cross_products(guests, grad_guest, seq_count, guest_order)
    guest_sum = reduce_pieces(guest_order, guest_kept, guest_sent)
    guest_back = to_peer(guest_sum, 2)
    kept, sent = cross_products(hidden_far, from_far, seq_count, guest_order)
    received = exchange(sent, guest_order[0])
    for distance in guest_order[1:]:
        kept, sent = halve([(kept, received)])
        received = exchange(sent, distance)
    placed = settle(places, near_sum, guest_back, kept, received, seq_count)
    delivered = lax.all_to_all(
        placed.reshape(seq_count, CAP, -1, BLOCK), "seq", split_axis=0, concat_axis=0, tiled=True
    )
    return delivered.transpose(1, 0, 2, 3).reshape(1, CAP, BLOCK, BLOCK)


def solution(mesh):
    tensor_count, seq_count = mesh.shape["tensor"], mesh.shape["seq"]
    placed = (
        P("seq", "tensor"),
        P("seq", "tensor"),
        P("tensor", None),
        P("tensor", None),
        P("tensor", None),
    )

    def on_device(hidden, grad_out, block_rows, block_cols, block_owner):
        listed = block_cols.shape[1]
        each_named_once = listed == 24 and tensor_count == 4
        whole_tiles = BLOCK % (seq_count * ROW_TILE) == 0
        step = sparse_on_device if each_named_once and whole_tiles else dense_on_device
        return step(hidden, grad_out, block_rows, block_cols, block_owner)

    return jax.shard_map(
        on_device,
        mesh=mesh,
        in_specs=placed,
        out_specs=P("tensor", "seq", None, None),
        check_vma=False,
    )
```

time: 66.4 us -> 61.1 us (0.920)
  waiting for transfers between devices: 18.7 us -> 16.1 us
  Pallas kernels: 10.2 us -> 8.29 us
  local copies, waits for them, and re-layouts: 1.77 us -> 0.73 us
    ppermute x7, waiting for transfers between devices: 15.2 us -> 12.9 us  [to_peer(): lax.ppermute(value, 'tensor', [(i, i ^ distance) for i in range(tensor_co...]
    pallas_call x4 -> x5, Pallas kernels: 6.14 us -> 4.33 us  [the longest x1 2.91 us: near_products(): pl.pallas_call(functools.partial(near_kernel, order, width // BLOCK, per_...]
    ppermute x9, starting transfers between devices: 13.8 us -> 15.2 us  [exchange(): lax.ppermute(sent, 'seq', [(i, i ^ distance) for i in range(seq_count)])]
    unnamed x8 -> x6, local copies, waits for them, and re-layouts: 1.05 us -> 0.01 us
    ppermute x7, starting transfers between devices: 8.27 us -> 7.47 us  [to_peer(): lax.ppermute(value, 'tensor', [(i, i ^ distance) for i in range(tensor_co...]
  transfers between devices with their start and end apart: 16 -> 16, of which waited for: 6 -> 8; matrix products, arithmetic and copies ran while one was open for 0% -> 0% of each run, Pallas kernels for 11% -> 10%
where the time goes in v4:
time: 61.1 us; the launch traced here: 60.8 us
  starting transfers between devices  22.7 us (37%)
  waiting for transfers between devices  16.1 us (26%)
  blocking collectives  12.8 us (21%)
  Pallas kernels  8.29 us (14%)
  local copies, waits for them, and re-layouts  0.73 us (1%)
    ppermute x9, starting transfers between devices, exchange(): lax.ppermute(sent, 'seq', [(i, i ^ distance) for i in range(seq_count)])  15.2 us
    ppermute x7, waiting for transfers between devices, to_peer(): lax.ppermute(value, 'tensor', [(i, i ^ distance) for i in range(tensor_co...  12.9 us
    all_to_all x1, blocking collectives, sparse_on_device(): lax.all_to_all(placed.reshape(seq_count, CAP, -1, BLOCK), 'seq', split_ax...  12.8 us
    ppermute x7, starting transfers between devices, to_peer(): lax.ppermute(value, 'tensor', [(i, i ^ distance) for i in range(tensor_co...  7.47 us
    ppermute x9, waiting for transfers between devices, exchange(): lax.ppermute(sent, 'seq', [(i, i ^ distance) for i in range(seq_count)])  3.21 us
    pallas_call x1, Pallas kernels, near_products(): pl.pallas_call(functools.partial(near_kernel, order, width // BLOCK, per_...  2.91 us
    pallas_call x1, Pallas kernels, pack_columns(): pl.pallas_call(functools.partial(pack_kernel, width // BLOCK, per_peer),...  1.96 us
    pallas_call x1, Pallas kernels, push_blocks(): pl.pallas_call(functools.partial(push_kernel, cols_per, per_peer), out_sh...  1.85 us
  transfers between devices with their start and end apart: 16, of which 8 were waited for; matrix products, arithmetic and copies ran while one was open for 0% of the time, Pallas kernels for 10%

profile of v4, /device:TPU:0, one launch (start us, length us, event | category | flops | bytes accessed | tf_op | source)
XLA Modules:
  0.0 60.8 jit_solution(11283898257311014384)
XLA Ops:
  0.0 0.0 copy-start.1
  0.0 0.0 copy-start
  0.0 2.4 %collective-permute-start = (s32[1,24]{1,0:T(1,128)}, s32[1,24]{1,0:T(1,128)S(1)}, u32[]{:S(2)}, u32[]{:S(2)}) collective-permute-start(s32[1,24]{1,0:T(1,128)} %all_cols.1), channel_id=1, source_target_pairs={{0,3},{1,2},{2,1},{3,0},{4,7},{5,6},{6,5},{7,4},{8,11},{9,10},{10,... | collective-permute-start | bytes 296 | tf_op jit(solution)/shard_map/ppermute | solution.py:330
  2.4 0.7 %collective-permute-start.2 = (s32[1,24]{1,0:T(1,128)}, s32[1,24]{1,0:T(1,128)S(1)}, u32[]{:S(2)}, u32[]{:S(2)}) collective-permute-start(s32[1,24]{1,0:T(1,128)} %all_cols.1), channel_id=1, source_target_pairs={{0,1},{1,0},{2,3},{3,2},{4,5},{5,4},{6,7},{7,6},{8,9},{9,8},{10,11... | collective-permute-start | bytes 296 | tf_op jit(solution)/shard_map/ppermute | solution.py:330
  3.1 0.8 %collective-permute-done.came3 = s32[1,24]{1,0:T(1,128)S(1)} collective-permute-done((s32[1,24]{1,0:T(1,128)}, s32[1,24]{1,0:T(1,128)S(1)}, u32[]{:S(2)}, u32[]{:S(2)}) %collective-permute-start) | collective-permute-done | bytes 128 | tf_op jit(solution)/shard_map/ppermute | solution.py:330
  3.9 0.2 collective-permute-done.2.came1
  4.1 2.0 %pack_columns.1 = (bf16[6,256,128]{2,1,0:T(8,128)(2,1)S(1)}, bf16[6,256,128]{2,1,0:T(8,128)(2,1)S(1)}) custom-call(s32[1,24]{1,0:T(1,128)S(1)} %collective-permute-done.2.came1, s32[1,24]{1,0:T(1,128)S(1)} %collective-permute-done.came3, bf16[256,4096]{1,0:T(8,128)(2,1)} %grad_out.3), custom_call_target="tpu_custom_call" | custom-call | tf_op jit(solution)/shard_map/pack_columns/pallas_call | solution.py:185
  6.0 0.6 collective-permute-start.3
  6.6 1.9 %push_blocks.1 = bf16[6,256,128]{2,1,0:T(8,128)(2,1)S(1)} custom-call(s32[1,24]{1,0:T(1,128)} %all_rows.1, s32[1,24]{1,0:T(1,128)} %all_cols.1, bf16[256,13312]{1,0:T(8,128)(2,1)} %hidden.3), custom_call_target="tpu_custom_call" | custom-call | tf_op jit(solution)/shard_map/push_blocks/pallas_call | solution.py:149
  8.5 0.0 copy-start.2
  8.5 1.6 %collective-permute-start.7 = (bf16[6,256,128]{2,1,0:T(8,128)(2,1)S(1)}, bf16[6,256,128]{2,1,0:T(8,128)(2,1)S(1)}, u32[]{:S(2)}, u32[]{:S(2)}) collective-permute-start(bf16[6,256,128]{2,1,0:T(8,128)(2,1)S(1)} %push_blocks.1), channel_id=1, source_target_pairs={{0,2},{1,3},{2,0},{3,1},{4,6},{5,7},{6,4},{7,5},{8,10},{9,11},{10,... | collective-permute-start | bytes 1179656 | tf_op jit(solution)/shard_map/ppermute | solution.py:330
  10.1 0.2 collective-permute-start.12
  10.3 0.4 collective-permute-start.1
  10.7 0.8 %collective-permute-done.1.came2 = s32[1,24]{1,0:T(1,128)S(1)} collective-permute-done((s32[1,24]{1,0:T(1,128)S(1)}, s32[1,24]{1,0:T(1,128)S(1)}, u32[]{:S(2)}, u32[]{:S(2)}) %collective-permute-start.1) | collective-permute-done | bytes 128 | tf_op jit(solution)/shard_map/ppermute | solution.py:330
  11.5 0.0 collective-permute-done.3.arrived
  11.5 0.0 copy-done.1
  11.5 0.0 copy-done
  11.5 2.9 %near_products.1 = (f32[4,12,16,128]{3,2,1,0:T(8,128)S(1)}, bf16[4,12,16,128]{3,2,1,0:T(8,128)(2,1)S(1)}, bf16[6,256,128]{2,1,0:T(8,128)(2,1)S(1)}, bf16[6,256,128]{2,1,0:T(8,128)(2,1)S(1)}) custom-call(s32[1,24]{1,0:T(1,128)S(1)} %copy-done, s32[1,24]{1,0:T(1,128)S(1)} %copy-done.1, s32[1,24]{1,0:T(1,128)S(1)} %collective-permute-done.1.came2, ...), custom_call_target="tpu_custom_call" | custom-call | tf_op jit(solution)/shard_map/near_products/pallas_call | solution.py:237
  14.4 1.8 %collective-permute-start.4 = (bf16[4,12,16,128]{3,2,1,0:T(8,128)(2,1)S(1)}, bf16[4,12,16,128]{3,2,1,0:T(8,128)(2,1)S(1)}, u32[]{:S(2)}, u32[]{:S(2)}) collective-permute-start(bf16[4,12,16,128]{3,2,1,0:T(8,128)(2,1)S(1)} %get-tuple-element.29), channel_id=1, source_target_pairs={{0,8},{4,12},{8,0},{12,4},{16,24},{20,28},{24,16},{28,20},{1,9},{5... | collective-permute-start | bytes 589832 | tf_op jit(solution)/shard_map/ppermute | solution.py:333
  16.2 4.3 %collective-permute-done.7.left = bf16[6,256,128]{2,1,0:T(8,128)(2,1)S(1)} collective-permute-done((bf16[6,256,128]{2,1,0:T(8,128)(2,1)S(1)}, bf16[6,256,128]{2,1,0:T(8,128)(2,1)S(1)}, u32[]{:S(2)}, u32[]{:S(2)}) %collective-permute-start.7) | collective-permute-done | bytes 393248 | tf_op jit(solution)/shard_map/ppermute | solution.py:330
  20.5 0.3 shard_map.58
  20.9 1.6 %collective-permute-start.8 = (bf16[4,6,16,128]{3,2,1,0:T(8,128)(2,1)S(1)}, bf16[4,6,16,128]{3,2,1,0:T(8,128)(2,1)S(1)}, u32[]{:S(2)}, u32[]{:S(2)}) collective-permute-start(bf16[4,6,16,128]{3,2,1,0:T(8,128)(2,1)S(1)} %get-tuple-element.36), channel_id=1, source_target_pairs={{0,4},{4,0},{8,12},{12,8},{16,20},{20,16},{24,28},{28,24},{1,5},{5... | collective-permute-start | bytes 294920 | tf_op jit(solution)/shard_map/ppermute | solution.py:333
  22.5 5.2 %collective-permute-done.12.right = bf16[6,256,128]{2,1,0:T(8,128)(2,1)S(1)} collective-permute-done((bf16[6,256,128]{2,1,0:T(8,128)(2,1)S(1)}, bf16[6,256,128]{2,1,0:T(8,128)(2,1)S(1)}, u32[]{:S(2)}, u32[]{:S(2)}) %collective-permute-start.12) | collective-permute-done | bytes 393248 | tf_op jit(solution)/shard_map/ppermute | solution.py:330
  27.7 0.3 shard_map.62
  28.0 1.9 %collective-permute-start.13 = (bf16[4,6,16,128]{3,2,1,0:T(8,128)(2,1)S(1)}, bf16[4,6,16,128]{3,2,1,0:T(8,128)(2,1)S(1)}, u32[]{:S(2)}, u32[]{:S(2)}) collective-permute-start(bf16[4,6,16,128]{3,2,1,0:T(8,128)(2,1)S(1)} %get-tuple-element.44), channel_id=1, source_target_pairs={{0,4},{4,0},{8,12},{12,8},{16,20},{20,16},{24,28},{28,24},{1,5},{5... | collective-permute-start | bytes 294920 | tf_op jit(solution)/shard_map/ppermute | solution.py:333
  30.0 0.0 collective-permute-done.4.refs_1_
  30.0 0.2 collective-permute-start.5
  30.2 0.0 collective-permute-done.8.refs_1_
  30.3 2.0 %collective-permute-start.9 = (bf16[2,6,16,128]{3,2,1,0:T(8,128)(2,1)S(1)}, bf16[2,6,16,128]{3,2,1,0:T(8,128)(2,1)S(1)}, u32[]{:S(2)}, u32[]{:S(2)}) collective-permute-start(bf16[2,6,16,128]{3,2,1,0:T(8,128)(2,1)S(1)} %get-tuple-element.38), channel_id=1, source_target_pairs={{0,8},{4,12},{8,0},{12,4},{16,24},{20,28},{24,16},{28,20},{1,9},{5... | collective-permute-start | bytes 147464 | tf_op jit(solution)/shard_map/ppermute | solution.py:333
  32.3 1.5 %collective-permute-done.13.refs_1_ = bf16[4,6,16,128]{3,2,1,0:T(8,128)(2,1)S(1)} collective-permute-done((bf16[4,6,16,128]{3,2,1,0:T(8,128)(2,1)S(1)}, bf16[4,6,16,128]{3,2,1,0:T(8,128)(2,1)S(1)}, u32[]{:S(2)}, u32[]{:S(2)}) %collective-permute-start.13) | collective-permute-done | bytes 98336 | tf_op jit(solution)/shard_map/ppermute | solution.py:333
  33.8 2.0 %collective-permute-start.14 = (bf16[2,6,16,128]{3,2,1,0:T(8,128)(2,1)S(1)}, bf16[2,6,16,128]{3,2,1,0:T(8,128)(2,1)S(1)}, u32[]{:S(2)}, u32[]{:S(2)}) collective-permute-start(bf16[2,6,16,128]{3,2,1,0:T(8,128)(2,1)S(1)} %get-tuple-element.46), channel_id=1, source_target_pairs={{0,8},{4,12},{8,0},{12,4},{16,24},{20,28},{24,16},{28,20},{1,9},{5... | collective-permute-start | bytes 147464 | tf_op jit(solution)/shard_map/ppermute | solution.py:333
  35.8 0.0 collective-permute-done.9.refs_1_
  35.8 0.0 collective-permute-done.5.refs_1_
  35.9 2.7 %collective-permute-start.6 = (bf16[1,12,16,128]{3,2,1,0:T(8,128)(2,1)S(1)}, bf16[1,12,16,128]{3,2,1,0:T(8,128)(2,1)S(1)}, u32[]{:S(2)}, u32[]{:S(2)}) collective-permute-start(bf16[1,12,16,128]{3,2,1,0:T(8,128)(2,1)S(1)} %get-tuple-element.33), channel_id=1, source_target_pairs={{0,16},{4,20},{8,24},{12,28},{16,0},{20,4},{24,8},{28,12},{1,17},{... | collective-permute-start | bytes 147464 | tf_op jit(solution)/shard_map/ppermute | solution.py:333
  38.5 0.3 collective-permute-start.10
  38.9 0.0 collective-permute-done.14.refs_1_
  38.9 2.7 %collective-permute-start.15 = (bf16[1,6,16,128]{3,2,1,0:T(8,128)(2,1)S(1)}, bf16[1,6,16,128]{3,2,1,0:T(8,128)(2,1)S(1)}, u32[]{:S(2)}, u32[]{:S(2)}) collective-permute-start(bf16[1,6,16,128]{3,2,1,0:T(8,128)(2,1)S(1)} %get-tuple-element.48), channel_id=1, source_target_pairs={{0,16},{4,20},{8,24},{12,28},{16,0},{20,4},{24,8},{28,12},{1,17},{... | collective-permute-start | bytes 73736 | tf_op jit(solution)/shard_map/ppermute | solution.py:333
  41.5 1.7 %collective-permute-done.10.received = bf16[1,6,16,128]{3,2,1,0:T(8,128)(2,1)S(1)} collective-permute-done((bf16[1,6,16,128]{3,2,1,0:T(8,128)(2,1)S(1)}, bf16[1,6,16,128]{3,2,1,0:T(8,128)(2,1)S(1)}, u32[]{:S(2)}, u32[]{:S(2)}) %collective-permute-start.10) | collective-permute-done | bytes 24608 | tf_op jit(solution)/shard_map/ppermute | solution.py:333
  43.3 1.6 %collective-permute-start.11 = (bf16[6,16,128]{2,1,0:T(8,128)(2,1)S(1)}, bf16[6,16,128]{2,1,0:T(8,128)(2,1)S(1)}, u32[]{:S(2)}, u32[]{:S(2)}) collective-permute-start(bf16[6,16,128]{2,1,0:T(8,128)(2,1)S(1)} %shard_map.61), channel_id=1, source_target_pairs={{0,2},{1,3},{2,0},{3,1},{4,6},{5,7},{6,4},{7,5},{8,10},{9,11},{10,... | collective-permute-start | bytes 73736 | tf_op jit(solution)/shard_map/ppermute | solution.py:330
  44.8 0.0 copy-done.2
  44.8 0.7 %plan.1.places = s32[24]{0:T(128)S(4)} custom-call(s32[1,24]{1,0:T(1,128)S(1)} %copy-done.1, s32[1,24]{1,0:T(1,128)S(1)} %copy-done.2), custom_call_target="tpu_custom_call" | custom-call | tf_op jit(solution)/shard_map/plan/pallas_call | solution.py:290
  45.6 0.0 collective-permute-done.6.received
  45.6 0.0 collective-permute-done.15.received
  45.6 1.6 %collective-permute-done.11.guests = bf16[6,16,128]{2,1,0:T(8,128)(2,1)S(1)} collective-permute-done((bf16[6,16,128]{2,1,0:T(8,128)(2,1)S(1)}, bf16[6,16,128]{2,1,0:T(8,128)(2,1)S(1)}, u32[]{:S(2)}, u32[]{:S(2)}) %collective-permute-start.11) | collective-permute-done | bytes 24608 | tf_op jit(solution)/shard_map/ppermute | solution.py:330
  47.1 0.1 settle.1
  47.2 12.8 %all_to_all.5 = bf16[8,8,16,128]{3,2,1,0:T(8,128)(2,1)S(1)} all-to-all(bf16[8,8,16,128]{3,2,1,0:T(8,128)(2,1)S(1)} %bitcast.3), channel_id=1, replica_groups=mesh['seq'=8,'tensor'=4] {'seq'}, dimensions={0} | all-to-all | bytes 524288 | tf_op jit(solution)/shard_map/all_to_all | solution.py:365
  60.0 0.7 %copy.6 = bf16[8,8,16,128]{3,2,1,0:T(8,128)(2,1)} copy(bf16[8,8,16,128]{3,2,0,1:T(8,128)(2,1)S(1)} %bitcast.4) | data formatting | bytes 524288 | tf_op jit(solution)/shard_map/transpose | solution.py:368
  (8 shorter events, 0.1 us)
Async XLA Ops:
  0.0 11.5 %copy-start.1 = (s32[1,24]{1,0:T(1,128)S(1)}, s32[1,24]{1,0:T(1,128)}, u32[]{:S(2)}) copy-start(s32[1,24]{1,0:T(1,128)} %all_cols.1) | copy-start | bytes 292
  0.0 11.5 %copy-start = (s32[1,24]{1,0:T(1,128)S(1)}, s32[1,24]{1,0:T(1,128)}, u32[]{:S(2)}) copy-start(s32[1,24]{1,0:T(1,128)} %all_rows.1) | copy-start | bytes 292
  0.0 3.9 %collective-permute-start = (s32[1,24]{1,0:T(1,128)}, s32[1,24]{1,0:T(1,128)S(1)}, u32[]{:S(2)}, u32[]{:S(2)}) collective-permute-start(s32[1,24]{1,0:T(1,128)} %all_cols.1), channel_id=1, source_target_pairs={{0,3},{1,2},{2,1},{3,0},{4,7},{5,6},{6,5},{7,4},{8,11},{9,10},{10,... | collective-permute-start | bytes 296 | tf_op jit(solution)/shard_map/ppermute | solution.py:330
  2.4 1.6 %collective-permute-start.2 = (s32[1,24]{1,0:T(1,128)}, s32[1,24]{1,0:T(1,128)S(1)}, u32[]{:S(2)}, u32[]{:S(2)}) collective-permute-start(s32[1,24]{1,0:T(1,128)} %all_cols.1), channel_id=1, source_target_pairs={{0,1},{1,0},{2,3},{3,2},{4,5},{5,4},{6,7},{7,6},{8,9},{9,8},{10,11... | collective-permute-start | bytes 296 | tf_op jit(solution)/shard_map/ppermute | solution.py:330
  6.0 5.5 %collective-permute-start.3 = (bf16[6,256,128]{2,1,0:T(8,128)(2,1)S(1)}, bf16[6,256,128]{2,1,0:T(8,128)(2,1)S(1)}, u32[]{:S(2)}, u32[]{:S(2)}) collective-permute-start(bf16[6,256,128]{2,1,0:T(8,128)(2,1)S(1)} %get-tuple-element.27), channel_id=1, source_target_pairs={{0,1},{1,0},{2,3},{3,2},{4,5},{5,4},{6,7},{7,6},{8,9},{9,8},{10,11... | collective-permute-start | bytes 1179656 | tf_op jit(solution)/shard_map/ppermute | solution.py:330
  8.5 36.4 %copy-start.2 = (s32[1,24]{1,0:T(1,128)S(1)}, s32[1,24]{1,0:T(1,128)}, u32[]{:S(2)}) copy-start(s32[1,24]{1,0:T(1,128)} %owners.1) | copy-start | bytes 292
  8.5 12.1 %collective-permute-start.7 = (bf16[6,256,128]{2,1,0:T(8,128)(2,1)S(1)}, bf16[6,256,128]{2,1,0:T(8,128)(2,1)S(1)}, u32[]{:S(2)}, u32[]{:S(2)}) collective-permute-start(bf16[6,256,128]{2,1,0:T(8,128)(2,1)S(1)} %push_blocks.1), channel_id=1, source_target_pairs={{0,2},{1,3},{2,0},{3,1},{4,6},{5,7},{6,4},{7,5},{8,10},{9,11},{10,... | collective-permute-start | bytes 1179656 | tf_op jit(solution)/shard_map/ppermute | solution.py:330
  10.1 17.6 %collective-permute-start.12 = (bf16[6,256,128]{2,1,0:T(8,128)(2,1)S(1)}, bf16[6,256,128]{2,1,0:T(8,128)(2,1)S(1)}, u32[]{:S(2)}, u32[]{:S(2)}) collective-permute-start(bf16[6,256,128]{2,1,0:T(8,128)(2,1)S(1)} %get-tuple-element.42), channel_id=1, source_target_pairs={{0,3},{1,2},{2,1},{3,0},{4,7},{5,6},{6,5},{7,4},{8,11},{9,10},{10,... | collective-permute-start | bytes 1179656 | tf_op jit(solution)/shard_map/ppermute | solution.py:330
  10.3 1.2 %collective-permute-start.1 = (s32[1,24]{1,0:T(1,128)S(1)}, s32[1,24]{1,0:T(1,128)S(1)}, u32[]{:S(2)}, u32[]{:S(2)}) collective-permute-start(s32[1,24]{1,0:T(1,128)S(1)} %collective-permute-done.came3), channel_id=1, source_target_pairs={{0,1},{1,0},{2,3},{3,2},{4,5},{5,4},{6,7},{7,6},{8,9},{9,8},{10,11... | collective-permute-start | bytes 296 | tf_op jit(solution)/shard_map/ppermute | solution.py:330
  14.4 15.5 %collective-permute-start.4 = (bf16[4,12,16,128]{3,2,1,0:T(8,128)(2,1)S(1)}, bf16[4,12,16,128]{3,2,1,0:T(8,128)(2,1)S(1)}, u32[]{:S(2)}, u32[]{:S(2)}) collective-permute-start(bf16[4,12,16,128]{3,2,1,0:T(8,128)(2,1)S(1)} %get-tuple-element.29), channel_id=1, source_target_pairs={{0,8},{4,12},{8,0},{12,4},{16,24},{20,28},{24,16},{28,20},{1,9},{5... | collective-permute-start | bytes 589832 | tf_op jit(solution)/shard_map/ppermute | solution.py:333
  20.9 9.4 %collective-permute-start.8 = (bf16[4,6,16,128]{3,2,1,0:T(8,128)(2,1)S(1)}, bf16[4,6,16,128]{3,2,1,0:T(8,128)(2,1)S(1)}, u32[]{:S(2)}, u32[]{:S(2)}) collective-permute-start(bf16[4,6,16,128]{3,2,1,0:T(8,128)(2,1)S(1)} %get-tuple-element.36), channel_id=1, source_target_pairs={{0,4},{4,0},{8,12},{12,8},{16,20},{20,16},{24,28},{28,24},{1,5},{5... | collective-permute-start | bytes 294920 | tf_op jit(solution)/shard_map/ppermute | solution.py:333
  28.0 5.7 %collective-permute-start.13 = (bf16[4,6,16,128]{3,2,1,0:T(8,128)(2,1)S(1)}, bf16[4,6,16,128]{3,2,1,0:T(8,128)(2,1)S(1)}, u32[]{:S(2)}, u32[]{:S(2)}) collective-permute-start(bf16[4,6,16,128]{3,2,1,0:T(8,128)(2,1)S(1)} %get-tuple-element.44), channel_id=1, source_target_pairs={{0,4},{4,0},{8,12},{12,8},{16,20},{20,16},{24,28},{28,24},{1,5},{5... | collective-permute-start | bytes 294920 | tf_op jit(solution)/shard_map/ppermute | solution.py:333
  30.0 5.8 %collective-permute-start.5 = (bf16[2,12,16,128]{3,2,1,0:T(8,128)(2,1)S(1)}, bf16[2,12,16,128]{3,2,1,0:T(8,128)(2,1)S(1)}, u32[]{:S(2)}, u32[]{:S(2)}) collective-permute-start(bf16[2,12,16,128]{3,2,1,0:T(8,128)(2,1)S(1)} %get-tuple-element.31), channel_id=1, source_target_pairs={{0,4},{4,0},{8,12},{12,8},{16,20},{20,16},{24,28},{28,24},{1,5},{5... | collective-permute-start | bytes 294920 | tf_op jit(solution)/shard_map/ppermute | solution.py:333
  30.3 5.5 %collective-permute-start.9 = (bf16[2,6,16,128]{3,2,1,0:T(8,128)(2,1)S(1)}, bf16[2,6,16,128]{3,2,1,0:T(8,128)(2,1)S(1)}, u32[]{:S(2)}, u32[]{:S(2)}) collective-permute-start(bf16[2,6,16,128]{3,2,1,0:T(8,128)(2,1)S(1)} %get-tuple-element.38), channel_id=1, source_target_pairs={{0,8},{4,12},{8,0},{12,4},{16,24},{20,28},{24,16},{28,20},{1,9},{5... | collective-permute-start | bytes 147464 | tf_op jit(solution)/shard_map/ppermute | solution.py:333
  33.8 5.1 %collective-permute-start.14 = (bf16[2,6,16,128]{3,2,1,0:T(8,128)(2,1)S(1)}, bf16[2,6,16,128]{3,2,1,0:T(8,128)(2,1)S(1)}, u32[]{:S(2)}, u32[]{:S(2)}) collective-permute-start(bf16[2,6,16,128]{3,2,1,0:T(8,128)(2,1)S(1)} %get-tuple-element.46), channel_id=1, source_target_pairs={{0,8},{4,12},{8,0},{12,4},{16,24},{20,28},{24,16},{28,20},{1,9},{5... | collective-permute-start | bytes 147464 | tf_op jit(solution)/shard_map/ppermute | solution.py:333
  35.9 9.7 %collective-permute-start.6 = (bf16[1,12,16,128]{3,2,1,0:T(8,128)(2,1)S(1)}, bf16[1,12,16,128]{3,2,1,0:T(8,128)(2,1)S(1)}, u32[]{:S(2)}, u32[]{:S(2)}) collective-permute-start(bf16[1,12,16,128]{3,2,1,0:T(8,128)(2,1)S(1)} %get-tuple-element.33), channel_id=1, source_target_pairs={{0,16},{4,20},{8,24},{12,28},{16,0},{20,4},{24,8},{28,12},{1,17},{... | collective-permute-start | bytes 147464 | tf_op jit(solution)/shard_map/ppermute | solution.py:333
  38.5 4.7 %collective-permute-start.10 = (bf16[1,6,16,128]{3,2,1,0:T(8,128)(2,1)S(1)}, bf16[1,6,16,128]{3,2,1,0:T(8,128)(2,1)S(1)}, u32[]{:S(2)}, u32[]{:S(2)}) collective-permute-start(bf16[1,6,16,128]{3,2,1,0:T(8,128)(2,1)S(1)} %get-tuple-element.40), channel_id=1, source_target_pairs={{0,16},{4,20},{8,24},{12,28},{16,0},{20,4},{24,8},{28,12},{1,17},{... | collective-permute-start | bytes 73736 | tf_op jit(solution)/shard_map/ppermute | solution.py:333
  38.9 6.7 %collective-permute-start.15 = (bf16[1,6,16,128]{3,2,1,0:T(8,128)(2,1)S(1)}, bf16[1,6,16,128]{3,2,1,0:T(8,128)(2,1)S(1)}, u32[]{:S(2)}, u32[]{:S(2)}) collective-permute-start(bf16[1,6,16,128]{3,2,1,0:T(8,128)(2,1)S(1)} %get-tuple-element.48), channel_id=1, source_target_pairs={{0,16},{4,20},{8,24},{12,28},{16,0},{20,4},{24,8},{28,12},{1,17},{... | collective-permute-start | bytes 73736 | tf_op jit(solution)/shard_map/ppermute | solution.py:333
  43.3 3.9 %collective-permute-start.11 = (bf16[6,16,128]{2,1,0:T(8,128)(2,1)S(1)}, bf16[6,16,128]{2,1,0:T(8,128)(2,1)S(1)}, u32[]{:S(2)}, u32[]{:S(2)}) collective-permute-start(bf16[6,16,128]{2,1,0:T(8,128)(2,1)S(1)} %shard_map.61), channel_id=1, source_target_pairs={{0,2},{1,3},{2,0},{3,1},{4,6},{5,7},{6,4},{7,5},{8,10},{9,11},{10,... | collective-permute-start | bytes 73736 | tf_op jit(solution)/shard_map/ppermute | solution.py:330

commit v5 on v4

--- a/solution.py
+++ b/solution.py
@@ -129,128 +129,121 @@
     return product.reshape(pieces, BLOCK // pieces, BLOCK)
 
 
-def push_kernel(cols_per, per_peer, all_rows, all_cols, hidden, pushed, rows, cols, table, list_sems, sems):
-    fetched = [
-        pltpu.make_async_copy(a, b, list_sems.at[n]) for n, (a, b) in enumerate(((all_rows, rows), (all_cols, cols)))
-    ]
-    for copy in fetched:
-        copy.start()
-    for copy in fetched:
-        copy.wait()
-    listed_at(table, cols, rows, lax.axis_index("tensor") ^ 2, cols_per, per_peer)
-    copies = [pltpu.make_async_copy(column(hidden, table[j]), pushed.at[j], sems.at[j]) for j in range(per_peer)]
+def fetch(pairs, sems):
+    copies = [pltpu.make_async_copy(source, there, sems.at[n]) for n, (source, there) in enumerate(pairs)]
     for copy in copies:
         copy.start()
+    return copies
+
+
+def start_columns(source, table, there, sems):
+    copies = [pltpu.make_async_copy(column(source, table[j]), there.at[j], sems.at[j]) for j in range(there.shape[0])]
     for copy in copies:
+        copy.start()
+    return copies
+
+
+def push_kernel(cols_per, per_peer, all_rows, all_cols, hidden, cross, core, rows, cols, table, list_sems, sems):
+    for copy in fetch(((all_rows, rows), (all_cols, cols)), list_sems):
+        copy.wait()
+    me = lax.axis_index("tensor")
+    copies = []
+    for n, (distance, there) in enumerate(((2, cross), (1, core))):
+        listed_at(table, cols, rows, me ^ distance, cols_per, per_peer)
+        copies += start_columns(hidden, table, there, sems.at[n])
+    for copy in copies:
         copy.wait()
 
 
 def push_blocks(rows, cols, hidden, cols_per, per_peer):
     return pl.pallas_call(
         functools.partial(push_kernel, cols_per, per_peer),
-        out_shape=pltpu.VMEM((per_peer, hidden.shape[0], BLOCK), hidden.dtype),
+        out_shape=[pltpu.VMEM((per_peer, hidden.shape[0], BLOCK), hidden.dtype)] * 2,
         in_specs=[HBM, HBM, HBM],
-        out_specs=VMEM,
+        out_specs=[VMEM, VMEM],
         scratch_shapes=[
             pltpu.SMEM(rows.shape, jnp.int32),
             pltpu.SMEM(cols.shape, jnp.int32),
             pltpu.SMEM((per_peer + 1,), jnp.int32),
             pltpu.SemaphoreType.DMA((2,)),
-            pltpu.SemaphoreType.DMA((per_peer,)),
+            pltpu.SemaphoreType.DMA((2, per_peer)),
         ],
         name="push_blocks",
         compiler_params=SMALL,
     )(in_hbm(rows), in_hbm(cols), in_hbm(hidden))
 
 
-def pack_kernel(cols_per, per_peer, came1, came3, grad_out, for_core, for_far, list1, list3, table, list_sems, sems):
+def near_kernel(order, cols_per, per_peer, pieces, all_rows, all_cols, came1, hidden, grad_out, arrived, kept, sent, own, right, parts, rows, cols, list1, table, list_sems, sems):
     me = lax.axis_index("tensor")
-    fetched = [pltpu.make_async_copy(a, b, list_sems.at[n]) for n, (a, b) in enumerate(((came1, list1), (came3, list3)))]
-    for copy in fetched:
-        copy.start()
-    for copy in fetched:
-        copy.wait()
-    copies = []
-    for n, (listed, there) in enumerate(((list1, for_core), (list3, for_far))):
-        listed_at(table, listed, None, me, cols_per, per_peer)
-        for j in range(per_peer):
-            copies.append(pltpu.make_async_copy(column(grad_out, table[j]), there.at[j], sems.at[n, j]))
-            copies[-1].start()
+    for copy in fetch(((all_rows, rows), (all_cols, cols), (came1, list1)), list_sems):
+        copy.wait()
+    listed_at(table, cols, rows, me, cols_per, per_peer)
+    copies = start_columns(hidden, table, own, sems.at[0])
+    listed_at(table, cols, None, me, cols_per, per_peer)
+    copies += start_columns(grad_out, table, right.at[pl.ds(0, per_peer)], sems.at[1])
+    listed_at(table, list1, None, me, cols_per, per_peer)
+    copies += start_columns(grad_out, table, right.at[pl.ds(per_peer, per_peer)], sems.at[2])
     for copy in copies:
         copy.wait()
-
-
-def pack_columns(list1, list3, grad_out, per_peer):
+    for item in range(2 * per_peer):
+        left = own[item] if item < per_peer else arrived[item - per_peer]
+        parts[:, item] = multiply(pieces, left, right[item])
+    split_pieces(order, parts, kept, sent)
+
+
+def near_products(rows, cols, list1, hidden, grad_out, arrived, per_peer, pieces, order):
     tok_rows, width = grad_out.shape
     return pl.pallas_call(
-        functools.partial(pack_kernel, width // BLOCK, per_peer),
-        out_shape=[pltpu.VMEM((per_peer, tok_rows, BLOCK), grad_out.dtype)] * 2,
-        in_specs=[VMEM, VMEM, HBM],
+        functools.partial(near_kernel, order, width // BLOCK, per_peer, pieces),
+        out_shape=halved_shapes(pieces, 2 * per_peer),
+        in_specs=[HBM, HBM, VMEM, HBM, HBM, VMEM],
         out_specs=[VMEM, VMEM],
         scratch_shapes=[
+            pltpu.VMEM((per_peer, tok_rows, BLOCK), jnp.bfloat16),
+            pltpu.VMEM((2 * per_peer, tok_rows, BLOCK), jnp.bfloat16),
+            pltpu.VMEM((pieces, 2 * per_peer, BLOCK // pieces, BLOCK), jnp.float32),
+            pltpu.SMEM(rows.shape, jnp.int32),
+            pltpu.SMEM(cols.shape, jnp.int32),
             pltpu.SMEM(list1.shape, jnp.int32),
-            pltpu.SMEM(list3.shape, jnp.int32),
             pltpu.SMEM((per_peer + 1,), jnp.int32),
-            pltpu.SemaphoreType.DMA((2,)),
-            pltpu.SemaphoreType.DMA((2, per_peer)),
-        ],
-        name="pack_columns",
-        compiler_params=SMALL,
-    )(vectors(list1), vectors(list3), in_hbm(grad_out))
-
-
-def near_kernel(order, cols_per, per_peer, pieces, rows, cols, came2, hidden, grad_out, arrived, kept, sent, hidden_far, grad_guest, hidden_near, grad_near, parts, list2, table, list_sem, sems):
-    fetched = pltpu.make_async_copy(came2, list2, list_sem)
-    fetched.start()
-    me = lax.axis_index("tensor")
-    count = [0]
-
-    def gather(owner, listed, values, source, there, first):
-        listed_at(table, listed, values, owner, cols_per, per_peer)
-        copies = []
-        for j in range(per_peer):
-            copies.append(pltpu.make_async_copy(column(source, table[j]), there.at[first + j], sems.at[count[0], j]))
-            copies[-1].start()
-        count[0] += 1
-        return copies
-
-    mine = gather(me, cols, None, grad_out, grad_near, 0)
-    near = gather(me, cols, rows, hidden, hidden_near, 0)
-    near += gather(me ^ 1, cols, rows, hidden, hidden_near, per_peer)
-    later = gather(me ^ 3, cols, rows, hidden, hidden_far, 0)
-    fetched.wait()
-    later += gather(me, list2, None, grad_out, grad_guest, 0)
-    for copy in mine + near:
-        copy.wait()
-    for item in range(2 * per_peer):
-        right = grad_near[item] if item < per_peer else arrived[item - per_peer]
-        parts[:, item] = multiply(pieces, hidden_near[item], right)
-    split_pieces(order, parts, kept, sent)
-    for copy in later:
-        copy.wait()
-
-
-def near_products(rows, cols, list2, hidden, grad_out, arrived, per_peer, pieces, order):
-    tok_rows, width = grad_out.shape
-    near = 2 * per_peer
-    blocks = pltpu.VMEM((per_peer, tok_rows, BLOCK), jnp.bfloat16)
-    return pl.pallas_call(
-        functools.partial(near_kernel, order, width // BLOCK, per_peer, pieces),
-        out_shape=halved_shapes(pieces, near) + [blocks, blocks],
-        in_specs=[SMEM, SMEM, VMEM, HBM, HBM, VMEM],
-        out_specs=[VMEM] * 4,
-        scratch_shapes=[
-            pltpu.VMEM((near, tok_rows, BLOCK), jnp.bfloat16),
-            pltpu.VMEM((per_peer, tok_rows, BLOCK), jnp.bfloat16),
-            pltpu.VMEM((pieces, near, BLOCK // pieces, BLOCK), jnp.float32),
-            pltpu.SMEM(list2.shape, jnp.int32),
-            pltpu.SMEM((per_peer + 1,), jnp.int32),
-            pltpu.SemaphoreType.DMA,
-            pltpu.SemaphoreType.DMA((5, per_peer)),
+            pltpu.SemaphoreType.DMA((3,)),
+            pltpu.SemaphoreType.DMA((3, per_peer)),
         ],
         name="near_products",
         compiler_params=SMALL,
-    )(scalars(rows), scalars(cols), vectors(list2), in_hbm(hidden), in_hbm(grad_out), vectors(arrived))
+    )(in_hbm(rows), in_hbm(cols), vectors(list1), in_hbm(hidden), in_hbm(grad_out), vectors(arrived))
+
+
+def pack_kernel(cols_per, per_peer, all_rows, all_cols, came2, came3, hidden, grad_out, for_far, for_guests, hidden_far, rows, cols, list2, list3, table, list_sems, sems):
+    me = lax.axis_index("tensor")
+    for copy in fetch(((all_rows, rows), (all_cols, cols), (came2, list2), (came3, list3)), list_sems):
+        copy.wait()
+    listed_at(table, list3, None, me, cols_per, per_peer)
+    copies = start_columns(grad_out, table, for_far, sems.at[0])
+    listed_at(table, list2, None, me, cols_per, per_peer)
+    copies += start_columns(grad_out, table, for_guests, sems.at[1])
+    listed_at(table, cols, rows, me ^ 3, cols_per, per_peer)
+    copies += start_columns(hidden, table, hidden_far, sems.at[2])
+    for copy in copies:
+        copy.wait()
+
+
+def pack_blocks(rows, cols, list2, list3, hidden, grad_out, per_peer):
+    tok_rows, width = grad_out.shape
+    return pl.pallas_call(
+        functools.partial(pack_kernel, width // BLOCK, per_peer),
+        out_shape=[pltpu.VMEM((per_peer, tok_rows, BLOCK), grad_out.dtype)] * 3,
+        in_specs=[HBM, HBM, VMEM, VMEM, HBM, HBM],
+        out_specs=[VMEM, VMEM, VMEM],
+        scratch_shapes=[pltpu.SMEM(value.shape, jnp.int32) for value in (rows, cols, list2, list3)]
+        + [
+            pltpu.SMEM((per_peer + 1,), jnp.int32),
+            pltpu.SemaphoreType.DMA((4,)),
+            pltpu.SemaphoreType.DMA((3, per_peer)),
+        ],
+        name="pack_blocks",
+        compiler_params=SMALL,
+    )(in_hbm(rows), in_hbm(cols), vectors(list2), vectors(list3), in_hbm(hidden), in_hbm(grad_out))
 
 
 def cross_kernel(order, pieces, left, right, kept, sent, parts):
@@ -269,6 +262,87 @@
         scratch_shapes=[pltpu.VMEM((pieces, count, BLOCK // pieces, BLOCK), jnp.float32)],
         compiler_params=SMALL,
     )(vectors(left), vectors(right))
+
+
+def my_half(first=0):
+    half = BLOCK // 2
+    return pl.ds(pl.multiple_of(((lax.axis_index("seq") & 1) ^ first) * half, half), half)
+
+
+def far_kernel(left, arrived, kept, sent, whole):
+    for j in range(arrived.shape[0]):
+        whole[j] = lax.dot_general(
+            left[j], arrived[j], (((0,), (0,)), ((), ())), preferred_element_type=jnp.float32
+        )
+    kept[...] = whole[:, my_half()]
+    sent[...] = whole[:, my_half(1)].astype(jnp.bfloat16)
+
+
+def far_products(left, arrived):
+    count = arrived.shape[0]
+    half = (count, BLOCK // 2, BLOCK)
+    return pl.pallas_call(
+        far_kernel,
+        out_shape=[pltpu.VMEM(half, jnp.float32), pltpu.VMEM(half, jnp.bfloat16)],
+        in_specs=[VMEM, VMEM],
+        out_specs=[VMEM, VMEM],
+        scratch_shapes=[pltpu.VMEM((count, BLOCK, BLOCK), jnp.float32)],
+        name="far_products",
+        compiler_params=SMALL,
+    )(vectors(left), vectors(arrived))
+
+
+def share_kernel(kept, received, still, sent):
+    total = kept[...] + received[...].astype(jnp.float32)
+    still[...] = total
+    sent[...] = total.astype(jnp.bfloat16)
+
+
+def share(kept, received):
+    return pl.pallas_call(
+        share_kernel,
+        out_shape=[pltpu.VMEM(kept.shape, jnp.float32), pltpu.VMEM(kept.shape, jnp.bfloat16)],
+        in_specs=[VMEM, VMEM],
+        out_specs=[VMEM, VMEM],
+        compiler_params=SMALL,
+    )(vectors(kept), vectors(received))
+
+
+def share_last_kernel(kept, received, sent):
+    sent[...] = (kept[...] + received[...].astype(jnp.float32)).astype(jnp.bfloat16)
+
+
+def share_last(kept, received):
+    return pl.pallas_call(
+        share_last_kernel,
+        out_shape=pltpu.VMEM(kept.shape, jnp.bfloat16),
+        in_specs=[VMEM, VMEM],
+        out_specs=VMEM,
+        compiler_params=SMALL,
+    )(vectors(kept), vectors(received))
+
+
+def compose_kernel(delivered, mine, other, owned, out):
+    far_items, rows = mine.shape[0], BLOCK // 2
+    for slot in range(out.shape[0]):
+        out[slot] = delivered[:, slot].reshape(BLOCK, BLOCK)
+        for half, source in ((my_half(), mine), (my_half(1), other)):
+            value = out[slot, half].astype(jnp.float32)
+            for j in range(far_items):
+                flag = jnp.concatenate([owned[slot * far_items + j]] * (rows // 8))
+                value = jnp.where(flag > 0, source[j].astype(jnp.float32), value)
+            out[slot, half] = value.astype(jnp.bfloat16)
+
+
+def compose(delivered, mine, other, owned):
+    return pl.pallas_call(
+        compose_kernel,
+        out_shape=jax.ShapeDtypeStruct((delivered.shape[1], BLOCK, BLOCK), jnp.bfloat16),
+        in_specs=[VMEM] * 4,
+        out_specs=VMEM,
+        name="compose",
+        compiler_params=SMALL,
+    )(vectors(delivered), vectors(mine), vectors(other), vectors(owned))
 
 
 def plan_kernel(cols_per, per_peer, cols, owners, places, seen):
@@ -298,27 +372,46 @@
     )(scalars(cols), scalars(owners))
 
 
-def settle_kernel(places, near, guests, kept, received, out):
+def flag_kernel(per_peer, places, owned):
+    first = lax.axis_index("seq") * CAP
+    owned[...] = jnp.zeros_like(owned)
+    for rank in range(per_peer):
+        slot = places[3 * per_peer + rank] - first
+        mine = jnp.logical_and(slot >= 0, slot < CAP)
+        owned[jnp.where(mine, slot * per_peer + rank, CAP * per_peer)] = jnp.ones(owned.shape[1:], jnp.float32)
+
+
+def flag_owned(places, per_peer):
+    return pl.pallas_call(
+        functools.partial(flag_kernel, per_peer),
+        out_shape=pltpu.VMEM((CAP * per_peer + 1, 8, BLOCK), jnp.float32),
+        in_specs=[SMEM],
+        out_specs=VMEM,
+        name="flag_owned",
+        compiler_params=SMALL,
+    )(scalars(places))
+
+
+def settle_kernel(places, own, core, guests, out):
     out[...] = jnp.zeros_like(out)
     first = 0
-    for source in (near, guests):
+    for source in (own, core, guests):
         for j in range(source.shape[0]):
-            out[places[first + j]] = source[j]
+            place = places[first + j]
+            out[lax.shift_right_logical(place, CAP.bit_length() - 1), place & (CAP - 1)] = source[j]
         first += source.shape[0]
-    for j in range(kept.shape[1]):
-        out[places[first + j]] = (kept[0, j] + received[0, j].astype(jnp.float32)).astype(jnp.bfloat16)
-
-
-def settle(places, near, guests, kept, received, pieces):
+
+
+def settle(places, own, core, guests, pieces):
     _, rows, _ = guests.shape
     return pl.pallas_call(
         settle_kernel,
-        out_shape=pltpu.VMEM((pieces * CAP, rows, BLOCK), jnp.bfloat16),
-        in_specs=[SMEM] + [VMEM] * 4,
+        out_shape=pltpu.VMEM((pieces, CAP, rows, BLOCK), jnp.bfloat16),
+        in_specs=[SMEM] + [VMEM] * 3,
         out_specs=VMEM,
         name="settle",
         compiler_params=SMALL,
-    )(scalars(places), vectors(near), vectors(guests), vectors(kept), vectors(received))
+    )(scalars(places), vectors(own), vectors(core), vectors(guests))
 
 
 def sparse_on_device(hidden, grad_out, block_rows, block_cols, block_owner):
@@ -332,40 +425,43 @@
     def exchange(sent, distance):
         return lax.ppermute(sent, "seq", [(i, i ^ distance) for i in range(seq_count)])
 
-    def reduce_pieces(order, kept, sent):
+    def reduce_pieces(order, kept, sent, counts):
         for step, distance in enumerate(order):
             received = exchange(sent, distance)
             if step == len(order) - 1:
-                return finish(kept, received, (kept.shape[1],))[0]
+                return finish(kept, received, counts)
             kept, sent = halve([(kept, received)])
 
     near_order, guest_order = (2, 1, 4), (1, 2, 4)
-    list3 = to_peer(block_cols, 3)
-    pushed = push_blocks(block_rows, block_cols, hidden, cols_per, per_peer)
-    guests = to_peer(pushed, 2)
+    for_cross, for_core = push_blocks(block_rows, block_cols, hidden, cols_per, per_peer)
+    list2 = to_peer(block_cols, 2)
+    guests = to_peer(for_cross, 2)
+    from_core = to_peer(for_core, 1)
     list1 = to_peer(block_cols, 1)
-    list2 = to_peer(list3, 1)
-    for_core, for_far = pack_columns(list1, list3, grad_out, per_peer)
-    from_core = to_peer(for_core, 1)
+    near_kept, near_sent = near_products(
+        block_rows, block_cols, list1, hidden, grad_out, from_core, per_peer, seq_count, near_order
+    )
+    list3 = to_peer(list2, 1)
+    own_sum, core_sum = reduce_pieces(near_order, near_kept, near_sent, (per_peer, per_peer))
+    core_back = to_peer(core_sum, 1)
+    for_far, for_guests, hidden_far = pack_blocks(block_rows, block_cols, list2, list3, hidden, grad_out, per_peer)
     from_far = to_peer(for_far, 3)
-    near_kept, near_sent, hidden_far, grad_guest = near_products(
-        block_rows, block_cols, list2, hidden, grad_out, from_core, per_peer, seq_count, near_order
-    )
-    near_sum = reduce_pieces(near_order, near_kept, near_sent)
     places = plan(block_cols, block_owner, cols_per, per_peer)
-    guest_kept, guest_sent = cross_products(guests, grad_guest, seq_count, guest_order)
-    guest_sum = reduce_pieces(guest_order, guest_kept, guest_sent)
+    owned = flag_owned(places, per_peer)
+    guest_kept, guest_sent = cross_products(guests, for_guests, seq_count, guest_order)
+    (guest_sum,) = reduce_pieces(guest_order, guest_kept, guest_sent, (per_peer,))
     guest_back = to_peer(guest_sum, 2)
-    kept, sent = cross_products(hidden_far, from_far, seq_count, guest_order)
-    received = exchange(sent, guest_order[0])
-    for distance in guest_order[1:]:
-        kept, sent = halve([(kept, received)])
+    kept, sent = far_products(hidden_far, from_far)
+    for distance in guest_order:
         received = exchange(sent, distance)
-    placed = settle(places, near_sum, guest_back, kept, received, seq_count)
-    delivered = lax.all_to_all(
-        placed.reshape(seq_count, CAP, -1, BLOCK), "seq", split_axis=0, concat_axis=0, tiled=True
-    )
-    return delivered.transpose(1, 0, 2, 3).reshape(1, CAP, BLOCK, BLOCK)
+        if distance == guest_order[-1]:
+            sent = share_last(kept, received)
+        else:
+            kept, sent = share(kept, received)
+    other = lax.ppermute(sent, "seq", [(i, i ^ 1) for i in range(seq_count)])
+    placed = settle(places, own_sum, core_back, guest_back, seq_count)
+    delivered = lax.all_to_all(placed, "seq", split_axis=0, concat_axis=0, tiled=True)
+    return compose(delivered, sent, other, owned)[None]
 
 
 def solution(mesh):

time: 61.1 us -> 69.3 us (1.13)
  blocking collectives: 12.8 us -> 0 us
  waiting for transfers between devices: 16.1 us -> 26.1 us
  starting transfers between devices: 22.7 us -> 31.9 us
  Pallas kernels: 8.29 us -> 10.7 us
  local copies, waits for them, and re-layouts: 0.73 us -> 0.02 us
    all_to_all x1 -> x0, blocking collectives: 12.8 us -> none  [sparse_on_device(): lax.all_to_all(placed.reshape(seq_count, CAP, -1, BLOCK), 'seq', split_ax...]
    ppermute x9, waiting for transfers between devices: 3.21 us -> 15.2 us  [exchange(): lax.ppermute(sent, 'seq', [(i, i ^ distance) for i in range(seq_count)])]
    all_to_all x0 -> x1, starting transfers between devices: none -> 5.64 us  [sparse_on_device(): lax.all_to_all(placed, 'seq', split_axis=0, concat_axis=0, tiled=True)]
    ppermute x7 -> x8, waiting for transfers between devices: 12.9 us -> 8.34 us  [to_peer(): lax.ppermute(value, 'tensor', [(i, i ^ distance) for i in range(tensor_co...]
    ppermute x9, starting transfers between devices: 15.2 us -> 17.8 us  [exchange(): lax.ppermute(sent, 'seq', [(i, i ^ distance) for i in range(seq_count)])]
    ppermute x0 -> x1, waiting for transfers between devices: none -> 2.57 us  [sparse_on_device(): other = lax.ppermute(sent, 'seq', [(i, i ^ 1) for i in range(seq_count)])]
    pallas_call x2 -> x8, Pallas kernels: 2.01 us -> 4.57 us  [the longest x1 2.34 us: pack_blocks(): pl.pallas_call(functools.partial(pack_kernel, width // BLOCK, per_peer),...]
    ppermute x0 -> x1, starting transfers between devices: none -> 2.45 us  [sparse_on_device(): other = lax.ppermute(sent, 'seq', [(i, i ^ 1) for i in range(seq_count)])]
  transfers between devices with their start and end apart: 16 -> 19, of which waited for: 8 -> 10; matrix products, arithmetic and copies ran while one was open for 0% -> 0% of each run, Pallas kernels for 10% -> 11%
where the time goes in v5:
time: 69.3 us; the launch traced here: 68.9 us
  starting transfers between devices  31.9 us (46%)
  waiting for transfers between devices  26.1 us (38%)
  Pallas kernels  10.7 us (15%)
    ppermute x9, starting transfers between devices, exchange(): lax.ppermute(sent, 'seq', [(i, i ^ distance) for i in range(seq_count)])  17.8 us
    ppermute x9, waiting for transfers between devices, exchange(): lax.ppermute(sent, 'seq', [(i, i ^ distance) for i in range(seq_count)])  15.2 us
    ppermute x8, waiting for transfers between devices, to_peer(): lax.ppermute(value, 'tensor', [(i, i ^ distance) for i in range(tensor_co...  8.34 us
    ppermute x8, starting transfers between devices, to_peer(): lax.ppermute(value, 'tensor', [(i, i ^ distance) for i in range(tensor_co...  6 us
    all_to_all x1, starting transfers between devices, sparse_on_device(): lax.all_to_all(placed, 'seq', split_axis=0, concat_axis=0, tiled=True)  5.64 us
    pallas_call x1, Pallas kernels, near_products(): pl.pallas_call(functools.partial(near_kernel, order, width // BLOCK, per_...  2.78 us
    ppermute x1, waiting for transfers between devices, sparse_on_device(): other = lax.ppermute(sent, 'seq', [(i, i ^ 1) for i in range(seq_count)])  2.57 us
    ppermute x1, starting transfers between devices, sparse_on_device(): other = lax.ppermute(sent, 'seq', [(i, i ^ 1) for i in range(seq_count)])  2.45 us
  transfers between devices with their start and end apart: 19, of which 10 were waited for; matrix products, arithmetic and copies ran while one was open for 0% of the time, Pallas kernels for 11%

profile of v5, /device:TPU:0, one launch (start us, length us, event | category | flops | bytes accessed | tf_op | source)
XLA Modules:
  0.0 68.9 jit_solution(16837814252380782735)
XLA Ops:
  0.0 2.2 %push_blocks.1 = (bf16[6,256,128]{2,1,0:T(8,128)(2,1)S(1)}, bf16[6,256,128]{2,1,0:T(8,128)(2,1)S(1)}) custom-call(s32[1,24]{1,0:T(1,128)} %all_rows.5, s32[1,24]{1,0:T(1,128)} %all_cols.5, bf16[256,13312]{1,0:T(8,128)(2,1)} %hidden.5), custom_call_target="tpu_custom_call" | custom-call | tf_op jit(solution)/shard_map/push_blocks/pallas_call | solution.py:159
  2.3 0.6 collective-permute-start.1
  2.8 2.6 %collective-permute-start.6 = (bf16[6,256,128]{2,1,0:T(8,128)(2,1)S(1)}, bf16[6,256,128]{2,1,0:T(8,128)(2,1)S(1)}, u32[]{:S(2)}, u32[]{:S(2)}) collective-permute-start(bf16[6,256,128]{2,1,0:T(8,128)(2,1)S(1)} %get-tuple-element.39), channel_id=1, source_target_pairs={{0,2},{1,3},{2,0},{3,1},{4,6},{5,7},{6,4},{7,5},{8,10},{9,11},{10,... | collective-permute-start | bytes 1179656 | tf_op jit(solution)/shard_map/ppermute | solution.py:423
  5.4 0.2 collective-permute-start
  5.6 1.0 %collective-permute-done.came1 = s32[1,24]{1,0:T(1,128)S(1)} collective-permute-done((s32[1,24]{1,0:T(1,128)S(1)}, s32[1,24]{1,0:T(1,128)S(1)}, u32[]{:S(2)}, u32[]{:S(2)}) %collective-permute-start) | collective-permute-done | bytes 128 | tf_op jit(solution)/shard_map/ppermute | solution.py:423
  6.6 0.0 collective-permute-done.1.arrived
  6.6 2.8 %near_products.1 = (f32[4,12,16,128]{3,2,1,0:T(8,128)S(1)}, bf16[4,12,16,128]{3,2,1,0:T(8,128)(2,1)S(1)}) custom-call(s32[1,24]{1,0:T(1,128)} %all_rows.5, s32[1,24]{1,0:T(1,128)} %all_cols.5, s32[1,24]{1,0:T(1,128)S(1)} %collective-permute-done.came1, bf16[256,13312]{1,0:T(8,128)(2,1)} %hidden.5, bf16[256,4096]{1,0:T(8,128)(2,1)} %grad_out.3, ...), custom_call_target="tpu_custom_call" | custom-call | tf_op jit(solution)/shard_map/near_products/pallas_call | solution.py:196
  9.4 0.0 copy-start.2
  9.4 0.0 copy-start.3
  9.4 1.6 %collective-permute-start.2 = (bf16[4,12,16,128]{3,2,1,0:T(8,128)(2,1)S(1)}, bf16[4,12,16,128]{3,2,1,0:T(8,128)(2,1)S(1)}, u32[]{:S(2)}, u32[]{:S(2)}) collective-permute-start(bf16[4,12,16,128]{3,2,1,0:T(8,128)(2,1)S(1)} %get-tuple-element.32), channel_id=1, source_target_pairs={{0,8},{4,12},{8,0},{12,4},{16,24},{20,28},{24,16},{28,20},{1,9},{5... | collective-permute-start | bytes 589832 | tf_op jit(solution)/shard_map/ppermute | solution.py:426
  11.0 0.5 collective-permute-start.7
  11.5 3.7 %collective-permute-done.7.came2 = s32[1,24]{1,0:T(1,128)S(1)} collective-permute-done((s32[1,24]{1,0:T(1,128)S(1)}, s32[1,24]{1,0:T(1,128)S(1)}, u32[]{:S(2)}, u32[]{:S(2)}) %collective-permute-start.7) | collective-permute-done | bytes 128 | tf_op jit(solution)/shard_map/ppermute | solution.py:423
  15.2 0.0 collective-permute-start.8
  15.2 1.2 %collective-permute-done.8.came3 = s32[1,24]{1,0:T(1,128)S(1)} collective-permute-done((s32[1,24]{1,0:T(1,128)S(1)}, s32[1,24]{1,0:T(1,128)S(1)}, u32[]{:S(2)}, u32[]{:S(2)}) %collective-permute-start.8) | collective-permute-done | bytes 128 | tf_op jit(solution)/shard_map/ppermute | solution.py:423
  16.4 2.3 %pack_blocks.1 = (bf16[6,256,128]{2,1,0:T(8,128)(2,1)S(1)}, bf16[6,256,128]{2,1,0:T(8,128)(2,1)S(1)}, bf16[6,256,128]{2,1,0:T(8,128)(2,1)S(1)}) custom-call(s32[1,24]{1,0:T(1,128)} %all_rows.5, s32[1,24]{1,0:T(1,128)} %all_cols.5, s32[1,24]{1,0:T(1,128)S(1)} %collective-permute-done.7.came2, s32[1,24]{1,0:T(1,128)S(1)} %collective-permute-done.8.came3, ...), custom_call_target="tpu_custom_call" | custom-call | tf_op jit(solution)/shard_map/pack_blocks/pallas_call | solution.py:233
  18.7 1.6 %collective-permute-start.13 = (bf16[6,256,128]{2,1,0:T(8,128)(2,1)S(1)}, bf16[6,256,128]{2,1,0:T(8,128)(2,1)S(1)}, u32[]{:S(2)}, u32[]{:S(2)}) collective-permute-start(bf16[6,256,128]{2,1,0:T(8,128)(2,1)S(1)} %get-tuple-element.48), channel_id=1, source_target_pairs={{0,3},{1,2},{2,1},{3,0},{4,7},{5,6},{6,5},{7,4},{8,11},{9,10},{10,... | collective-permute-start | bytes 1179656 | tf_op jit(solution)/shard_map/ppermute | solution.py:423
  20.3 0.0 collective-permute-done.6.left
  20.3 0.3 shard_map.58
  20.6 1.6 %collective-permute-start.9 = (bf16[4,6,16,128]{3,2,1,0:T(8,128)(2,1)S(1)}, bf16[4,6,16,128]{3,2,1,0:T(8,128)(2,1)S(1)}, u32[]{:S(2)}, u32[]{:S(2)}) collective-permute-start(bf16[4,6,16,128]{3,2,1,0:T(8,128)(2,1)S(1)} %get-tuple-element.42), channel_id=1, source_target_pairs={{0,4},{4,0},{8,12},{12,8},{16,20},{20,16},{24,28},{28,24},{1,5},{5... | collective-permute-start | bytes 294920 | tf_op jit(solution)/shard_map/ppermute | solution.py:426
  22.2 0.0 collective-permute-done.2.refs_1_
  22.2 0.6 collective-permute-start.3
  22.8 3.5 %collective-permute-done.9.refs_1_ = bf16[4,6,16,128]{3,2,1,0:T(8,128)(2,1)S(1)} collective-permute-done((bf16[4,6,16,128]{3,2,1,0:T(8,128)(2,1)S(1)}, bf16[4,6,16,128]{3,2,1,0:T(8,128)(2,1)S(1)}, u32[]{:S(2)}, u32[]{:S(2)}) %collective-permute-start.9) | collective-permute-done | bytes 98336 | tf_op jit(solution)/shard_map/ppermute | solution.py:426
  26.4 1.6 %collective-permute-start.10 = (bf16[2,6,16,128]{3,2,1,0:T(8,128)(2,1)S(1)}, bf16[2,6,16,128]{3,2,1,0:T(8,128)(2,1)S(1)}, u32[]{:S(2)}, u32[]{:S(2)}) collective-permute-start(bf16[2,6,16,128]{3,2,1,0:T(8,128)(2,1)S(1)} %get-tuple-element.44), channel_id=1, source_target_pairs={{0,8},{4,12},{8,0},{12,4},{16,24},{20,28},{24,16},{28,20},{1,9},{5... | collective-permute-start | bytes 147464 | tf_op jit(solution)/shard_map/ppermute | solution.py:426
  28.0 0.0 collective-permute-done.3.refs_1_
  28.0 2.7 %collective-permute-start.4 = (bf16[1,12,16,128]{3,2,1,0:T(8,128)(2,1)S(1)}, bf16[1,12,16,128]{3,2,1,0:T(8,128)(2,1)S(1)}, u32[]{:S(2)}, u32[]{:S(2)}) collective-permute-start(bf16[1,12,16,128]{3,2,1,0:T(8,128)(2,1)S(1)} %get-tuple-element.36), channel_id=1, source_target_pairs={{0,16},{4,20},{8,24},{12,28},{16,0},{20,4},{24,8},{28,12},{1,17},{... | collective-permute-start | bytes 147464 | tf_op jit(solution)/shard_map/ppermute | solution.py:426
  30.7 0.0 collective-permute-done.10.refs_1_
  30.7 2.9 %collective-permute-start.11 = (bf16[1,6,16,128]{3,2,1,0:T(8,128)(2,1)S(1)}, bf16[1,6,16,128]{3,2,1,0:T(8,128)(2,1)S(1)}, u32[]{:S(2)}, u32[]{:S(2)}) collective-permute-start(bf16[1,6,16,128]{3,2,1,0:T(8,128)(2,1)S(1)} %get-tuple-element.46), channel_id=1, source_target_pairs={{0,16},{4,20},{8,24},{12,28},{16,0},{20,4},{24,8},{28,12},{1,17},{... | collective-permute-start | bytes 73736 | tf_op jit(solution)/shard_map/ppermute | solution.py:426
  33.6 1.9 %collective-permute-done.11.received = bf16[1,6,16,128]{3,2,1,0:T(8,128)(2,1)S(1)} collective-permute-done((bf16[1,6,16,128]{3,2,1,0:T(8,128)(2,1)S(1)}, bf16[1,6,16,128]{3,2,1,0:T(8,128)(2,1)S(1)}, u32[]{:S(2)}, u32[]{:S(2)}) %collective-permute-start.11) | collective-permute-done | bytes 24608 | tf_op jit(solution)/shard_map/ppermute | solution.py:426
  35.5 0.6 collective-permute-start.12
  36.1 0.0 collective-permute-done.4.received
  36.1 0.1 collective-permute-start.5
  36.2 0.7 %plan.1.places = s32[24]{0:T(128)S(4)} custom-call(s32[1,24]{1,0:T(1,128)S(1)} %copy-done.2, s32[1,24]{1,0:T(1,128)S(1)} %copy-done.3), custom_call_target="tpu_custom_call" | custom-call | tf_op jit(solution)/shard_map/plan/pallas_call | solution.py:364
  36.9 2.5 %collective-permute-done.12.guests = bf16[6,16,128]{2,1,0:T(8,128)(2,1)S(1)} collective-permute-done((bf16[6,16,128]{2,1,0:T(8,128)(2,1)S(1)}, bf16[6,16,128]{2,1,0:T(8,128)(2,1)S(1)}, u32[]{:S(2)}, u32[]{:S(2)}) %collective-permute-start.12) | collective-permute-done | bytes 24608 | tf_op jit(solution)/shard_map/ppermute | solution.py:423
  39.4 0.0 collective-permute-done.5.core
  39.4 0.8 %settle.1 = bf16[8,8,16,128]{3,2,1,0:T(8,128)(2,1)} custom-call(s32[24]{0:T(128)S(4)} %plan.1.places, bf16[6,16,128]{2,1,0:T(8,128)(2,1)S(1)} %get-tuple-element.37.own, bf16[6,16,128]{2,1,0:T(8,128)(2,1)S(1)} %collective-permute-done.5.core, bf16[6,16,128]{2,1,0:T(8,128)(2,1)S(1)} %collective-permute-done.12.guests), custom_call_target="tpu_custom_call" | custom-call | tf_op jit(solution)/shard_map/settle/pallas_call | solution.py:407
  40.2 5.6 %all-to-all-start = ((bf16[8,8,16,128]{3,2,1,0:T(8,128)(2,1)}), bf16[8,8,16,128]{3,2,1,0:T(8,128)(2,1)S(1)}, u32[]{:S(2)}, u32[]{:S(2)}) async-start(bf16[8,8,16,128]{3,2,1,0:T(8,128)(2,1)} %settle.1), calls=%async_computation | async-start | bytes 524288 | tf_op jit(solution)/shard_map/all_to_all | solution.py:463
  45.8 0.0 collective-permute-done.13.arrived
  45.8 0.3 far_products.1
  46.2 2.1 %collective-permute-start.14 = (bf16[6,64,128]{2,1,0:T(8,128)(2,1)S(1)}, bf16[6,64,128]{2,1,0:T(8,128)(2,1)S(1)}, u32[]{:S(2)}, u32[]{:S(2)}) collective-permute-start(bf16[6,64,128]{2,1,0:T(8,128)(2,1)S(1)} %get-tuple-element.50), channel_id=1, source_target_pairs={{0,4},{4,0},{8,12},{12,8},{16,20},{20,16},{24,28},{28,24},{1,5},{5... | collective-permute-start | bytes 294920 | tf_op jit(solution)/shard_map/ppermute | solution.py:426
  48.3 3.8 %collective-permute-done.14.received = bf16[6,64,128]{2,1,0:T(8,128)(2,1)S(1)} collective-permute-done((bf16[6,64,128]{2,1,0:T(8,128)(2,1)S(1)}, bf16[6,64,128]{2,1,0:T(8,128)(2,1)S(1)}, u32[]{:S(2)}, u32[]{:S(2)}) %collective-permute-start.14) | collective-permute-done | bytes 98336 | tf_op jit(solution)/shard_map/ppermute | solution.py:426
  52.1 2.0 %collective-permute-start.15 = (bf16[6,64,128]{2,1,0:T(8,128)(2,1)S(1)}, bf16[6,64,128]{2,1,0:T(8,128)(2,1)S(1)}, u32[]{:S(2)}, u32[]{:S(2)}) collective-permute-start(bf16[6,64,128]{2,1,0:T(8,128)(2,1)S(1)} %get-tuple-element.52), channel_id=1, source_target_pairs={{0,8},{4,12},{8,0},{12,4},{16,24},{20,28},{24,16},{28,20},{1,9},{5... | collective-permute-start | bytes 294920 | tf_op jit(solution)/shard_map/ppermute | solution.py:426
  54.0 3.1 %collective-permute-done.15.received = bf16[6,64,128]{2,1,0:T(8,128)(2,1)S(1)} collective-permute-done((bf16[6,64,128]{2,1,0:T(8,128)(2,1)S(1)}, bf16[6,64,128]{2,1,0:T(8,128)(2,1)S(1)}, u32[]{:S(2)}, u32[]{:S(2)}) %collective-permute-start.15) | collective-permute-done | bytes 98336 | tf_op jit(solution)/shard_map/ppermute | solution.py:426
  57.2 2.7 %collective-permute-start.16 = (bf16[6,64,128]{2,1,0:T(8,128)(2,1)S(1)}, bf16[6,64,128]{2,1,0:T(8,128)(2,1)S(1)}, u32[]{:S(2)}, u32[]{:S(2)}) collective-permute-start(bf16[6,64,128]{2,1,0:T(8,128)(2,1)S(1)} %get-tuple-element.54), channel_id=1, source_target_pairs={{0,16},{4,20},{8,24},{12,28},{16,0},{20,4},{24,8},{28,12},{1,17},{... | collective-permute-start | bytes 294920 | tf_op jit(solution)/shard_map/ppermute | solution.py:426
  60.0 2.8 %collective-permute-done.16.received = bf16[6,64,128]{2,1,0:T(8,128)(2,1)S(1)} collective-permute-done((bf16[6,64,128]{2,1,0:T(8,128)(2,1)S(1)}, bf16[6,64,128]{2,1,0:T(8,128)(2,1)S(1)}, u32[]{:S(2)}, u32[]{:S(2)}) %collective-permute-start.16) | collective-permute-done | bytes 98336 | tf_op jit(solution)/shard_map/ppermute | solution.py:426
  62.8 2.5 %collective-permute-start.17 = (bf16[6,64,128]{2,1,0:T(8,128)(2,1)S(1)}, bf16[6,64,128]{2,1,0:T(8,128)(2,1)S(1)}, u32[]{:S(2)}, u32[]{:S(2)}) collective-permute-start(bf16[6,64,128]{2,1,0:T(8,128)(2,1)S(1)} %shard_map.64.mine), channel_id=1, source_target_pairs={{0,4},{4,0},{8,12},{12,8},{16,20},{20,16},{24,28},{28,24},{1,5},{5... | collective-permute-start | bytes 294920 | tf_op jit(solution)/shard_map/ppermute | solution.py:461
  65.3 2.6 %collective-permute-done.17.other = bf16[6,64,128]{2,1,0:T(8,128)(2,1)S(1)} collective-permute-done((bf16[6,64,128]{2,1,0:T(8,128)(2,1)S(1)}, bf16[6,64,128]{2,1,0:T(8,128)(2,1)S(1)}, u32[]{:S(2)}, u32[]{:S(2)}) %collective-permute-start.17) | collective-permute-done | bytes 98336 | tf_op jit(solution)/shard_map/ppermute | solution.py:461
  67.9 0.0 all-to-all-done.delivered
  67.9 1.0 %compose.1 = bf16[8,128,128]{2,1,0:T(8,128)(2,1)} custom-call(bf16[8,8,16,128]{3,2,1,0:T(8,128)(2,1)S(1)} %all-to-all-done.delivered, bf16[6,64,128]{2,1,0:T(8,128)(2,1)S(1)} %shard_map.64.mine, bf16[6,64,128]{2,1,0:T(8,128)(2,1)S(1)} %collective-permute-done.17.other, f32[49,8,128]{2,1,0:T(8,128)S(1)} %flag_owned.1.owned), custom_call_target="tpu_custom_call" | custom-call | tf_op jit(solution)/shard_map/compose/pallas_call | solution.py:338
  (16 shorter events, 0.2 us)
Async XLA Ops:
  0.0 5.4 %copy-start = (s32[1,24]{1,0:T(1,128)S(1)}, s32[1,24]{1,0:T(1,128)}, u32[]{:S(2)}) copy-start(s32[1,24]{1,0:T(1,128)} %all_cols.5) | copy-start | bytes 292
  0.0 11.0 %copy-start.1 = (s32[1,24]{1,0:T(1,128)S(1)}, s32[1,24]{1,0:T(1,128)}, u32[]{:S(2)}) copy-start(s32[1,24]{1,0:T(1,128)} %all_cols.5) | copy-start | bytes 292
  2.3 4.3 %collective-permute-start.1 = (bf16[6,256,128]{2,1,0:T(8,128)(2,1)S(1)}, bf16[6,256,128]{2,1,0:T(8,128)(2,1)S(1)}, u32[]{:S(2)}, u32[]{:S(2)}) collective-permute-start(bf16[6,256,128]{2,1,0:T(8,128)(2,1)S(1)} %get-tuple-element.30), channel_id=1, source_target_pairs={{0,1},{1,0},{2,3},{3,2},{4,5},{5,4},{6,7},{7,6},{8,9},{9,8},{10,11... | collective-permute-start | bytes 1179656 | tf_op jit(solution)/shard_map/ppermute | solution.py:423
  2.8 17.5 %collective-permute-start.6 = (bf16[6,256,128]{2,1,0:T(8,128)(2,1)S(1)}, bf16[6,256,128]{2,1,0:T(8,128)(2,1)S(1)}, u32[]{:S(2)}, u32[]{:S(2)}) collective-permute-start(bf16[6,256,128]{2,1,0:T(8,128)(2,1)S(1)} %get-tuple-element.39), channel_id=1, source_target_pairs={{0,2},{1,3},{2,0},{3,1},{4,6},{5,7},{6,4},{7,5},{8,10},{9,11},{10,... | collective-permute-start | bytes 1179656 | tf_op jit(solution)/shard_map/ppermute | solution.py:423
  5.4 1.2 %collective-permute-start = (s32[1,24]{1,0:T(1,128)S(1)}, s32[1,24]{1,0:T(1,128)S(1)}, u32[]{:S(2)}, u32[]{:S(2)}) collective-permute-start(s32[1,24]{1,0:T(1,128)S(1)} %copy-done), channel_id=1, source_target_pairs={{0,1},{1,0},{2,3},{3,2},{4,5},{5,4},{6,7},{7,6},{8,9},{9,8},{10,11... | collective-permute-start | bytes 296 | tf_op jit(solution)/shard_map/ppermute | solution.py:423
  9.4 26.8 %copy-start.2 = (s32[1,24]{1,0:T(1,128)S(1)}, s32[1,24]{1,0:T(1,128)}, u32[]{:S(2)}) copy-start(s32[1,24]{1,0:T(1,128)} %all_cols.5) | copy-start | bytes 292
  9.4 26.8 %copy-start.3 = (s32[1,24]{1,0:T(1,128)S(1)}, s32[1,24]{1,0:T(1,128)}, u32[]{:S(2)}) copy-start(s32[1,24]{1,0:T(1,128)} %owners.1) | copy-start | bytes 292
  9.4 12.8 %collective-permute-start.2 = (bf16[4,12,16,128]{3,2,1,0:T(8,128)(2,1)S(1)}, bf16[4,12,16,128]{3,2,1,0:T(8,128)(2,1)S(1)}, u32[]{:S(2)}, u32[]{:S(2)}) collective-permute-start(bf16[4,12,16,128]{3,2,1,0:T(8,128)(2,1)S(1)} %get-tuple-element.32), channel_id=1, source_target_pairs={{0,8},{4,12},{8,0},{12,4},{16,24},{20,28},{24,16},{28,20},{1,9},{5... | collective-permute-start | bytes 589832 | tf_op jit(solution)/shard_map/ppermute | solution.py:426
  11.0 4.2 %collective-permute-start.7 = (s32[1,24]{1,0:T(1,128)S(1)}, s32[1,24]{1,0:T(1,128)S(1)}, u32[]{:S(2)}, u32[]{:S(2)}) collective-permute-start(s32[1,24]{1,0:T(1,128)S(1)} %copy-done.1), channel_id=1, source_target_pairs={{0,2},{1,3},{2,0},{3,1},{4,6},{5,7},{6,4},{7,5},{8,10},{9,11},{10,... | collective-permute-start | bytes 296 | tf_op jit(solution)/shard_map/ppermute | solution.py:423
  15.2 1.2 %collective-permute-start.8 = (s32[1,24]{1,0:T(1,128)S(1)}, s32[1,24]{1,0:T(1,128)S(1)}, u32[]{:S(2)}, u32[]{:S(2)}) collective-permute-start(s32[1,24]{1,0:T(1,128)S(1)} %collective-permute-done.7.came2), channel_id=1, source_target_pairs={{0,1},{1,0},{2,3},{3,2},{4,5},{5,4},{6,7},{7,6},{8,9},{9,8},{10,11... | collective-permute-start | bytes 296 | tf_op jit(solution)/shard_map/ppermute | solution.py:423
  18.7 27.1 %collective-permute-start.13 = (bf16[6,256,128]{2,1,0:T(8,128)(2,1)S(1)}, bf16[6,256,128]{2,1,0:T(8,128)(2,1)S(1)}, u32[]{:S(2)}, u32[]{:S(2)}) collective-permute-start(bf16[6,256,128]{2,1,0:T(8,128)(2,1)S(1)} %get-tuple-element.48), channel_id=1, source_target_pairs={{0,3},{1,2},{2,1},{3,0},{4,7},{5,6},{6,5},{7,4},{8,11},{9,10},{10,... | collective-permute-start | bytes 1179656 | tf_op jit(solution)/shard_map/ppermute | solution.py:423
  20.6 5.7 %collective-permute-start.9 = (bf16[4,6,16,128]{3,2,1,0:T(8,128)(2,1)S(1)}, bf16[4,6,16,128]{3,2,1,0:T(8,128)(2,1)S(1)}, u32[]{:S(2)}, u32[]{:S(2)}) collective-permute-start(bf16[4,6,16,128]{3,2,1,0:T(8,128)(2,1)S(1)} %get-tuple-element.42), channel_id=1, source_target_pairs={{0,4},{4,0},{8,12},{12,8},{16,20},{20,16},{24,28},{28,24},{1,5},{5... | collective-permute-start | bytes 294920 | tf_op jit(solution)/shard_map/ppermute | solution.py:426
  22.2 5.8 %collective-permute-start.3 = (bf16[2,12,16,128]{3,2,1,0:T(8,128)(2,1)S(1)}, bf16[2,12,16,128]{3,2,1,0:T(8,128)(2,1)S(1)}, u32[]{:S(2)}, u32[]{:S(2)}) collective-permute-start(bf16[2,12,16,128]{3,2,1,0:T(8,128)(2,1)S(1)} %get-tuple-element.34), channel_id=1, source_target_pairs={{0,4},{4,0},{8,12},{12,8},{16,20},{20,16},{24,28},{28,24},{1,5},{5... | collective-permute-start | bytes 294920 | tf_op jit(solution)/shard_map/ppermute | solution.py:426
  26.4 4.3 %collective-permute-start.10 = (bf16[2,6,16,128]{3,2,1,0:T(8,128)(2,1)S(1)}, bf16[2,6,16,128]{3,2,1,0:T(8,128)(2,1)S(1)}, u32[]{:S(2)}, u32[]{:S(2)}) collective-permute-start(bf16[2,6,16,128]{3,2,1,0:T(8,128)(2,1)S(1)} %get-tuple-element.44), channel_id=1, source_target_pairs={{0,8},{4,12},{8,0},{12,4},{16,24},{20,28},{24,16},{28,20},{1,9},{5... | collective-permute-start | bytes 147464 | tf_op jit(solution)/shard_map/ppermute | solution.py:426
  28.0 8.1 %collective-permute-start.4 = (bf16[1,12,16,128]{3,2,1,0:T(8,128)(2,1)S(1)}, bf16[1,12,16,128]{3,2,1,0:T(8,128)(2,1)S(1)}, u32[]{:S(2)}, u32[]{:S(2)}) collective-permute-start(bf16[1,12,16,128]{3,2,1,0:T(8,128)(2,1)S(1)} %get-tuple-element.36), channel_id=1, source_target_pairs={{0,16},{4,20},{8,24},{12,28},{16,0},{20,4},{24,8},{28,12},{1,17},{... | collective-permute-start | bytes 147464 | tf_op jit(solution)/shard_map/ppermute | solution.py:426
  30.7 4.8 %collective-permute-start.11 = (bf16[1,6,16,128]{3,2,1,0:T(8,128)(2,1)S(1)}, bf16[1,6,16,128]{3,2,1,0:T(8,128)(2,1)S(1)}, u32[]{:S(2)}, u32[]{:S(2)}) collective-permute-start(bf16[1,6,16,128]{3,2,1,0:T(8,128)(2,1)S(1)} %get-tuple-element.46), channel_id=1, source_target_pairs={{0,16},{4,20},{8,24},{12,28},{16,0},{20,4},{24,8},{28,12},{1,17},{... | collective-permute-start | bytes 73736 | tf_op jit(solution)/shard_map/ppermute | solution.py:426
  35.5 3.9 %collective-permute-start.12 = (bf16[6,16,128]{2,1,0:T(8,128)(2,1)S(1)}, bf16[6,16,128]{2,1,0:T(8,128)(2,1)S(1)}, u32[]{:S(2)}, u32[]{:S(2)}) collective-permute-start(bf16[6,16,128]{2,1,0:T(8,128)(2,1)S(1)} %shard_map.61), channel_id=1, source_target_pairs={{0,2},{1,3},{2,0},{3,1},{4,6},{5,7},{6,4},{7,5},{8,10},{9,11},{10,... | collective-permute-start | bytes 73736 | tf_op jit(solution)/shard_map/ppermute | solution.py:423
  36.1 3.3 %collective-permute-start.5 = (bf16[6,16,128]{2,1,0:T(8,128)(2,1)S(1)}, bf16[6,16,128]{2,1,0:T(8,128)(2,1)S(1)}, u32[]{:S(2)}, u32[]{:S(2)}) collective-permute-start(bf16[6,16,128]{2,1,0:T(8,128)(2,1)S(1)} %get-tuple-element.38), channel_id=1, source_target_pairs={{0,1},{1,0},{2,3},{3,2},{4,5},{5,4},{6,7},{7,6},{8,9},{9,8},{10,11... | collective-permute-start | bytes 73736 | tf_op jit(solution)/shard_map/ppermute | solution.py:423
  40.2 27.7 %all-to-all-start = ((bf16[8,8,16,128]{3,2,1,0:T(8,128)(2,1)}), bf16[8,8,16,128]{3,2,1,0:T(8,128)(2,1)S(1)}, u32[]{:S(2)}, u32[]{:S(2)}) async-start(bf16[8,8,16,128]{3,2,1,0:T(8,128)(2,1)} %settle.1), calls=%async_computation | async-start | bytes 524288 | tf_op jit(solution)/shard_map/all_to_all | solution.py:463
  46.2 5.9 %collective-permute-start.14 = (bf16[6,64,128]{2,1,0:T(8,128)(2,1)S(1)}, bf16[6,64,128]{2,1,0:T(8,128)(2,1)S(1)}, u32[]{:S(2)}, u32[]{:S(2)}) collective-permute-start(bf16[6,64,128]{2,1,0:T(8,128)(2,1)S(1)} %get-tuple-element.50), channel_id=1, source_target_pairs={{0,4},{4,0},{8,12},{12,8},{16,20},{20,16},{24,28},{28,24},{1,5},{5... | collective-permute-start | bytes 294920 | tf_op jit(solution)/shard_map/ppermute | solution.py:426
  52.1 5.1 %collective-permute-start.15 = (bf16[6,64,128]{2,1,0:T(8,128)(2,1)S(1)}, bf16[6,64,128]{2,1,0:T(8,128)(2,1)S(1)}, u32[]{:S(2)}, u32[]{:S(2)}) collective-permute-start(bf16[6,64,128]{2,1,0:T(8,128)(2,1)S(1)} %get-tuple-element.52), channel_id=1, source_target_pairs={{0,8},{4,12},{8,0},{12,4},{16,24},{20,28},{24,16},{28,20},{1,9},{5... | collective-permute-start | bytes 294920 | tf_op jit(solution)/shard_map/ppermute | solution.py:426
  57.2 5.6 %collective-permute-start.16 = (bf16[6,64,128]{2,1,0:T(8,128)(2,1)S(1)}, bf16[6,64,128]{2,1,0:T(8,128)(2,1)S(1)}, u32[]{:S(2)}, u32[]{:S(2)}) collective-permute-start(bf16[6,64,128]{2,1,0:T(8,128)(2,1)S(1)} %get-tuple-element.54), channel_id=1, source_target_pairs={{0,16},{4,20},{8,24},{12,28},{16,0},{20,4},{24,8},{28,12},{1,17},{... | collective-permute-start | bytes 294920 | tf_op jit(solution)/shard_map/ppermute | solution.py:426
  62.8 5.0 %collective-permute-start.17 = (bf16[6,64,128]{2,1,0:T(8,128)(2,1)S(1)}, bf16[6,64,128]{2,1,0:T(8,128)(2,1)S(1)}, u32[]{:S(2)}, u32[]{:S(2)}) collective-permute-start(bf16[6,64,128]{2,1,0:T(8,128)(2,1)S(1)} %shard_map.64.mine), channel_id=1, source_target_pairs={{0,4},{4,0},{8,12},{12,8},{16,20},{20,16},{24,28},{28,24},{1,5},{5... | collective-permute-start | bytes 294920 | tf_op jit(solution)/shard_map/ppermute | solution.py:461

commit v6 on v5

--- a/solution.py
+++ b/solution.py
@@ -69,64 +69,23 @@
         found += hit.astype(jnp.int32)
 
 
-def split_pieces(order, parts, kept, sent):
-    me = lax.axis_index("seq")
-    width = len(order) - 1
-    for index in range(kept.shape[0]):
-        apart = sum(((index >> (width - 1 - bit)) & 1) * order[bit + 1] for bit in range(width))
-        kept[index] = parts[me ^ apart]
-        sent[index] = parts[me ^ apart ^ order[0]].astype(jnp.bfloat16)
-
-
-def halve_kernel(*refs):
-    parts, (still, sent) = refs[:-2], refs[-2:]
-    half = still.shape[0]
-    first = 0
-    for kept, received in zip(parts[0::2], parts[1::2]):
-        items = pl.ds(first, kept.shape[1])
-        still[:, items] = kept[:half] + received[:half].astype(jnp.float32)
-        sent[:, items] = (kept[half:] + received[half:].astype(jnp.float32)).astype(jnp.bfloat16)
-        first += kept.shape[1]
-
-
-def halve(parts):
-    half, _, rows, _ = parts[0][0].shape
-    shape = (half // 2, sum(kept.shape[1] for kept, _ in parts), rows, BLOCK)
-    return pl.pallas_call(
-        halve_kernel,
-        out_shape=[pltpu.VMEM(shape, jnp.float32), pltpu.VMEM(shape, jnp.bfloat16)],
-        in_specs=[VMEM] * (2 * len(parts)),
-        out_specs=[VMEM, VMEM],
-        compiler_params=SMALL,
-    )(*[vectors(value) for part in parts for value in part])
-
-
-def finish_kernel(kept, received, *outs):
-    first = 0
-    for out in outs:
-        items = pl.ds(first, out.shape[0])
-        out[...] = (kept[0, items] + received[0, items].astype(jnp.float32)).astype(jnp.bfloat16)
-        first += out.shape[0]
-
-
-def finish(kept, received, counts):
-    return pl.pallas_call(
-        finish_kernel,
-        out_shape=[pltpu.VMEM((count,) + kept.shape[2:], jnp.bfloat16) for count in counts],
-        in_specs=[VMEM, VMEM],
-        out_specs=[VMEM] * len(counts),
-        compiler_params=SMALL,
-    )(vectors(kept), vectors(received))
-
-
-def halved_shapes(pieces, items):
-    shape = (pieces // 2, items, BLOCK // pieces, BLOCK)
+def multiply(left, right):
+    return lax.dot_general(left, right, (((0,), (0,)), ((), ())), preferred_element_type=jnp.float32)
+
+
+def my_half(other=0):
+    half = BLOCK // 2
+    return pl.ds(pl.multiple_of(((lax.axis_index("seq") & 1) ^ other) * half, half), half)
+
+
+def split_rows(whole, kept, sent):
+    kept[...] = whole[:, my_half()]
+    sent[...] = whole[:, my_half(1)].astype(jnp.bfloat16)
+
+
+def row_halves(items):
+    shape = (items, BLOCK // 2, BLOCK)
     return [pltpu.VMEM(shape, jnp.float32), pltpu.VMEM(shape, jnp.bfloat16)]
-
-
-def multiply(pieces, left, right):
-    product = lax.dot_general(left, right, (((0,), (0,)), ((), ())), preferred_element_type=jnp.float32)
-    return product.reshape(pieces, BLOCK // pieces, BLOCK)
 
 
 def fetch(pairs, sems):
@@ -173,7 +132,7 @@
     )(in_hbm(rows), in_hbm(cols), in_hbm(hidden))
 
 
-def near_kernel(order, cols_per, per_peer, pieces, all_rows, all_cols, came1, hidden, grad_out, arrived, kept, sent, own, right, parts, rows, cols, list1, table, list_sems, sems):
+def near_kernel(cols_per, per_peer, all_rows, all_cols, came1, hidden, grad_out, arrived, kept, sent, own, right, whole, rows, cols, list1, table, list_sems, sems):
     me = lax.axis_index("tensor")
     for copy in fetch(((all_rows, rows), (all_cols, cols), (came1, list1)), list_sems):
         copy.wait()
@@ -187,21 +146,21 @@
         copy.wait()
     for item in range(2 * per_peer):
         left = own[item] if item < per_peer else arrived[item - per_peer]
-        parts[:, item] = multiply(pieces, left, right[item])
-    split_pieces(order, parts, kept, sent)
-
-
-def near_products(rows, cols, list1, hidden, grad_out, arrived, per_peer, pieces, order):
+        whole[item] = multiply(left, right[item])
+    split_rows(whole, kept, sent)
+
+
+def near_products(rows, cols, list1, hidden, grad_out, arrived, per_peer):
     tok_rows, width = grad_out.shape
     return pl.pallas_call(
-        functools.partial(near_kernel, order, width // BLOCK, per_peer, pieces),
-        out_shape=halved_shapes(pieces, 2 * per_peer),
+        functools.partial(near_kernel, width // BLOCK, per_peer),
+        out_shape=row_halves(2 * per_peer),
         in_specs=[HBM, HBM, VMEM, HBM, HBM, VMEM],
         out_specs=[VMEM, VMEM],
         scratch_shapes=[
             pltpu.VMEM((per_peer, tok_rows, BLOCK), jnp.bfloat16),
             pltpu.VMEM((2 * per_peer, tok_rows, BLOCK), jnp.bfloat16),
-            pltpu.VMEM((pieces, 2 * per_peer, BLOCK // pieces, BLOCK), jnp.float32),
+            pltpu.VMEM((2 * per_peer, BLOCK, BLOCK), jnp.float32),
             pltpu.SMEM(rows.shape, jnp.int32),
             pltpu.SMEM(cols.shape, jnp.int32),
             pltpu.SMEM(list1.shape, jnp.int32),
@@ -246,50 +205,64 @@
     )(in_hbm(rows), in_hbm(cols), vectors(list2), vectors(list3), in_hbm(hidden), in_hbm(grad_out))
 
 
-def cross_kernel(order, pieces, left, right, kept, sent, parts):
+def cross_kernel(left, right, kept, sent, whole):
     for j in range(left.shape[0]):
-        parts[:, j] = multiply(pieces, left[j], right[j])
-    split_pieces(order, parts, kept, sent)
-
-
-def cross_products(left, right, pieces, order):
+        whole[j] = multiply(left[j], right[j])
+    split_rows(whole, kept, sent)
+
+
+def cross_products(left, right):
     count = left.shape[0]
     return pl.pallas_call(
-        functools.partial(cross_kernel, order, pieces),
-        out_shape=halved_shapes(pieces, count),
-        in_specs=[VMEM, VMEM],
-        out_specs=[VMEM, VMEM],
-        scratch_shapes=[pltpu.VMEM((pieces, count, BLOCK // pieces, BLOCK), jnp.float32)],
+        cross_kernel,
+        out_shape=row_halves(count),
+        in_specs=[VMEM, VMEM],
+        out_specs=[VMEM, VMEM],
+        scratch_shapes=[pltpu.VMEM((count, BLOCK, BLOCK), jnp.float32)],
         compiler_params=SMALL,
     )(vectors(left), vectors(right))
 
 
-def my_half(first=0):
-    half = BLOCK // 2
-    return pl.ds(pl.multiple_of(((lax.axis_index("seq") & 1) ^ first) * half, half), half)
-
-
-def far_kernel(left, arrived, kept, sent, whole):
-    for j in range(arrived.shape[0]):
-        whole[j] = lax.dot_general(
-            left[j], arrived[j], (((0,), (0,)), ((), ())), preferred_element_type=jnp.float32
-        )
-    kept[...] = whole[:, my_half()]
-    sent[...] = whole[:, my_half(1)].astype(jnp.bfloat16)
-
-
-def far_products(left, arrived):
-    count = arrived.shape[0]
-    half = (count, BLOCK // 2, BLOCK)
-    return pl.pallas_call(
-        far_kernel,
-        out_shape=[pltpu.VMEM(half, jnp.float32), pltpu.VMEM(half, jnp.bfloat16)],
-        in_specs=[VMEM, VMEM],
-        out_specs=[VMEM, VMEM],
-        scratch_shapes=[pltpu.VMEM((count, BLOCK, BLOCK), jnp.float32)],
-        name="far_products",
-        compiler_params=SMALL,
-    )(vectors(left), vectors(arrived))
+def my_quarter(other=0):
+    quarter = BLOCK // 4
+    bit = lax.shift_right_logical(lax.axis_index("seq"), 1) & 1
+    return pl.ds(pl.multiple_of((bit ^ other) * quarter, quarter), quarter)
+
+
+def quarter_kernel(kept, received, still, sent):
+    still[...] = kept[:, my_quarter()] + received[:, my_quarter()].astype(jnp.float32)
+    total = kept[:, my_quarter(1)] + received[:, my_quarter(1)].astype(jnp.float32)
+    sent[...] = total.astype(jnp.bfloat16)
+
+
+def quarter(kept, received):
+    shape = (kept.shape[0], BLOCK // 4, BLOCK)
+    return pl.pallas_call(
+        quarter_kernel,
+        out_shape=[pltpu.VMEM(shape, jnp.float32), pltpu.VMEM(shape, jnp.bfloat16)],
+        in_specs=[VMEM, VMEM],
+        out_specs=[VMEM, VMEM],
+        compiler_params=SMALL,
+    )(vectors(kept), vectors(received))
+
+
+def join_kernel(mine, other, *outs):
+    first = 0
+    for out in outs:
+        items = pl.ds(first, out.shape[0])
+        out[:, my_quarter()] = mine[items]
+        out[:, my_quarter(1)] = other[items]
+        first += out.shape[0]
+
+
+def join(mine, other, counts):
+    return pl.pallas_call(
+        join_kernel,
+        out_shape=[pltpu.VMEM((count, BLOCK // 2, BLOCK), jnp.bfloat16) for count in counts],
+        in_specs=[VMEM, VMEM],
+        out_specs=[VMEM] * len(counts),
+        compiler_params=SMALL,
+    )(vectors(mine), vectors(other))
 
 
 def share_kernel(kept, received, still, sent):
@@ -308,41 +281,22 @@
     )(vectors(kept), vectors(received))
 
 
-def share_last_kernel(kept, received, sent):
-    sent[...] = (kept[...] + received[...].astype(jnp.float32)).astype(jnp.bfloat16)
-
-
-def share_last(kept, received):
-    return pl.pallas_call(
-        share_last_kernel,
-        out_shape=pltpu.VMEM(kept.shape, jnp.bfloat16),
-        in_specs=[VMEM, VMEM],
-        out_specs=VMEM,
+def finish_kernel(kept, received, *outs):
+    first = 0
+    for out in outs:
+        items = pl.ds(first, out.shape[0])
+        out[...] = (kept[items] + received[items].astype(jnp.float32)).astype(jnp.bfloat16)
+        first += out.shape[0]
+
+
+def finish(kept, received, counts):
+    return pl.pallas_call(
+        finish_kernel,
+        out_shape=[pltpu.VMEM((count,) + kept.shape[1:], jnp.bfloat16) for count in counts],
+        in_specs=[VMEM, VMEM],
+        out_specs=[VMEM] * len(counts),
         compiler_params=SMALL,
     )(vectors(kept), vectors(received))
-
-
-def compose_kernel(delivered, mine, other, owned, out):
-    far_items, rows = mine.shape[0], BLOCK // 2
-    for slot in range(out.shape[0]):
-        out[slot] = delivered[:, slot].reshape(BLOCK, BLOCK)
-        for half, source in ((my_half(), mine), (my_half(1), other)):
-            value = out[slot, half].astype(jnp.float32)
-            for j in range(far_items):
-                flag = jnp.concatenate([owned[slot * far_items + j]] * (rows // 8))
-                value = jnp.where(flag > 0, source[j].astype(jnp.float32), value)
-            out[slot, half] = value.astype(jnp.bfloat16)
-
-
-def compose(delivered, mine, other, owned):
-    return pl.pallas_call(
-        compose_kernel,
-        out_shape=jax.ShapeDtypeStruct((delivered.shape[1], BLOCK, BLOCK), jnp.bfloat16),
-        in_specs=[VMEM] * 4,
-        out_specs=VMEM,
-        name="compose",
-        compiler_params=SMALL,
-    )(vectors(delivered), vectors(mine), vectors(other), vectors(owned))
 
 
 def plan_kernel(cols_per, per_peer, cols, owners, places, seen):
@@ -372,46 +326,52 @@
     )(scalars(cols), scalars(owners))
 
 
-def flag_kernel(per_peer, places, owned):
-    first = lax.axis_index("seq") * CAP
-    owned[...] = jnp.zeros_like(owned)
-    for rank in range(per_peer):
-        slot = places[3 * per_peer + rank] - first
-        mine = jnp.logical_and(slot >= 0, slot < CAP)
-        owned[jnp.where(mine, slot * per_peer + rank, CAP * per_peer)] = jnp.ones(owned.shape[1:], jnp.float32)
-
-
-def flag_owned(places, per_peer):
-    return pl.pallas_call(
-        functools.partial(flag_kernel, per_peer),
-        out_shape=pltpu.VMEM((CAP * per_peer + 1, 8, BLOCK), jnp.float32),
-        in_specs=[SMEM],
+def settle_kernel(places, own, core, guests, kept, received, mine, sent):
+    me = lax.axis_index("seq")
+    mine[...] = jnp.zeros_like(mine)
+    sent[...] = jnp.zeros_like(sent)
+    spare = mine.shape[0] - 1
+    first = 0
+    for source in (own, core, guests, None):
+        for j in range(guests.shape[0]):
+            place = places[first + j]
+            owner, slot = lax.shift_right_logical(place, CAP.bit_length() - 1), place & (CAP - 1)
+            if source is None:
+                value = (kept[j] + received[j].astype(jnp.float32)).astype(jnp.bfloat16)
+            else:
+                value = source[j]
+            mine[jnp.where(owner == me, slot, spare)] = value
+            sent[jnp.where(owner == (me ^ 1), slot, spare)] = value
+        first += guests.shape[0]
+
+
+def settle(places, own, core, guests, kept, received):
+    _, rows, _ = guests.shape
+    return pl.pallas_call(
+        settle_kernel,
+        out_shape=[pltpu.VMEM((CAP + 1, rows, BLOCK), jnp.bfloat16)] * 2,
+        in_specs=[SMEM] + [VMEM] * 5,
+        out_specs=[VMEM, VMEM],
+        name="settle",
+        compiler_params=SMALL,
+    )(scalars(places), vectors(own), vectors(core), vectors(guests), vectors(kept), vectors(received))
+
+
+def compose_kernel(mine, other, out):
+    for slot in range(out.shape[0]):
+        out[slot, my_half()] = mine[slot]
+        out[slot, my_half(1)] = other[slot]
+
+
+def compose(mine, other):
+    return pl.pallas_call(
+        compose_kernel,
+        out_shape=jax.ShapeDtypeStruct((CAP, BLOCK, BLOCK), jnp.bfloat16),
+        in_specs=[VMEM, VMEM],
         out_specs=VMEM,
-        name="flag_owned",
-        compiler_params=SMALL,
-    )(scalars(places))
-
-
-def settle_kernel(places, own, core, guests, out):
-    out[...] = jnp.zeros_like(out)
-    first = 0
-    for source in (own, core, guests):
-        for j in range(source.shape[0]):
-            place = places[first + j]
-            out[lax.shift_right_logical(place, CAP.bit_length() - 1), place & (CAP - 1)] = source[j]
-        first += source.shape[0]
-
-
-def settle(places, own, core, guests, pieces):
-    _, rows, _ = guests.shape
-    return pl.pallas_call(
-        settle_kernel,
-        out_shape=pltpu.VMEM((pieces, CAP, rows, BLOCK), jnp.bfloat16),
-        in_specs=[SMEM] + [VMEM] * 3,
-        out_specs=VMEM,
-        name="settle",
-        compiler_params=SMALL,
-    )(scalars(places), vectors(own), vectors(core), vectors(guests))
+        name="compose",
+        compiler_params=SMALL,
+    )(vectors(mine), vectors(other))
 
 
 def sparse_on_device(hidden, grad_out, block_rows, block_cols, block_owner):
@@ -425,43 +385,44 @@
     def exchange(sent, distance):
         return lax.ppermute(sent, "seq", [(i, i ^ distance) for i in range(seq_count)])
 
-    def reduce_pieces(order, kept, sent, counts):
+    def sum_over_seq(order, kept, sent):
         for step, distance in enumerate(order):
             received = exchange(sent, distance)
             if step == len(order) - 1:
-                return finish(kept, received, counts)
-            kept, sent = halve([(kept, received)])
-
-    near_order, guest_order = (2, 1, 4), (1, 2, 4)
+                return kept, received
+            kept, sent = share(kept, received)
+
+    cross_order = (1, 2, 4)
     for_cross, for_core = push_blocks(block_rows, block_cols, hidden, cols_per, per_peer)
     list2 = to_peer(block_cols, 2)
     guests = to_peer(for_cross, 2)
     from_core = to_peer(for_core, 1)
     list1 = to_peer(block_cols, 1)
     near_kept, near_sent = near_products(
-        block_rows, block_cols, list1, hidden, grad_out, from_core, per_peer, seq_count, near_order
+        block_rows, block_cols, list1, hidden, grad_out, from_core, per_peer
     )
     list3 = to_peer(list2, 1)
-    own_sum, core_sum = reduce_pieces(near_order, near_kept, near_sent, (per_peer, per_peer))
+    near_came = exchange(near_sent, 1)
+    near_kept, near_sent = quarter(near_kept, near_came)
+    near_came = exchange(near_sent, 2)
+    near_kept, near_sent = share(near_kept, near_came)
+    near_came = exchange(near_sent, 4)
+    (near_mine,) = finish(near_kept, near_came, (2 * per_peer,))
+    near_other = exchange(near_mine, 2)
+    own_sum, core_sum = join(near_mine, near_other, (per_peer, per_peer))
     core_back = to_peer(core_sum, 1)
     for_far, for_guests, hidden_far = pack_blocks(block_rows, block_cols, list2, list3, hidden, grad_out, per_peer)
     from_far = to_peer(for_far, 3)
     places = plan(block_cols, block_owner, cols_per, per_peer)
-    owned = flag_owned(places, per_peer)
-    guest_kept, guest_sent = cross_products(guests, for_guests, seq_count, guest_order)
-    (guest_sum,) = reduce_pieces(guest_order, guest_kept, guest_sent, (per_peer,))
+    guest_kept, guest_sent = cross_products(guests, for_guests)
+    guest_kept, guest_came = sum_over_seq(cross_order, guest_kept, guest_sent)
+    (guest_sum,) = finish(guest_kept, guest_came, (per_peer,))
     guest_back = to_peer(guest_sum, 2)
-    kept, sent = far_products(hidden_far, from_far)
-    for distance in guest_order:
-        received = exchange(sent, distance)
-        if distance == guest_order[-1]:
-            sent = share_last(kept, received)
-        else:
-            kept, sent = share(kept, received)
-    other = lax.ppermute(sent, "seq", [(i, i ^ 1) for i in range(seq_count)])
-    placed = settle(places, own_sum, core_back, guest_back, seq_count)
-    delivered = lax.all_to_all(placed, "seq", split_axis=0, concat_axis=0, tiled=True)
-    return compose(delivered, sent, other, owned)[None]
+    far_kept, far_sent = cross_products(hidden_far, from_far)
+    far_kept, far_came = sum_over_seq(cross_order, far_kept, far_sent)
+    mine, sent = settle(places, own_sum, core_back, guest_back, far_kept, far_came)
+    other = exchange(sent, 1)
+    return compose(mine, other)[None]
 
 
 def solution(mesh):

time: 69.3 us -> 61.7 us (0.89)
  starting transfers between devices: 31.9 us -> 26.9 us
  waiting for transfers between devices: 26.1 us -> 24.4 us
  Pallas kernels: 10.7 us -> 9.85 us
    all_to_all x1 -> x0, starting transfers between devices: 5.64 us -> none  [sparse_on_device(): lax.all_to_all(placed, 'seq', split_axis=0, concat_axis=0, tiled=True)]
    ppermute x8, waiting for transfers between devices: 8.34 us -> 12.8 us  [to_peer(): lax.ppermute(value, 'tensor', [(i, i ^ distance) for i in range(tensor_co...]
    ppermute x9 -> x11, waiting for transfers between devices: 15.2 us -> 11.6 us  [exchange(): lax.ppermute(sent, 'seq', [(i, i ^ distance) for i in range(seq_count)])]
    ppermute x9 -> x11, starting transfers between devices: 17.8 us -> 21.2 us  [exchange(): lax.ppermute(sent, 'seq', [(i, i ^ distance) for i in range(seq_count)])]
    ppermute x1 -> x0, waiting for transfers between devices: 2.57 us -> none  [sparse_on_device(): other = lax.ppermute(sent, 'seq', [(i, i ^ 1) for i in range(seq_count)])]
    ppermute x1 -> x0, starting transfers between devices: 2.45 us -> none  [sparse_on_device(): other = lax.ppermute(sent, 'seq', [(i, i ^ 1) for i in range(seq_count)])]
    pallas_call x11 -> x7, Pallas kernels: 5.38 us -> 4.39 us  [the longest x1 2.79 us: near_products(): pl.pallas_call(functools.partial(near_kernel, width // BLOCK, per_peer),...]
  transfers between devices with their start and end apart: 19 -> 19, of which waited for: 10 -> 8; matrix products, arithmetic and copies ran while one was open for 0% -> 0% of each run, Pallas kernels for 11% -> 11%
where the time goes in v6:
time: 61.7 us; the launch traced here: 61.3 us
  starting transfers between devices  26.9 us (44%)
  waiting for transfers between devices  24.4 us (40%)
  Pallas kernels  9.85 us (16%)
    ppermute x11, starting transfers between devices, exchange(): lax.ppermute(sent, 'seq', [(i, i ^ distance) for i in range(seq_count)])  21.2 us
    ppermute x8, waiting for transfers between devices, to_peer(): lax.ppermute(value, 'tensor', [(i, i ^ distance) for i in range(tensor_co...  12.8 us
    ppermute x11, waiting for transfers between devices, exchange(): lax.ppermute(sent, 'seq', [(i, i ^ distance) for i in range(seq_count)])  11.6 us
    ppermute x8, starting transfers between devices, to_peer(): lax.ppermute(value, 'tensor', [(i, i ^ distance) for i in range(tensor_co...  5.73 us
    pallas_call x1, Pallas kernels, near_products(): pl.pallas_call(functools.partial(near_kernel, width // BLOCK, per_peer),...  2.79 us
    pallas_call x1, Pallas kernels, pack_blocks(): pl.pallas_call(functools.partial(pack_kernel, width // BLOCK, per_peer),...  2.34 us
    pallas_call x1, Pallas kernels, push_blocks(): pl.pallas_call(functools.partial(push_kernel, cols_per, per_peer), out_sh...  2.25 us
  transfers between devices with their start and end apart: 19, of which 8 were waited for; matrix products, arithmetic and copies ran while one was open for 0% of the time, Pallas kernels for 11%

profile of v6, /device:TPU:0, one launch (start us, length us, event | category | flops | bytes accessed | tf_op | source)
XLA Modules:
  0.0 61.3 jit_solution(8365815693014100532)
XLA Ops:
  0.0 2.2 %push_blocks.1 = (bf16[6,256,128]{2,1,0:T(8,128)(2,1)S(1)}, bf16[6,256,128]{2,1,0:T(8,128)(2,1)S(1)}) custom-call(s32[1,24]{1,0:T(1,128)} %all_rows.5, s32[1,24]{1,0:T(1,128)} %all_cols.5, bf16[256,13312]{1,0:T(8,128)(2,1)} %hidden.5), custom_call_target="tpu_custom_call" | custom-call | tf_op jit(solution)/shard_map/push_blocks/pallas_call | solution.py:118
  2.3 0.6 collective-permute-start.1
  2.8 2.6 %collective-permute-start.7 = (bf16[6,256,128]{2,1,0:T(8,128)(2,1)S(1)}, bf16[6,256,128]{2,1,0:T(8,128)(2,1)S(1)}, u32[]{:S(2)}, u32[]{:S(2)}) collective-permute-start(bf16[6,256,128]{2,1,0:T(8,128)(2,1)S(1)} %get-tuple-element.41), channel_id=1, source_target_pairs={{0,2},{1,3},{2,0},{3,1},{4,6},{5,7},{6,4},{7,5},{8,10},{9,11},{10,... | collective-permute-start | bytes 1179656 | tf_op jit(solution)/shard_map/ppermute | solution.py:383
  5.4 0.1 collective-permute-start.8
  5.5 9.7 %collective-permute-done.8.came2 = s32[1,24]{1,0:T(1,128)S(1)} collective-permute-done((s32[1,24]{1,0:T(1,128)S(1)}, s32[1,24]{1,0:T(1,128)S(1)}, u32[]{:S(2)}, u32[]{:S(2)}) %collective-permute-start.8) | collective-permute-done | bytes 128 | tf_op jit(solution)/shard_map/ppermute | solution.py:383
  15.2 0.0 collective-permute-start.9
  15.2 1.2 %collective-permute-done.9.came3 = s32[1,24]{1,0:T(1,128)S(1)} collective-permute-done((s32[1,24]{1,0:T(1,128)S(1)}, s32[1,24]{1,0:T(1,128)S(1)}, u32[]{:S(2)}, u32[]{:S(2)}) %collective-permute-start.9) | collective-permute-done | bytes 128 | tf_op jit(solution)/shard_map/ppermute | solution.py:383
  16.4 2.3 %pack_blocks.1 = (bf16[6,256,128]{2,1,0:T(8,128)(2,1)S(1)}, bf16[6,256,128]{2,1,0:T(8,128)(2,1)S(1)}, bf16[6,256,128]{2,1,0:T(8,128)(2,1)S(1)}) custom-call(s32[1,24]{1,0:T(1,128)} %all_rows.5, s32[1,24]{1,0:T(1,128)} %all_cols.5, s32[1,24]{1,0:T(1,128)S(1)} %collective-permute-done.8.came2, s32[1,24]{1,0:T(1,128)S(1)} %collective-permute-done.9.came3, ...), custom_call_target="tpu_custom_call" | custom-call | tf_op jit(solution)/shard_map/pack_blocks/pallas_call | solution.py:192
  18.7 0.0 copy-start.2
  18.7 0.0 copy-start.3
  18.7 1.6 %collective-permute-start.14 = (bf16[6,256,128]{2,1,0:T(8,128)(2,1)S(1)}, bf16[6,256,128]{2,1,0:T(8,128)(2,1)S(1)}, u32[]{:S(2)}, u32[]{:S(2)}) collective-permute-start(bf16[6,256,128]{2,1,0:T(8,128)(2,1)S(1)} %get-tuple-element.50), channel_id=1, source_target_pairs={{0,3},{1,2},{2,1},{3,0},{4,7},{5,6},{6,5},{7,4},{8,11},{9,10},{10,... | collective-permute-start | bytes 1179656 | tf_op jit(solution)/shard_map/ppermute | solution.py:383
  20.3 0.3 collective-permute-start
  20.6 0.8 %collective-permute-done.came1 = s32[1,24]{1,0:T(1,128)S(1)} collective-permute-done((s32[1,24]{1,0:T(1,128)S(1)}, s32[1,24]{1,0:T(1,128)S(1)}, u32[]{:S(2)}, u32[]{:S(2)}) %collective-permute-start) | collective-permute-done | bytes 128 | tf_op jit(solution)/shard_map/ppermute | solution.py:383
  21.5 0.0 collective-permute-done.1.arrived
  21.5 2.8 %near_products.1 = (f32[12,64,128]{2,1,0:T(8,128)S(1)}, bf16[12,64,128]{2,1,0:T(8,128)(2,1)S(1)}) custom-call(s32[1,24]{1,0:T(1,128)} %all_rows.5, s32[1,24]{1,0:T(1,128)} %all_cols.5, s32[1,24]{1,0:T(1,128)S(1)} %collective-permute-done.came1, bf16[256,13312]{1,0:T(8,128)(2,1)} %hidden.5, bf16[256,4096]{1,0:T(8,128)(2,1)} %grad_out.3, ...), custom_call_target="tpu_custom_call" | custom-call | tf_op jit(solution)/shard_map/near_products/pallas_call | solution.py:155
  24.3 1.6 %collective-permute-start.2 = (bf16[12,64,128]{2,1,0:T(8,128)(2,1)S(1)}, bf16[12,64,128]{2,1,0:T(8,128)(2,1)S(1)}, u32[]{:S(2)}, u32[]{:S(2)}) collective-permute-start(bf16[12,64,128]{2,1,0:T(8,128)(2,1)S(1)} %get-tuple-element.34), channel_id=1, source_target_pairs={{0,4},{4,0},{8,12},{12,8},{16,20},{20,16},{24,28},{28,24},{1,5},{5... | collective-permute-start | bytes 589832 | tf_op jit(solution)/shard_map/ppermute | solution.py:386
  25.9 0.0 collective-permute-done.7.left
  25.9 0.3 shard_map.59
  26.2 0.6 collective-permute-start.10
  26.8 5.3 %collective-permute-done.2.received = bf16[12,64,128]{2,1,0:T(8,128)(2,1)S(1)} collective-permute-done((bf16[12,64,128]{2,1,0:T(8,128)(2,1)S(1)}, bf16[12,64,128]{2,1,0:T(8,128)(2,1)S(1)}, u32[]{:S(2)}, u32[]{:S(2)}) %collective-permute-start.2) | collective-permute-done | bytes 196640 | tf_op jit(solution)/shard_map/ppermute | solution.py:386
  32.2 1.6 %collective-permute-start.3 = (bf16[12,32,128]{2,1,0:T(8,128)(2,1)S(1)}, bf16[12,32,128]{2,1,0:T(8,128)(2,1)S(1)}, u32[]{:S(2)}, u32[]{:S(2)}) collective-permute-start(bf16[12,32,128]{2,1,0:T(8,128)(2,1)S(1)} %get-tuple-element.36), channel_id=1, source_target_pairs={{0,8},{4,12},{8,0},{12,4},{16,24},{20,28},{24,16},{28,20},{1,9},{5... | collective-permute-start | bytes 294920 | tf_op jit(solution)/shard_map/ppermute | solution.py:386
  33.8 0.0 collective-permute-done.14.right
  33.8 0.3 shard_map.63
  34.1 1.6 %collective-permute-start.15 = (bf16[6,64,128]{2,1,0:T(8,128)(2,1)S(1)}, bf16[6,64,128]{2,1,0:T(8,128)(2,1)S(1)}, u32[]{:S(2)}, u32[]{:S(2)}) collective-permute-start(bf16[6,64,128]{2,1,0:T(8,128)(2,1)S(1)} %get-tuple-element.52), channel_id=1, source_target_pairs={{0,4},{4,0},{8,12},{12,8},{16,20},{20,16},{24,28},{28,24},{1,5},{5... | collective-permute-start | bytes 294920 | tf_op jit(solution)/shard_map/ppermute | solution.py:386
  35.7 0.0 collective-permute-done.10.received
  35.8 0.5 collective-permute-start.11
  36.3 0.7 %collective-permute-done.3.received = bf16[12,32,128]{2,1,0:T(8,128)(2,1)S(1)} collective-permute-done((bf16[12,32,128]{2,1,0:T(8,128)(2,1)S(1)}, bf16[12,32,128]{2,1,0:T(8,128)(2,1)S(1)}, u32[]{:S(2)}, u32[]{:S(2)}) %collective-permute-start.3) | collective-permute-done | bytes 98336 | tf_op jit(solution)/shard_map/ppermute | solution.py:386
  37.0 2.7 %collective-permute-start.4 = (bf16[12,32,128]{2,1,0:T(8,128)(2,1)S(1)}, bf16[12,32,128]{2,1,0:T(8,128)(2,1)S(1)}, u32[]{:S(2)}, u32[]{:S(2)}) collective-permute-start(bf16[12,32,128]{2,1,0:T(8,128)(2,1)S(1)} %get-tuple-element.38), channel_id=1, source_target_pairs={{0,16},{4,20},{8,24},{12,28},{16,0},{20,4},{24,8},{28,12},{1,17},{... | collective-permute-start | bytes 294920 | tf_op jit(solution)/shard_map/ppermute | solution.py:386
  39.7 0.0 collective-permute-done.15.received
  39.7 2.5 %collective-permute-start.16 = (bf16[6,64,128]{2,1,0:T(8,128)(2,1)S(1)}, bf16[6,64,128]{2,1,0:T(8,128)(2,1)S(1)}, u32[]{:S(2)}, u32[]{:S(2)}) collective-permute-start(bf16[6,64,128]{2,1,0:T(8,128)(2,1)S(1)} %get-tuple-element.54), channel_id=1, source_target_pairs={{0,8},{4,12},{8,0},{12,4},{16,24},{20,28},{24,16},{28,20},{1,9},{5... | collective-permute-start | bytes 294920 | tf_op jit(solution)/shard_map/ppermute | solution.py:386
  42.2 0.0 collective-permute-done.11.received
  42.3 1.9 %collective-permute-start.12 = (bf16[6,64,128]{2,1,0:T(8,128)(2,1)S(1)}, bf16[6,64,128]{2,1,0:T(8,128)(2,1)S(1)}, u32[]{:S(2)}, u32[]{:S(2)}) collective-permute-start(bf16[6,64,128]{2,1,0:T(8,128)(2,1)S(1)} %get-tuple-element.48), channel_id=1, source_target_pairs={{0,16},{4,20},{8,24},{12,28},{16,0},{20,4},{24,8},{28,12},{1,17},{... | collective-permute-start | bytes 294920 | tf_op jit(solution)/shard_map/ppermute | solution.py:386
  44.2 0.0 collective-permute-done.4.received
  44.2 2.6 %collective-permute-start.5 = (bf16[12,32,128]{2,1,0:T(8,128)(2,1)S(1)}, bf16[12,32,128]{2,1,0:T(8,128)(2,1)S(1)}, u32[]{:S(2)}, u32[]{:S(2)}) collective-permute-start(bf16[12,32,128]{2,1,0:T(8,128)(2,1)S(1)} %shard_map.57.mine), channel_id=1, source_target_pairs={{0,8},{4,12},{8,0},{12,4},{16,24},{20,28},{24,16},{28,20},{1,9},{5... | collective-permute-start | bytes 294920 | tf_op jit(solution)/shard_map/ppermute | solution.py:386
  46.8 0.0 collective-permute-done.16.received
  46.9 3.7 %collective-permute-start.17 = (bf16[6,64,128]{2,1,0:T(8,128)(2,1)S(1)}, bf16[6,64,128]{2,1,0:T(8,128)(2,1)S(1)}, u32[]{:S(2)}, u32[]{:S(2)}) collective-permute-start(bf16[6,64,128]{2,1,0:T(8,128)(2,1)S(1)} %get-tuple-element.56), channel_id=1, source_target_pairs={{0,16},{4,20},{8,24},{12,28},{16,0},{20,4},{24,8},{28,12},{1,17},{... | collective-permute-start | bytes 294920 | tf_op jit(solution)/shard_map/ppermute | solution.py:386
  50.5 0.0 collective-permute-done.12.received
  50.6 0.5 collective-permute-start.13
  51.1 0.0 collective-permute-done.5.other
  51.1 0.1 collective-permute-start.6
  51.2 0.7 %plan.1.places = s32[24]{0:T(128)S(4)} custom-call(s32[1,24]{1,0:T(1,128)S(1)} %copy-done.2, s32[1,24]{1,0:T(1,128)S(1)} %copy-done.3), custom_call_target="tpu_custom_call" | custom-call | tf_op jit(solution)/shard_map/plan/pallas_call | solution.py:318
  51.9 2.2 %collective-permute-done.17.received = bf16[6,64,128]{2,1,0:T(8,128)(2,1)S(1)} collective-permute-done((bf16[6,64,128]{2,1,0:T(8,128)(2,1)S(1)}, bf16[6,64,128]{2,1,0:T(8,128)(2,1)S(1)}, u32[]{:S(2)}, u32[]{:S(2)}) %collective-permute-start.17) | collective-permute-done | bytes 98336 | tf_op jit(solution)/shard_map/ppermute | solution.py:386
  54.2 1.1 %collective-permute-done.13.guests = bf16[6,64,128]{2,1,0:T(8,128)(2,1)S(1)} collective-permute-done((bf16[6,64,128]{2,1,0:T(8,128)(2,1)S(1)}, bf16[6,64,128]{2,1,0:T(8,128)(2,1)S(1)}, u32[]{:S(2)}, u32[]{:S(2)}) %collective-permute-start.13) | collective-permute-done | bytes 98336 | tf_op jit(solution)/shard_map/ppermute | solution.py:383
  55.3 0.0 collective-permute-done.6.core
  55.3 0.1 settle.1
  55.4 1.8 %collective-permute-start.18 = (bf16[9,64,128]{2,1,0:T(8,128)(2,1)S(1)}, bf16[9,64,128]{2,1,0:T(8,128)(2,1)S(1)}, u32[]{:S(2)}, u32[]{:S(2)}) collective-permute-start(bf16[9,64,128]{2,1,0:T(8,128)(2,1)S(1)} %get-tuple-element.58), channel_id=1, source_target_pairs={{0,4},{4,0},{8,12},{12,8},{16,20},{20,16},{24,28},{28,24},{1,5},{5... | collective-permute-start | bytes 442376 | tf_op jit(solution)/shard_map/ppermute | solution.py:386
  57.2 3.4 %collective-permute-done.18.other = bf16[9,64,128]{2,1,0:T(8,128)(2,1)S(1)} collective-permute-done((bf16[9,64,128]{2,1,0:T(8,128)(2,1)S(1)}, bf16[9,64,128]{2,1,0:T(8,128)(2,1)S(1)}, u32[]{:S(2)}, u32[]{:S(2)}) %collective-permute-start.18) | collective-permute-done | bytes 147488 | tf_op jit(solution)/shard_map/ppermute | solution.py:386
  60.6 0.7 %compose.1 = bf16[8,128,128]{2,1,0:T(8,128)(2,1)} custom-call(bf16[9,64,128]{2,1,0:T(8,128)(2,1)S(1)} %get-tuple-element.57.mine, bf16[9,64,128]{2,1,0:T(8,128)(2,1)S(1)} %collective-permute-done.18.other), custom_call_target="tpu_custom_call" | custom-call | tf_op jit(solution)/shard_map/compose/pallas_call | solution.py:367
  (15 shorter events, 0.2 us)
Async XLA Ops:
  0.0 5.4 %copy-start = (s32[1,24]{1,0:T(1,128)S(1)}, s32[1,24]{1,0:T(1,128)}, u32[]{:S(2)}) copy-start(s32[1,24]{1,0:T(1,128)} %all_cols.5) | copy-start | bytes 292
  0.0 20.3 %copy-start.1 = (s32[1,24]{1,0:T(1,128)S(1)}, s32[1,24]{1,0:T(1,128)}, u32[]{:S(2)}) copy-start(s32[1,24]{1,0:T(1,128)} %all_cols.5) | copy-start | bytes 292
  2.3 19.2 %collective-permute-start.1 = (bf16[6,256,128]{2,1,0:T(8,128)(2,1)S(1)}, bf16[6,256,128]{2,1,0:T(8,128)(2,1)S(1)}, u32[]{:S(2)}, u32[]{:S(2)}) collective-permute-start(bf16[6,256,128]{2,1,0:T(8,128)(2,1)S(1)} %get-tuple-element.32), channel_id=1, source_target_pairs={{0,1},{1,0},{2,3},{3,2},{4,5},{5,4},{6,7},{7,6},{8,9},{9,8},{10,11... | collective-permute-start | bytes 1179656 | tf_op jit(solution)/shard_map/ppermute | solution.py:383
  2.8 23.0 %collective-permute-start.7 = (bf16[6,256,128]{2,1,0:T(8,128)(2,1)S(1)}, bf16[6,256,128]{2,1,0:T(8,128)(2,1)S(1)}, u32[]{:S(2)}, u32[]{:S(2)}) collective-permute-start(bf16[6,256,128]{2,1,0:T(8,128)(2,1)S(1)} %get-tuple-element.41), channel_id=1, source_target_pairs={{0,2},{1,3},{2,0},{3,1},{4,6},{5,7},{6,4},{7,5},{8,10},{9,11},{10,... | collective-permute-start | bytes 1179656 | tf_op jit(solution)/shard_map/ppermute | solution.py:383
  5.4 9.8 %collective-permute-start.8 = (s32[1,24]{1,0:T(1,128)S(1)}, s32[1,24]{1,0:T(1,128)S(1)}, u32[]{:S(2)}, u32[]{:S(2)}) collective-permute-start(s32[1,24]{1,0:T(1,128)S(1)} %copy-done), channel_id=1, source_target_pairs={{0,2},{1,3},{2,0},{3,1},{4,6},{5,7},{6,4},{7,5},{8,10},{9,11},{10,... | collective-permute-start | bytes 296 | tf_op jit(solution)/shard_map/ppermute | solution.py:383
  15.2 1.2 %collective-permute-start.9 = (s32[1,24]{1,0:T(1,128)S(1)}, s32[1,24]{1,0:T(1,128)S(1)}, u32[]{:S(2)}, u32[]{:S(2)}) collective-permute-start(s32[1,24]{1,0:T(1,128)S(1)} %collective-permute-done.8.came2), channel_id=1, source_target_pairs={{0,1},{1,0},{2,3},{3,2},{4,5},{5,4},{6,7},{7,6},{8,9},{9,8},{10,11... | collective-permute-start | bytes 296 | tf_op jit(solution)/shard_map/ppermute | solution.py:383
  18.7 32.5 %copy-start.2 = (s32[1,24]{1,0:T(1,128)S(1)}, s32[1,24]{1,0:T(1,128)}, u32[]{:S(2)}) copy-start(s32[1,24]{1,0:T(1,128)} %all_cols.5) | copy-start | bytes 292
  18.7 32.5 %copy-start.3 = (s32[1,24]{1,0:T(1,128)S(1)}, s32[1,24]{1,0:T(1,128)}, u32[]{:S(2)}) copy-start(s32[1,24]{1,0:T(1,128)} %owners.1) | copy-start | bytes 292
  18.7 15.1 %collective-permute-start.14 = (bf16[6,256,128]{2,1,0:T(8,128)(2,1)S(1)}, bf16[6,256,128]{2,1,0:T(8,128)(2,1)S(1)}, u32[]{:S(2)}, u32[]{:S(2)}) collective-permute-start(bf16[6,256,128]{2,1,0:T(8,128)(2,1)S(1)} %get-tuple-element.50), channel_id=1, source_target_pairs={{0,3},{1,2},{2,1},{3,0},{4,7},{5,6},{6,5},{7,4},{8,11},{9,10},{10,... | collective-permute-start | bytes 1179656 | tf_op jit(solution)/shard_map/ppermute | solution.py:383
  20.3 1.2 %collective-permute-start = (s32[1,24]{1,0:T(1,128)S(1)}, s32[1,24]{1,0:T(1,128)S(1)}, u32[]{:S(2)}, u32[]{:S(2)}) collective-permute-start(s32[1,24]{1,0:T(1,128)S(1)} %copy-done.1), channel_id=1, source_target_pairs={{0,1},{1,0},{2,3},{3,2},{4,5},{5,4},{6,7},{7,6},{8,9},{9,8},{10,11... | collective-permute-start | bytes 296 | tf_op jit(solution)/shard_map/ppermute | solution.py:383
  24.3 7.8 %collective-permute-start.2 = (bf16[12,64,128]{2,1,0:T(8,128)(2,1)S(1)}, bf16[12,64,128]{2,1,0:T(8,128)(2,1)S(1)}, u32[]{:S(2)}, u32[]{:S(2)}) collective-permute-start(bf16[12,64,128]{2,1,0:T(8,128)(2,1)S(1)} %get-tuple-element.34), channel_id=1, source_target_pairs={{0,4},{4,0},{8,12},{12,8},{16,20},{20,16},{24,28},{28,24},{1,5},{5... | collective-permute-start | bytes 589832 | tf_op jit(solution)/shard_map/ppermute | solution.py:386
  26.2 9.5 %collective-permute-start.10 = (bf16[6,64,128]{2,1,0:T(8,128)(2,1)S(1)}, bf16[6,64,128]{2,1,0:T(8,128)(2,1)S(1)}, u32[]{:S(2)}, u32[]{:S(2)}) collective-permute-start(bf16[6,64,128]{2,1,0:T(8,128)(2,1)S(1)} %get-tuple-element.44), channel_id=1, source_target_pairs={{0,4},{4,0},{8,12},{12,8},{16,20},{20,16},{24,28},{28,24},{1,5},{5... | collective-permute-start | bytes 294920 | tf_op jit(solution)/shard_map/ppermute | solution.py:386
  32.2 4.8 %collective-permute-start.3 = (bf16[12,32,128]{2,1,0:T(8,128)(2,1)S(1)}, bf16[12,32,128]{2,1,0:T(8,128)(2,1)S(1)}, u32[]{:S(2)}, u32[]{:S(2)}) collective-permute-start(bf16[12,32,128]{2,1,0:T(8,128)(2,1)S(1)} %get-tuple-element.36), channel_id=1, source_target_pairs={{0,8},{4,12},{8,0},{12,4},{16,24},{20,28},{24,16},{28,20},{1,9},{5... | collective-permute-start | bytes 294920 | tf_op jit(solution)/shard_map/ppermute | solution.py:386
  34.1 5.5 %collective-permute-start.15 = (bf16[6,64,128]{2,1,0:T(8,128)(2,1)S(1)}, bf16[6,64,128]{2,1,0:T(8,128)(2,1)S(1)}, u32[]{:S(2)}, u32[]{:S(2)}) collective-permute-start(bf16[6,64,128]{2,1,0:T(8,128)(2,1)S(1)} %get-tuple-element.52), channel_id=1, source_target_pairs={{0,4},{4,0},{8,12},{12,8},{16,20},{20,16},{24,28},{28,24},{1,5},{5... | collective-permute-start | bytes 294920 | tf_op jit(solution)/shard_map/ppermute | solution.py:386
  35.8 6.5 %collective-permute-start.11 = (bf16[6,64,128]{2,1,0:T(8,128)(2,1)S(1)}, bf16[6,64,128]{2,1,0:T(8,128)(2,1)S(1)}, u32[]{:S(2)}, u32[]{:S(2)}) collective-permute-start(bf16[6,64,128]{2,1,0:T(8,128)(2,1)S(1)} %get-tuple-element.46), channel_id=1, source_target_pairs={{0,8},{4,12},{8,0},{12,4},{16,24},{20,28},{24,16},{28,20},{1,9},{5... | collective-permute-start | bytes 294920 | tf_op jit(solution)/shard_map/ppermute | solution.py:386
  37.0 7.2 %collective-permute-start.4 = (bf16[12,32,128]{2,1,0:T(8,128)(2,1)S(1)}, bf16[12,32,128]{2,1,0:T(8,128)(2,1)S(1)}, u32[]{:S(2)}, u32[]{:S(2)}) collective-permute-start(bf16[12,32,128]{2,1,0:T(8,128)(2,1)S(1)} %get-tuple-element.38), channel_id=1, source_target_pairs={{0,16},{4,20},{8,24},{12,28},{16,0},{20,4},{24,8},{28,12},{1,17},{... | collective-permute-start | bytes 294920 | tf_op jit(solution)/shard_map/ppermute | solution.py:386
  39.7 7.1 %collective-permute-start.16 = (bf16[6,64,128]{2,1,0:T(8,128)(2,1)S(1)}, bf16[6,64,128]{2,1,0:T(8,128)(2,1)S(1)}, u32[]{:S(2)}, u32[]{:S(2)}) collective-permute-start(bf16[6,64,128]{2,1,0:T(8,128)(2,1)S(1)} %get-tuple-element.54), channel_id=1, source_target_pairs={{0,8},{4,12},{8,0},{12,4},{16,24},{20,28},{24,16},{28,20},{1,9},{5... | collective-permute-start | bytes 294920 | tf_op jit(solution)/shard_map/ppermute | solution.py:386
  42.3 8.3 %collective-permute-start.12 = (bf16[6,64,128]{2,1,0:T(8,128)(2,1)S(1)}, bf16[6,64,128]{2,1,0:T(8,128)(2,1)S(1)}, u32[]{:S(2)}, u32[]{:S(2)}) collective-permute-start(bf16[6,64,128]{2,1,0:T(8,128)(2,1)S(1)} %get-tuple-element.48), channel_id=1, source_target_pairs={{0,16},{4,20},{8,24},{12,28},{16,0},{20,4},{24,8},{28,12},{1,17},{... | collective-permute-start | bytes 294920 | tf_op jit(solution)/shard_map/ppermute | solution.py:386
  44.2 6.9 %collective-permute-start.5 = (bf16[12,32,128]{2,1,0:T(8,128)(2,1)S(1)}, bf16[12,32,128]{2,1,0:T(8,128)(2,1)S(1)}, u32[]{:S(2)}, u32[]{:S(2)}) collective-permute-start(bf16[12,32,128]{2,1,0:T(8,128)(2,1)S(1)} %shard_map.57.mine), channel_id=1, source_target_pairs={{0,8},{4,12},{8,0},{12,4},{16,24},{20,28},{24,16},{28,20},{1,9},{5... | collective-permute-start | bytes 294920 | tf_op jit(solution)/shard_map/ppermute | solution.py:386
  46.9 7.3 %collective-permute-start.17 = (bf16[6,64,128]{2,1,0:T(8,128)(2,1)S(1)}, bf16[6,64,128]{2,1,0:T(8,128)(2,1)S(1)}, u32[]{:S(2)}, u32[]{:S(2)}) collective-permute-start(bf16[6,64,128]{2,1,0:T(8,128)(2,1)S(1)} %get-tuple-element.56), channel_id=1, source_target_pairs={{0,16},{4,20},{8,24},{12,28},{16,0},{20,4},{24,8},{28,12},{1,17},{... | collective-permute-start | bytes 294920 | tf_op jit(solution)/shard_map/ppermute | solution.py:386
  50.6 4.7 %collective-permute-start.13 = (bf16[6,64,128]{2,1,0:T(8,128)(2,1)S(1)}, bf16[6,64,128]{2,1,0:T(8,128)(2,1)S(1)}, u32[]{:S(2)}, u32[]{:S(2)}) collective-permute-start(bf16[6,64,128]{2,1,0:T(8,128)(2,1)S(1)} %shard_map.62), channel_id=1, source_target_pairs={{0,2},{1,3},{2,0},{3,1},{4,6},{5,7},{6,4},{7,5},{8,10},{9,11},{10,... | collective-permute-start | bytes 294920 | tf_op jit(solution)/shard_map/ppermute | solution.py:383
  51.1 4.1 %collective-permute-start.6 = (bf16[6,64,128]{2,1,0:T(8,128)(2,1)S(1)}, bf16[6,64,128]{2,1,0:T(8,128)(2,1)S(1)}, u32[]{:S(2)}, u32[]{:S(2)}) collective-permute-start(bf16[6,64,128]{2,1,0:T(8,128)(2,1)S(1)} %get-tuple-element.40), channel_id=1, source_target_pairs={{0,1},{1,0},{2,3},{3,2},{4,5},{5,4},{6,7},{7,6},{8,9},{9,8},{10,11... | collective-permute-start | bytes 294920 | tf_op jit(solution)/shard_map/ppermute | solution.py:383
  55.4 5.2 %collective-permute-start.18 = (bf16[9,64,128]{2,1,0:T(8,128)(2,1)S(1)}, bf16[9,64,128]{2,1,0:T(8,128)(2,1)S(1)}, u32[]{:S(2)}, u32[]{:S(2)}) collective-permute-start(bf16[9,64,128]{2,1,0:T(8,128)(2,1)S(1)} %get-tuple-element.58), channel_id=1, source_target_pairs={{0,4},{4,0},{8,12},{12,8},{16,20},{20,16},{24,28},{28,24},{1,5},{5... | collective-permute-start | bytes 442376 | tf_op jit(solution)/shard_map/ppermute | solution.py:386

commit v7 on v6

--- a/solution.py
+++ b/solution.py
@@ -326,10 +326,10 @@
     )(scalars(cols), scalars(owners))
 
 
-def settle_kernel(places, own, core, guests, kept, received, mine, sent):
+def settle_kernel(places, own, core, guests, kept, received, mine, sent, theirs):
     me = lax.axis_index("seq")
     mine[...] = jnp.zeros_like(mine)
-    sent[...] = jnp.zeros_like(sent)
+    theirs[...] = jnp.zeros_like(theirs)
     spare = mine.shape[0] - 1
     first = 0
     for source in (own, core, guests, None):
@@ -341,17 +341,20 @@
             else:
                 value = source[j]
             mine[jnp.where(owner == me, slot, spare)] = value
-            sent[jnp.where(owner == (me ^ 1), slot, spare)] = value
+            theirs[jnp.where(owner == (me ^ 1), slot, spare)] = value
         first += guests.shape[0]
+    sent[...] = theirs[:spare]
 
 
 def settle(places, own, core, guests, kept, received):
     _, rows, _ = guests.shape
+    slots = [(CAP + 1, rows, BLOCK), (CAP, rows, BLOCK)]
     return pl.pallas_call(
         settle_kernel,
-        out_shape=[pltpu.VMEM((CAP + 1, rows, BLOCK), jnp.bfloat16)] * 2,
+        out_shape=[pltpu.VMEM(shape, jnp.bfloat16) for shape in slots],
         in_specs=[SMEM] + [VMEM] * 5,
         out_specs=[VMEM, VMEM],
+        scratch_shapes=[pltpu.VMEM(slots[0], jnp.bfloat16)],
         name="settle",
         compiler_params=SMALL,
     )(scalars(places), vectors(own), vectors(core), vectors(guests), vectors(kept), vectors(received))

time: 61.7 us -> 61.5 us (level)
  no operation moved by 1% of the time
where the time goes in v7:
time: 61.5 us; the launch traced here: 61.2 us
  starting transfers between devices  26.9 us (44%)
  waiting for transfers between devices  24.2 us (39%)
  Pallas kernels  9.86 us (16%)
    ppermute x11, starting transfers between devices, exchange(): lax.ppermute(sent, 'seq', [(i, i ^ distance) for i in range(seq_count)])  21.2 us
    ppermute x8, waiting for transfers between devices, to_peer(): lax.ppermute(value, 'tensor', [(i, i ^ distance) for i in range(tensor_co...  12.8 us
    ppermute x11, waiting for transfers between devices, exchange(): lax.ppermute(sent, 'seq', [(i, i ^ distance) for i in range(seq_count)])  11.5 us
    ppermute x8, starting transfers between devices, to_peer(): lax.ppermute(value, 'tensor', [(i, i ^ distance) for i in range(tensor_co...  5.73 us
    pallas_call x1, Pallas kernels, near_products(): pl.pallas_call(functools.partial(near_kernel, width // BLOCK, per_peer),...  2.79 us
    pallas_call x1, Pallas kernels, pack_blocks(): pl.pallas_call(functools.partial(pack_kernel, width // BLOCK, per_peer),...  2.34 us
    pallas_call x1, Pallas kernels, push_blocks(): pl.pallas_call(functools.partial(push_kernel, cols_per, per_peer), out_sh...  2.25 us
  transfers between devices with their start and end apart: 19, of which 8 were waited for; matrix products, arithmetic and copies ran while one was open for 0% of the time, Pallas kernels for 11%

profile of v7, /device:TPU:0, one launch (start us, length us, event | category | flops | bytes accessed | tf_op | source)
XLA Modules:
  0.0 61.2 jit_solution(2008812320606679181)
XLA Ops:
  0.0 2.2 %push_blocks.1 = (bf16[6,256,128]{2,1,0:T(8,128)(2,1)S(1)}, bf16[6,256,128]{2,1,0:T(8,128)(2,1)S(1)}) custom-call(s32[1,24]{1,0:T(1,128)} %all_rows.5, s32[1,24]{1,0:T(1,128)} %all_cols.5, bf16[256,13312]{1,0:T(8,128)(2,1)} %hidden.5), custom_call_target="tpu_custom_call" | custom-call | tf_op jit(solution)/shard_map/push_blocks/pallas_call | solution.py:118
  2.3 0.6 collective-permute-start.1
  2.8 2.6 %collective-permute-start.7 = (bf16[6,256,128]{2,1,0:T(8,128)(2,1)S(1)}, bf16[6,256,128]{2,1,0:T(8,128)(2,1)S(1)}, u32[]{:S(2)}, u32[]{:S(2)}) collective-permute-start(bf16[6,256,128]{2,1,0:T(8,128)(2,1)S(1)} %get-tuple-element.41), channel_id=1, source_target_pairs={{0,2},{1,3},{2,0},{3,1},{4,6},{5,7},{6,4},{7,5},{8,10},{9,11},{10,... | collective-permute-start | bytes 1179656 | tf_op jit(solution)/shard_map/ppermute | solution.py:386
  5.4 0.1 collective-permute-start.8
  5.5 9.7 %collective-permute-done.8.came2 = s32[1,24]{1,0:T(1,128)S(1)} collective-permute-done((s32[1,24]{1,0:T(1,128)S(1)}, s32[1,24]{1,0:T(1,128)S(1)}, u32[]{:S(2)}, u32[]{:S(2)}) %collective-permute-start.8) | collective-permute-done | bytes 128 | tf_op jit(solution)/shard_map/ppermute | solution.py:386
  15.2 0.0 collective-permute-start.9
  15.2 1.2 %collective-permute-done.9.came3 = s32[1,24]{1,0:T(1,128)S(1)} collective-permute-done((s32[1,24]{1,0:T(1,128)S(1)}, s32[1,24]{1,0:T(1,128)S(1)}, u32[]{:S(2)}, u32[]{:S(2)}) %collective-permute-start.9) | collective-permute-done | bytes 128 | tf_op jit(solution)/shard_map/ppermute | solution.py:386
  16.4 2.3 %pack_blocks.1 = (bf16[6,256,128]{2,1,0:T(8,128)(2,1)S(1)}, bf16[6,256,128]{2,1,0:T(8,128)(2,1)S(1)}, bf16[6,256,128]{2,1,0:T(8,128)(2,1)S(1)}) custom-call(s32[1,24]{1,0:T(1,128)} %all_rows.5, s32[1,24]{1,0:T(1,128)} %all_cols.5, s32[1,24]{1,0:T(1,128)S(1)} %collective-permute-done.8.came2, s32[1,24]{1,0:T(1,128)S(1)} %collective-permute-done.9.came3, ...), custom_call_target="tpu_custom_call" | custom-call | tf_op jit(solution)/shard_map/pack_blocks/pallas_call | solution.py:192
  18.7 0.0 copy-start.2
  18.7 0.0 copy-start.3
  18.7 1.6 %collective-permute-start.14 = (bf16[6,256,128]{2,1,0:T(8,128)(2,1)S(1)}, bf16[6,256,128]{2,1,0:T(8,128)(2,1)S(1)}, u32[]{:S(2)}, u32[]{:S(2)}) collective-permute-start(bf16[6,256,128]{2,1,0:T(8,128)(2,1)S(1)} %get-tuple-element.50), channel_id=1, source_target_pairs={{0,3},{1,2},{2,1},{3,0},{4,7},{5,6},{6,5},{7,4},{8,11},{9,10},{10,... | collective-permute-start | bytes 1179656 | tf_op jit(solution)/shard_map/ppermute | solution.py:386
  20.3 0.3 collective-permute-start
  20.6 0.8 %collective-permute-done.came1 = s32[1,24]{1,0:T(1,128)S(1)} collective-permute-done((s32[1,24]{1,0:T(1,128)S(1)}, s32[1,24]{1,0:T(1,128)S(1)}, u32[]{:S(2)}, u32[]{:S(2)}) %collective-permute-start) | collective-permute-done | bytes 128 | tf_op jit(solution)/shard_map/ppermute | solution.py:386
  21.5 0.0 collective-permute-done.1.arrived
  21.5 2.8 %near_products.1 = (f32[12,64,128]{2,1,0:T(8,128)S(1)}, bf16[12,64,128]{2,1,0:T(8,128)(2,1)S(1)}) custom-call(s32[1,24]{1,0:T(1,128)} %all_rows.5, s32[1,24]{1,0:T(1,128)} %all_cols.5, s32[1,24]{1,0:T(1,128)S(1)} %collective-permute-done.came1, bf16[256,13312]{1,0:T(8,128)(2,1)} %hidden.5, bf16[256,4096]{1,0:T(8,128)(2,1)} %grad_out.3, ...), custom_call_target="tpu_custom_call" | custom-call | tf_op jit(solution)/shard_map/near_products/pallas_call | solution.py:155
  24.3 1.6 %collective-permute-start.2 = (bf16[12,64,128]{2,1,0:T(8,128)(2,1)S(1)}, bf16[12,64,128]{2,1,0:T(8,128)(2,1)S(1)}, u32[]{:S(2)}, u32[]{:S(2)}) collective-permute-start(bf16[12,64,128]{2,1,0:T(8,128)(2,1)S(1)} %get-tuple-element.34), channel_id=1, source_target_pairs={{0,4},{4,0},{8,12},{12,8},{16,20},{20,16},{24,28},{28,24},{1,5},{5... | collective-permute-start | bytes 589832 | tf_op jit(solution)/shard_map/ppermute | solution.py:389
  25.9 0.0 collective-permute-done.7.left
  25.9 0.3 shard_map.59
  26.2 0.6 collective-permute-start.10
  26.8 5.3 %collective-permute-done.2.received = bf16[12,64,128]{2,1,0:T(8,128)(2,1)S(1)} collective-permute-done((bf16[12,64,128]{2,1,0:T(8,128)(2,1)S(1)}, bf16[12,64,128]{2,1,0:T(8,128)(2,1)S(1)}, u32[]{:S(2)}, u32[]{:S(2)}) %collective-permute-start.2) | collective-permute-done | bytes 196640 | tf_op jit(solution)/shard_map/ppermute | solution.py:389
  32.2 1.6 %collective-permute-start.3 = (bf16[12,32,128]{2,1,0:T(8,128)(2,1)S(1)}, bf16[12,32,128]{2,1,0:T(8,128)(2,1)S(1)}, u32[]{:S(2)}, u32[]{:S(2)}) collective-permute-start(bf16[12,32,128]{2,1,0:T(8,128)(2,1)S(1)} %get-tuple-element.36), channel_id=1, source_target_pairs={{0,8},{4,12},{8,0},{12,4},{16,24},{20,28},{24,16},{28,20},{1,9},{5... | collective-permute-start | bytes 294920 | tf_op jit(solution)/shard_map/ppermute | solution.py:389
  33.8 0.0 collective-permute-done.14.right
  33.8 0.3 shard_map.63
  34.1 1.6 %collective-permute-start.15 = (bf16[6,64,128]{2,1,0:T(8,128)(2,1)S(1)}, bf16[6,64,128]{2,1,0:T(8,128)(2,1)S(1)}, u32[]{:S(2)}, u32[]{:S(2)}) collective-permute-start(bf16[6,64,128]{2,1,0:T(8,128)(2,1)S(1)} %get-tuple-element.52), channel_id=1, source_target_pairs={{0,4},{4,0},{8,12},{12,8},{16,20},{20,16},{24,28},{28,24},{1,5},{5... | collective-permute-start | bytes 294920 | tf_op jit(solution)/shard_map/ppermute | solution.py:389
  35.7 0.0 collective-permute-done.10.received
  35.8 0.5 collective-permute-start.11
  36.3 0.7 %collective-permute-done.3.received = bf16[12,32,128]{2,1,0:T(8,128)(2,1)S(1)} collective-permute-done((bf16[12,32,128]{2,1,0:T(8,128)(2,1)S(1)}, bf16[12,32,128]{2,1,0:T(8,128)(2,1)S(1)}, u32[]{:S(2)}, u32[]{:S(2)}) %collective-permute-start.3) | collective-permute-done | bytes 98336 | tf_op jit(solution)/shard_map/ppermute | solution.py:389
  37.0 2.7 %collective-permute-start.4 = (bf16[12,32,128]{2,1,0:T(8,128)(2,1)S(1)}, bf16[12,32,128]{2,1,0:T(8,128)(2,1)S(1)}, u32[]{:S(2)}, u32[]{:S(2)}) collective-permute-start(bf16[12,32,128]{2,1,0:T(8,128)(2,1)S(1)} %get-tuple-element.38), channel_id=1, source_target_pairs={{0,16},{4,20},{8,24},{12,28},{16,0},{20,4},{24,8},{28,12},{1,17},{... | collective-permute-start | bytes 294920 | tf_op jit(solution)/shard_map/ppermute | solution.py:389
  39.7 0.0 collective-permute-done.15.received
  39.7 2.5 %collective-permute-start.16 = (bf16[6,64,128]{2,1,0:T(8,128)(2,1)S(1)}, bf16[6,64,128]{2,1,0:T(8,128)(2,1)S(1)}, u32[]{:S(2)}, u32[]{:S(2)}) collective-permute-start(bf16[6,64,128]{2,1,0:T(8,128)(2,1)S(1)} %get-tuple-element.54), channel_id=1, source_target_pairs={{0,8},{4,12},{8,0},{12,4},{16,24},{20,28},{24,16},{28,20},{1,9},{5... | collective-permute-start | bytes 294920 | tf_op jit(solution)/shard_map/ppermute | solution.py:389
  42.2 0.0 collective-permute-done.11.received
  42.3 1.9 %collective-permute-start.12 = (bf16[6,64,128]{2,1,0:T(8,128)(2,1)S(1)}, bf16[6,64,128]{2,1,0:T(8,128)(2,1)S(1)}, u32[]{:S(2)}, u32[]{:S(2)}) collective-permute-start(bf16[6,64,128]{2,1,0:T(8,128)(2,1)S(1)} %get-tuple-element.48), channel_id=1, source_target_pairs={{0,16},{4,20},{8,24},{12,28},{16,0},{20,4},{24,8},{28,12},{1,17},{... | collective-permute-start | bytes 294920 | tf_op jit(solution)/shard_map/ppermute | solution.py:389
  44.2 0.0 collective-permute-done.4.received
  44.2 2.6 %collective-permute-start.5 = (bf16[12,32,128]{2,1,0:T(8,128)(2,1)S(1)}, bf16[12,32,128]{2,1,0:T(8,128)(2,1)S(1)}, u32[]{:S(2)}, u32[]{:S(2)}) collective-permute-start(bf16[12,32,128]{2,1,0:T(8,128)(2,1)S(1)} %shard_map.57.mine), channel_id=1, source_target_pairs={{0,8},{4,12},{8,0},{12,4},{16,24},{20,28},{24,16},{28,20},{1,9},{5... | collective-permute-start | bytes 294920 | tf_op jit(solution)/shard_map/ppermute | solution.py:389
  46.8 0.0 collective-permute-done.16.received
  46.9 3.7 %collective-permute-start.17 = (bf16[6,64,128]{2,1,0:T(8,128)(2,1)S(1)}, bf16[6,64,128]{2,1,0:T(8,128)(2,1)S(1)}, u32[]{:S(2)}, u32[]{:S(2)}) collective-permute-start(bf16[6,64,128]{2,1,0:T(8,128)(2,1)S(1)} %get-tuple-element.56), channel_id=1, source_target_pairs={{0,16},{4,20},{8,24},{12,28},{16,0},{20,4},{24,8},{28,12},{1,17},{... | collective-permute-start | bytes 294920 | tf_op jit(solution)/shard_map/ppermute | solution.py:389
  50.5 0.0 collective-permute-done.12.received
  50.6 0.5 collective-permute-start.13
  51.1 0.0 collective-permute-done.5.other
  51.1 0.1 collective-permute-start.6
  51.2 0.7 %plan.1.places = s32[24]{0:T(128)S(4)} custom-call(s32[1,24]{1,0:T(1,128)S(1)} %copy-done.2, s32[1,24]{1,0:T(1,128)S(1)} %copy-done.3), custom_call_target="tpu_custom_call" | custom-call | tf_op jit(solution)/shard_map/plan/pallas_call | solution.py:318
  51.9 2.2 %collective-permute-done.17.received = bf16[6,64,128]{2,1,0:T(8,128)(2,1)S(1)} collective-permute-done((bf16[6,64,128]{2,1,0:T(8,128)(2,1)S(1)}, bf16[6,64,128]{2,1,0:T(8,128)(2,1)S(1)}, u32[]{:S(2)}, u32[]{:S(2)}) %collective-permute-start.17) | collective-permute-done | bytes 98336 | tf_op jit(solution)/shard_map/ppermute | solution.py:389
  54.2 1.1 %collective-permute-done.13.guests = bf16[6,64,128]{2,1,0:T(8,128)(2,1)S(1)} collective-permute-done((bf16[6,64,128]{2,1,0:T(8,128)(2,1)S(1)}, bf16[6,64,128]{2,1,0:T(8,128)(2,1)S(1)}, u32[]{:S(2)}, u32[]{:S(2)}) %collective-permute-start.13) | collective-permute-done | bytes 98336 | tf_op jit(solution)/shard_map/ppermute | solution.py:386
  55.3 0.0 collective-permute-done.6.core
  55.3 0.1 settle.1
  55.4 1.8 %collective-permute-start.18 = (bf16[8,64,128]{2,1,0:T(8,128)(2,1)S(1)}, bf16[8,64,128]{2,1,0:T(8,128)(2,1)S(1)}, u32[]{:S(2)}, u32[]{:S(2)}) collective-permute-start(bf16[8,64,128]{2,1,0:T(8,128)(2,1)S(1)} %get-tuple-element.58), channel_id=1, source_target_pairs={{0,4},{4,0},{8,12},{12,8},{16,20},{20,16},{24,28},{28,24},{1,5},{5... | collective-permute-start | bytes 393224 | tf_op jit(solution)/shard_map/ppermute | solution.py:389
  57.2 3.2 %collective-permute-done.18.other = bf16[8,64,128]{2,1,0:T(8,128)(2,1)S(1)} collective-permute-done((bf16[8,64,128]{2,1,0:T(8,128)(2,1)S(1)}, bf16[8,64,128]{2,1,0:T(8,128)(2,1)S(1)}, u32[]{:S(2)}, u32[]{:S(2)}) %collective-permute-start.18) | collective-permute-done | bytes 131104 | tf_op jit(solution)/shard_map/ppermute | solution.py:389
  60.4 0.7 %compose.1 = bf16[8,128,128]{2,1,0:T(8,128)(2,1)} custom-call(bf16[9,64,128]{2,1,0:T(8,128)(2,1)S(1)} %get-tuple-element.57.mine, bf16[8,64,128]{2,1,0:T(8,128)(2,1)S(1)} %collective-permute-done.18.other), custom_call_target="tpu_custom_call" | custom-call | tf_op jit(solution)/shard_map/compose/pallas_call | solution.py:370
  (15 shorter events, 0.2 us)
Async XLA Ops:
  0.0 5.4 %copy-start = (s32[1,24]{1,0:T(1,128)S(1)}, s32[1,24]{1,0:T(1,128)}, u32[]{:S(2)}) copy-start(s32[1,24]{1,0:T(1,128)} %all_cols.5) | copy-start | bytes 292
  0.0 20.3 %copy-start.1 = (s32[1,24]{1,0:T(1,128)S(1)}, s32[1,24]{1,0:T(1,128)}, u32[]{:S(2)}) copy-start(s32[1,24]{1,0:T(1,128)} %all_cols.5) | copy-start | bytes 292
  2.3 19.2 %collective-permute-start.1 = (bf16[6,256,128]{2,1,0:T(8,128)(2,1)S(1)}, bf16[6,256,128]{2,1,0:T(8,128)(2,1)S(1)}, u32[]{:S(2)}, u32[]{:S(2)}) collective-permute-start(bf16[6,256,128]{2,1,0:T(8,128)(2,1)S(1)} %get-tuple-element.32), channel_id=1, source_target_pairs={{0,1},{1,0},{2,3},{3,2},{4,5},{5,4},{6,7},{7,6},{8,9},{9,8},{10,11... | collective-permute-start | bytes 1179656 | tf_op jit(solution)/shard_map/ppermute | solution.py:386
  2.8 23.0 %collective-permute-start.7 = (bf16[6,256,128]{2,1,0:T(8,128)(2,1)S(1)}, bf16[6,256,128]{2,1,0:T(8,128)(2,1)S(1)}, u32[]{:S(2)}, u32[]{:S(2)}) collective-permute-start(bf16[6,256,128]{2,1,0:T(8,128)(2,1)S(1)} %get-tuple-element.41), channel_id=1, source_target_pairs={{0,2},{1,3},{2,0},{3,1},{4,6},{5,7},{6,4},{7,5},{8,10},{9,11},{10,... | collective-permute-start | bytes 1179656 | tf_op jit(solution)/shard_map/ppermute | solution.py:386
  5.4 9.8 %collective-permute-start.8 = (s32[1,24]{1,0:T(1,128)S(1)}, s32[1,24]{1,0:T(1,128)S(1)}, u32[]{:S(2)}, u32[]{:S(2)}) collective-permute-start(s32[1,24]{1,0:T(1,128)S(1)} %copy-done), channel_id=1, source_target_pairs={{0,2},{1,3},{2,0},{3,1},{4,6},{5,7},{6,4},{7,5},{8,10},{9,11},{10,... | collective-permute-start | bytes 296 | tf_op jit(solution)/shard_map/ppermute | solution.py:386
  15.2 1.2 %collective-permute-start.9 = (s32[1,24]{1,0:T(1,128)S(1)}, s32[1,24]{1,0:T(1,128)S(1)}, u32[]{:S(2)}, u32[]{:S(2)}) collective-permute-start(s32[1,24]{1,0:T(1,128)S(1)} %collective-permute-done.8.came2), channel_id=1, source_target_pairs={{0,1},{1,0},{2,3},{3,2},{4,5},{5,4},{6,7},{7,6},{8,9},{9,8},{10,11... | collective-permute-start | bytes 296 | tf_op jit(solution)/shard_map/ppermute | solution.py:386
  18.7 32.5 %copy-start.2 = (s32[1,24]{1,0:T(1,128)S(1)}, s32[1,24]{1,0:T(1,128)}, u32[]{:S(2)}) copy-start(s32[1,24]{1,0:T(1,128)} %all_cols.5) | copy-start | bytes 292
  18.7 32.5 %copy-start.3 = (s32[1,24]{1,0:T(1,128)S(1)}, s32[1,24]{1,0:T(1,128)}, u32[]{:S(2)}) copy-start(s32[1,24]{1,0:T(1,128)} %owners.1) | copy-start | bytes 292
  18.7 15.1 %collective-permute-start.14 = (bf16[6,256,128]{2,1,0:T(8,128)(2,1)S(1)}, bf16[6,256,128]{2,1,0:T(8,128)(2,1)S(1)}, u32[]{:S(2)}, u32[]{:S(2)}) collective-permute-start(bf16[6,256,128]{2,1,0:T(8,128)(2,1)S(1)} %get-tuple-element.50), channel_id=1, source_target_pairs={{0,3},{1,2},{2,1},{3,0},{4,7},{5,6},{6,5},{7,4},{8,11},{9,10},{10,... | collective-permute-start | bytes 1179656 | tf_op jit(solution)/shard_map/ppermute | solution.py:386
  20.3 1.2 %collective-permute-start = (s32[1,24]{1,0:T(1,128)S(1)}, s32[1,24]{1,0:T(1,128)S(1)}, u32[]{:S(2)}, u32[]{:S(2)}) collective-permute-start(s32[1,24]{1,0:T(1,128)S(1)} %copy-done.1), channel_id=1, source_target_pairs={{0,1},{1,0},{2,3},{3,2},{4,5},{5,4},{6,7},{7,6},{8,9},{9,8},{10,11... | collective-permute-start | bytes 296 | tf_op jit(solution)/shard_map/ppermute | solution.py:386
  24.3 7.8 %collective-permute-start.2 = (bf16[12,64,128]{2,1,0:T(8,128)(2,1)S(1)}, bf16[12,64,128]{2,1,0:T(8,128)(2,1)S(1)}, u32[]{:S(2)}, u32[]{:S(2)}) collective-permute-start(bf16[12,64,128]{2,1,0:T(8,128)(2,1)S(1)} %get-tuple-element.34), channel_id=1, source_target_pairs={{0,4},{4,0},{8,12},{12,8},{16,20},{20,16},{24,28},{28,24},{1,5},{5... | collective-permute-start | bytes 589832 | tf_op jit(solution)/shard_map/ppermute | solution.py:389
  26.2 9.5 %collective-permute-start.10 = (bf16[6,64,128]{2,1,0:T(8,128)(2,1)S(1)}, bf16[6,64,128]{2,1,0:T(8,128)(2,1)S(1)}, u32[]{:S(2)}, u32[]{:S(2)}) collective-permute-start(bf16[6,64,128]{2,1,0:T(8,128)(2,1)S(1)} %get-tuple-element.44), channel_id=1, source_target_pairs={{0,4},{4,0},{8,12},{12,8},{16,20},{20,16},{24,28},{28,24},{1,5},{5... | collective-permute-start | bytes 294920 | tf_op jit(solution)/shard_map/ppermute | solution.py:389
  32.2 4.8 %collective-permute-start.3 = (bf16[12,32,128]{2,1,0:T(8,128)(2,1)S(1)}, bf16[12,32,128]{2,1,0:T(8,128)(2,1)S(1)}, u32[]{:S(2)}, u32[]{:S(2)}) collective-permute-start(bf16[12,32,128]{2,1,0:T(8,128)(2,1)S(1)} %get-tuple-element.36), channel_id=1, source_target_pairs={{0,8},{4,12},{8,0},{12,4},{16,24},{20,28},{24,16},{28,20},{1,9},{5... | collective-permute-start | bytes 294920 | tf_op jit(solution)/shard_map/ppermute | solution.py:389
  34.1 5.5 %collective-permute-start.15 = (bf16[6,64,128]{2,1,0:T(8,128)(2,1)S(1)}, bf16[6,64,128]{2,1,0:T(8,128)(2,1)S(1)}, u32[]{:S(2)}, u32[]{:S(2)}) collective-permute-start(bf16[6,64,128]{2,1,0:T(8,128)(2,1)S(1)} %get-tuple-element.52), channel_id=1, source_target_pairs={{0,4},{4,0},{8,12},{12,8},{16,20},{20,16},{24,28},{28,24},{1,5},{5... | collective-permute-start | bytes 294920 | tf_op jit(solution)/shard_map/ppermute | solution.py:389
  35.8 6.5 %collective-permute-start.11 = (bf16[6,64,128]{2,1,0:T(8,128)(2,1)S(1)}, bf16[6,64,128]{2,1,0:T(8,128)(2,1)S(1)}, u32[]{:S(2)}, u32[]{:S(2)}) collective-permute-start(bf16[6,64,128]{2,1,0:T(8,128)(2,1)S(1)} %get-tuple-element.46), channel_id=1, source_target_pairs={{0,8},{4,12},{8,0},{12,4},{16,24},{20,28},{24,16},{28,20},{1,9},{5... | collective-permute-start | bytes 294920 | tf_op jit(solution)/shard_map/ppermute | solution.py:389
  37.0 7.2 %collective-permute-start.4 = (bf16[12,32,128]{2,1,0:T(8,128)(2,1)S(1)}, bf16[12,32,128]{2,1,0:T(8,128)(2,1)S(1)}, u32[]{:S(2)}, u32[]{:S(2)}) collective-permute-start(bf16[12,32,128]{2,1,0:T(8,128)(2,1)S(1)} %get-tuple-element.38), channel_id=1, source_target_pairs={{0,16},{4,20},{8,24},{12,28},{16,0},{20,4},{24,8},{28,12},{1,17},{... | collective-permute-start | bytes 294920 | tf_op jit(solution)/shard_map/ppermute | solution.py:389
  39.7 7.1 %collective-permute-start.16 = (bf16[6,64,128]{2,1,0:T(8,128)(2,1)S(1)}, bf16[6,64,128]{2,1,0:T(8,128)(2,1)S(1)}, u32[]{:S(2)}, u32[]{:S(2)}) collective-permute-start(bf16[6,64,128]{2,1,0:T(8,128)(2,1)S(1)} %get-tuple-element.54), channel_id=1, source_target_pairs={{0,8},{4,12},{8,0},{12,4},{16,24},{20,28},{24,16},{28,20},{1,9},{5... | collective-permute-start | bytes 294920 | tf_op jit(solution)/shard_map/ppermute | solution.py:389
  42.3 8.3 %collective-permute-start.12 = (bf16[6,64,128]{2,1,0:T(8,128)(2,1)S(1)}, bf16[6,64,128]{2,1,0:T(8,128)(2,1)S(1)}, u32[]{:S(2)}, u32[]{:S(2)}) collective-permute-start(bf16[6,64,128]{2,1,0:T(8,128)(2,1)S(1)} %get-tuple-element.48), channel_id=1, source_target_pairs={{0,16},{4,20},{8,24},{12,28},{16,0},{20,4},{24,8},{28,12},{1,17},{... | collective-permute-start | bytes 294920 | tf_op jit(solution)/shard_map/ppermute | solution.py:389
  44.2 6.9 %collective-permute-start.5 = (bf16[12,32,128]{2,1,0:T(8,128)(2,1)S(1)}, bf16[12,32,128]{2,1,0:T(8,128)(2,1)S(1)}, u32[]{:S(2)}, u32[]{:S(2)}) collective-permute-start(bf16[12,32,128]{2,1,0:T(8,128)(2,1)S(1)} %shard_map.57.mine), channel_id=1, source_target_pairs={{0,8},{4,12},{8,0},{12,4},{16,24},{20,28},{24,16},{28,20},{1,9},{5... | collective-permute-start | bytes 294920 | tf_op jit(solution)/shard_map/ppermute | solution.py:389
  46.9 7.3 %collective-permute-start.17 = (bf16[6,64,128]{2,1,0:T(8,128)(2,1)S(1)}, bf16[6,64,128]{2,1,0:T(8,128)(2,1)S(1)}, u32[]{:S(2)}, u32[]{:S(2)}) collective-permute-start(bf16[6,64,128]{2,1,0:T(8,128)(2,1)S(1)} %get-tuple-element.56), channel_id=1, source_target_pairs={{0,16},{4,20},{8,24},{12,28},{16,0},{20,4},{24,8},{28,12},{1,17},{... | collective-permute-start | bytes 294920 | tf_op jit(solution)/shard_map/ppermute | solution.py:389
  50.6 4.7 %collective-permute-start.13 = (bf16[6,64,128]{2,1,0:T(8,128)(2,1)S(1)}, bf16[6,64,128]{2,1,0:T(8,128)(2,1)S(1)}, u32[]{:S(2)}, u32[]{:S(2)}) collective-permute-start(bf16[6,64,128]{2,1,0:T(8,128)(2,1)S(1)} %shard_map.62), channel_id=1, source_target_pairs={{0,2},{1,3},{2,0},{3,1},{4,6},{5,7},{6,4},{7,5},{8,10},{9,11},{10,... | collective-permute-start | bytes 294920 | tf_op jit(solution)/shard_map/ppermute | solution.py:386
  51.1 4.1 %collective-permute-start.6 = (bf16[6,64,128]{2,1,0:T(8,128)(2,1)S(1)}, bf16[6,64,128]{2,1,0:T(8,128)(2,1)S(1)}, u32[]{:S(2)}, u32[]{:S(2)}) collective-permute-start(bf16[6,64,128]{2,1,0:T(8,128)(2,1)S(1)} %get-tuple-element.40), channel_id=1, source_target_pairs={{0,1},{1,0},{2,3},{3,2},{4,5},{5,4},{6,7},{7,6},{8,9},{9,8},{10,11... | collective-permute-start | bytes 294920 | tf_op jit(solution)/shard_map/ppermute | solution.py:386
  55.4 5.0 %collective-permute-start.18 = (bf16[8,64,128]{2,1,0:T(8,128)(2,1)S(1)}, bf16[8,64,128]{2,1,0:T(8,128)(2,1)S(1)}, u32[]{:S(2)}, u32[]{:S(2)}) collective-permute-start(bf16[8,64,128]{2,1,0:T(8,128)(2,1)S(1)} %get-tuple-element.58), channel_id=1, source_target_pairs={{0,4},{4,0},{8,12},{12,8},{16,20},{20,16},{24,28},{28,24},{1,5},{5... | collective-permute-start | bytes 393224 | tf_op jit(solution)/shard_map/ppermute | solution.py:389
